TPU v7x, 128 devices: a whole 4x4x4 slice. The times are simulated.
128 devices in a mesh: row: 8 (over y, core), col: 16 (over x, z).
Axes of the slice: x: 4, y: 4, z: 4, core: 2. Of those that a mesh axis runs over, the one named last changes fastest.
Arguments:
- points: float32 [3, 4, 16384], P(None, None, ('row', 'col')), may hold values from 0 to 1
- weights: float32 [4, 16384], P(None, ('row', 'col')), may hold values from 0.05 to 0.2
- shift: float32 [16384], P(('row', 'col')), may hold values from 0.5 to 4
- cluster_rank: int32 [32], replicated, may hold values from 0 to 31, each once
Outputs:
- factor: float32 [4, 8, 512, 2, 16, 512], P(None, 'row', None, None, 'col')
Inputs may be any that keep to these rules, and one draw needn't show every extreme that they name: `cluster_rank`: every cluster has a distinct elimination position.
All inputs are finite; a program needn't handle non-finite values.
Results may differ from a plain program's by a relative error of at most 0.0003.
Values sent between devices are 32-bit elements; how exact they have to be, the bound alone decides.
No kernel may reach another device: no remote copies, remote signals or barrier semaphores. Data moves between devices by JAX's collectives and lax.ppermute only.
A program may use at most 128 MiB of HBM per device.

v0:
```python
import jax
import jax.numpy as jnp
from jax import lax
from jax.sharding import PartitionSpec as P

SOFTENING_SQUARED = 0.0004
COLUMN_GROUP = 4


def broadcast(value, axis, source):
    kept = jnp.where(lax.axis_index(axis) == source, value, 0).astype(value.dtype)
    return lax.psum(kept, axis)


def kernel_block(row_geometry, col_geometry):
    values = jnp.zeros((row_geometry.shape[2], col_geometry.shape[2]), jnp.float32)
    for first in range(row_geometry.shape[1]):
        for second in range(col_geometry.shape[1]):
            squared = SOFTENING_SQUARED
            for coordinate in range(3):
                offset = (
                    row_geometry[coordinate, first][:, None]
                    - col_geometry[coordinate, second][None, :]
                )
                squared = squared + offset * offset
            product = row_geometry[3, first][:, None] * col_geometry[3, second][None, :]
            values = values + product * lax.rsqrt(squared)
    return values


def reorder(points, weights, shift, cluster_rank):
    clusters = cluster_rank.shape[0]
    positions = jnp.arange(clusters, dtype=jnp.int32)
    order = jnp.sum(
        jnp.where(cluster_rank[None, :] == positions[:, None], positions[None, :], 0), axis=1
    )
    geometry = jnp.concatenate([points, weights[None]], axis=0)
    quadrature = geometry.shape[1]
    geometry = geometry.reshape(4, quadrature, clusters, -1)
    geometry = jnp.take(geometry, order, axis=2).reshape(4, quadrature, -1)
    shifted = jnp.take(shift.reshape(clusters, -1), order, axis=0).reshape(-1)
    return (geometry, shifted)


def shards(points, weights, shift, cluster_rank):
    row_count = lax.axis_size("row")
    col_count = lax.axis_size("col")
    row_index = lax.axis_index("row")
    col_index = lax.axis_index("col")
    all_points, all_weights, all_shift = (
        lax.all_gather(points, ("row", "col"), axis=2, tiled=True),
        lax.all_gather(weights, ("row", "col"), axis=1, tiled=True),
        lax.all_gather(shift, ("row", "col"), axis=0, tiled=True),
    )
    geometry, shifted = reorder(all_points, all_weights, all_shift, cluster_rank)
    clusters = cluster_rank.shape[0]
    tile = shifted.shape[0] // clusters
    row_tiles = clusters // row_count
    col_tiles = clusters // col_count

    def assemble(row_start, col_start, row_length, col_length):
        rows = lax.dynamic_slice_in_dim(geometry, row_start, row_length, 2)
        columns = lax.dynamic_slice_in_dim(geometry, col_start, col_length, 2)
        values = kernel_block(rows, columns)
        row_ids = row_start + jnp.arange(row_length, dtype=jnp.int32)
        col_ids = col_start + jnp.arange(col_length, dtype=jnp.int32)
        row_shift = lax.dynamic_slice_in_dim(shifted, row_start, row_length, 0)
        return values + jnp.where(row_ids[:, None] == col_ids[None, :], row_shift[:, None], 0.0)

    share = tile // col_count
    group_width = COLUMN_GROUP * tile
    outgoing = jnp.zeros((col_count, row_tiles, share, col_tiles, tile), jnp.float32)
    for slot_row in range(row_tiles):
        block_row = slot_row * row_count + row_index
        row_start = block_row * tile + col_index * share

        def add_group(group, buffer):
            values = assemble(row_start, group * group_width, share, group_width)
            values = values.reshape(share, COLUMN_GROUP, tile)
            block_cols = group * COLUMN_GROUP + jnp.arange(COLUMN_GROUP, dtype=jnp.int32)
            values = jnp.where((block_cols <= block_row)[None, :, None], values, 0.0)
            placed = jnp.transpose(values, (1, 0, 2))[:, None, :, None, :]
            first_col = group * COLUMN_GROUP
            starts = (
                first_col % col_count,
                jnp.int32(slot_row),
                jnp.int32(0),
                first_col // col_count,
                jnp.int32(0),
            )
            starts = tuple((jnp.asarray(value, jnp.int32) for value in starts))
            return lax.dynamic_update_slice(buffer, placed, starts)

        group_limit = block_row // COLUMN_GROUP + 1
        outgoing = lax.fori_loop(jnp.int32(0), group_limit, add_group, outgoing)
    incoming = lax.all_to_all(outgoing, "col", split_axis=0, concat_axis=2, tiled=True)
    tiles = incoming.reshape(row_tiles, tile, col_tiles, tile)
    block_rows = jnp.arange(row_tiles, dtype=jnp.int32) * row_count + row_index
    block_cols = jnp.arange(col_tiles, dtype=jnp.int32) * col_count + col_index
    for step in range(2):
        diagonal_row = step % row_count
        diagonal_slot = step // row_count
        column_root = step % col_count
        column_slot = step // col_count
        diagonal = broadcast(tiles[diagonal_slot, :, column_slot, :], "row", diagonal_row)
        diagonal_factor = jnp.linalg.cholesky(diagonal)
        column = tiles[:, :, column_slot, :]
        repeated = jnp.broadcast_to(diagonal_factor, (row_tiles, tile, tile))
        solved = lax.linalg.triangular_solve(
            repeated, column, left_side=False, lower=True, transpose_a=True
        )
        below = (block_rows > step)[:, None, None]
        at_step = (block_rows == step)[:, None, None]
        panel = jnp.where(below, solved, jnp.where(at_step, diagonal_factor[None], column))
        tiles = tiles.at[:, :, column_slot, :].set(
            jnp.where(col_index == column_root, panel, column)
        )
        row_factors = broadcast(panel, "col", column_root)
        slots = (jnp.arange(col_tiles, dtype=jnp.int32) * col_count + col_index) // row_count
        candidates = jnp.take(row_factors, slots, axis=0)
        col_factors = broadcast(candidates, "row", col_index % row_count)
        product = jnp.einsum(
            "iab,jcb->iajc", row_factors, col_factors, precision=lax.Precision.HIGHEST
        )
        active = (block_rows[:, None] >= block_cols[None, :]) & (block_cols[None, :] > step)
        tiles = tiles - jnp.where(active[:, None, :, None], product, 0.0)
    return tiles.reshape(row_tiles, 1, tile, col_tiles, 1, tile)


def solution(mesh):
    return jax.shard_map(
        shards,
        mesh=mesh,
        in_specs=(P(None, None, ("row", "col")), P(None, ("row", "col")), P(("row", "col")), P()),
        out_specs=P(None, "row", None, None, "col", None),
        check_vma=False,
    )
```

profile of v0, /device:TPU:73, one launch (start us, length us, event | category | flops | bytes accessed | tf_op | source)
XLA Modules:
  0.0 1519.7 jit_solution(9004311954200575139)
XLA Ops:
  7.5 42.7 %all-gather = f32[128,1,128]{2,1,0:T(1,128)S(1)} all-gather(f32[1,1,128]{2,1,0:T(1,128)} %bitcast.331), channel_id=1, replica_groups=mesh['row'=8,'col'=16] {'row','col'}, dimensions={0}, use_global_device_ids=true | all-gather | bytes 66048 | tf_op jit(solution)/shard_map/all_gather | solution.py:53
  52.1 58.3 %all_gather.10 = f32[4,16384]{1,0:T(4,128)S(1)} all-gather(f32[4,128]{1,0:T(4,128)} %param.22), channel_id=1, replica_groups=mesh['row'=8,'col'=16] {'row','col'}, dimensions={1}, use_global_device_ids=true | all-gather | bytes 264192 | tf_op jit(solution)/shard_map/all_gather | solution.py:52
  110.4 60.4 %all_gather.9 = f32[3,4,16384]{2,1,0:T(4,128)S(1)} all-gather(f32[3,4,128]{2,1,0:T(4,128)} %param.21), channel_id=1, replica_groups=mesh['row'=8,'col'=16] {'row','col'}, dimensions={2}, use_global_device_ids=true | all-gather | bytes 792576 | tf_op jit(solution)/shard_map/all_gather | solution.py:51
  172.9 4.5 broadcast_in_dim.239
  177.3 3.3 while.54
  178.0 2.6 select_dynamic-update-slice_fusion.8
  180.6 9.8 while.55
  181.3 2.6 select_dynamic-update-slice_fusion.9
  187.8 2.6 select_dynamic-update-slice_fusion.9
  190.4 16.4 %while.56 = (s32[]{:T(128)}, f32[16,4,32,2,512]{4,2,3,1,0:T(8,128)}, s32[]{:T(128)}, s32[]{:T(128)}, f32[4,4,32]{2,1,0:T(4,128)S(1)}, /*index=5*/f32[4,4,16384]{...) while((s32[]{:T(128)}, ...), condition=%wide.region_6.7_spmd, body=%wide.region_5.6_spmd.sunk | while | flops 12785739 | bytes 941002 | solution.py:95
  191.1 2.6 select_dynamic-update-slice_fusion.10
  194.4 2.6 select_dynamic-update-slice_fusion.10
  197.7 2.6 select_dynamic-update-slice_fusion.10
  200.9 2.6 select_dynamic-update-slice_fusion.10
  206.8 23.3 %while.57 = (s32[]{:T(128)}, f32[16,4,32,2,512]{4,2,3,1,0:T(8,128)}, s32[]{:T(128)}, s32[]{:T(128)}, f32[4,4,32]{2,1,0:T(4,128)S(1)}, /*index=5*/f32[4,4,16384]{...) while((s32[]{:T(128)}, ...), condition=%wide.region_8.9_spmd, body=%wide.region_7.8_spmd.sunk | while | flops 12785739 | bytes 941002 | solution.py:95
  207.8 2.6 select_dynamic-update-slice_fusion.11
  211.1 2.6 select_dynamic-update-slice_fusion.11
  214.4 2.6 select_dynamic-update-slice_fusion.11
  230.1 6.0 all-to-all-start
  236.1 131.6 %all-to-all-done = f32[16,4,32,2,512]{4,2,3,1,0:T(8,128)} async-done(((f32[16,4,32,2,512]{4,2,3,1,0:T(8,128)}), f32[16,4,32,2,512]{4,2,3,1,0:T(8,128)}, u32[]{:S(2)}, u32[]{:S(2)}) %all-to-all-start) | async-done | bytes 8388640 | tf_op jit(solution)/shard_map/all_to_all | solution.py:96
  367.7 8.6 copy.248
  376.4 9.9 copy.272
  388.7 4.6 slice.1367
  393.3 5.2 copy.355
  398.6 67.9 %all-reduce.8.cloned.1.call-done = f32[512,512]{0,1:T(8,128)} async-done(((f32[512,512]{0,1:T(8,128)}), f32[512,512]{0,1:T(8,128)}) %all-reduce.8.cloned.1.call-update) | async-done | bytes 1048592 | tf_op jit(solution)/shard_map/psum | solution.py:12
  469.5 11.7 cholesky.286
  481.2 9.8 custom-call.27
  491.9 11.7 cholesky.305
  503.6 18.5 %custom-call.28 = f32[1,128,128]{1,2,0:T(8,128)S(1)} custom-call(f32[1,128,128]{2,1,0:T(8,128)S(1)} %get-tuple-element.762), custom_call_target="InvertDiagBlocksLowerTriangular" | custom-call | tf_op jit(solution)/shard_map/jit(cholesky)/cholesky | solution.py:106
  522.8 11.7 cholesky.326
  535.3 9.8 custom-call.29
  545.7 11.7 cholesky.343
  565.0 13.2 while.58
  579.3 158.0 %custom-call.30 = f32[4,4,128,128]{2,3,1,0:T(8,128)S(1)} custom-call(f32[4,4,128,128]{3,2,1,0:T(8,128)} %bitcast.325), custom_call_target="InvertDiagBlocksLowerTriangular" | custom-call | tf_op jit(solution)/shard_map/triangular_solve/custom-call.3 | solution.py:109
  737.3 2.7 fusion.45
  748.2 3.8 fusion.33
  754.2 2.7 broadcast_select_fusion.2
  757.0 106.8 %all-reduce.10.cloned.1.call-done = f32[4,512,512]{1,2,0:T(8,128)} async-done(((f32[4,512,512]{1,2,0:T(8,128)}), f32[4,512,512]{1,2,0:T(8,128)}) %all-reduce.10.cloned.1.call-update) | async-done | bytes 4194320 | tf_op jit(solution)/shard_map/psum | solution.py:12
  863.8 4.2 gather_fusion.2
  868.0 3.3 select_select_fusion.1
  871.5 5.6 bitcast_dynamic-update-slice_fusion.2
  877.1 56.3 %all-reduce.12.cloned.1.call-done = f32[2,512,512]{1,2,0:T(8,128)} async-done(((f32[2,512,512]{1,2,0:T(8,128)}), f32[2,512,512]{1,2,0:T(8,128)}) %all-reduce.12.cloned.1.call-update) | async-done | bytes 2097168 | tf_op jit(solution)/shard_map/psum | solution.py:12
  933.3 18.4 %select_subtract_fusion = f32[4,512,2,512]{1,3,2,0:T(8,128)S(1)} fusion(f32[4,512,2,512]{1,3,2,0:T(8,128)} %bitcast_dynamic-update-slice_fusion.2, pred[4,2]{1,0:T(4,128)(4,1)S(1)} %get-tuple-element.771, f32[4,512,512]{1,2,0:T(8,128)} %all-reduce.10.cloned.1.call-done, f32[2,512,512]{1,2,0:T(8,128)} %all-reduce.12.cloned.1.call-done), kind=kOutput, calls=%fused_computation.155 | convolution fusion | flops 12889096192 | bytes 23068680 | tf_op jit(solution)/shard_map/iab,jcb->iajc/dot_general | solution.py:122
  951.8 3.4 copy-done
  956.3 4.6 slice_bitcast_fusion.64
  960.9 57.7 %all-reduce.14.cloned.1.call-done = f32[512,512]{0,1:T(8,128)} async-done(((f32[512,512]{0,1:T(8,128)}), f32[512,512]{0,1:T(8,128)}) %all-reduce.14.cloned.1.call-update) | async-done | bytes 1048592 | tf_op jit(solution)/shard_map/psum | solution.py:12
  1021.6 11.7 cholesky.358
  1034.0 9.8 custom-call.31
  1044.6 11.7 cholesky.377
  1057.1 10.2 custom-call.32
  1067.9 11.7 cholesky.398
  1080.4 9.8 custom-call.33
  1090.8 11.9 cholesky.415
  1108.9 12.7 while.59
  1122.7 158.0 %custom-call.34 = f32[4,4,128,128]{2,3,1,0:T(8,128)S(1)} custom-call(f32[4,4,128,128]{3,2,1,0:T(8,128)} %bitcast.324), custom_call_target="InvertDiagBlocksLowerTriangular" | custom-call | tf_op jit(solution)/shard_map/triangular_solve/custom-call.3 | solution.py:109
  1286.6 2.7 fusion.36
  1290.4 3.6 fusion.30
  1295.2 4.4 broadcast_select_fusion.1
  1299.6 106.9 %all-reduce.16.cloned.1.call-done = f32[4,512,512]{1,2,0:T(8,128)} async-done(((f32[4,512,512]{1,2,0:T(8,128)}), f32[4,512,512]{1,2,0:T(8,128)}) %all-reduce.16.cloned.1.call-update) | async-done | bytes 4194320 | tf_op jit(solution)/shard_map/psum | solution.py:12
  1406.5 2.9 gather_fusion.3
  1411.1 5.4 bitcast_dynamic-update-slice_fusion.3
  1416.5 56.7 %all-reduce.18.cloned.1.call-done = f32[2,512,512]{1,2,0:T(8,128)} async-done(((f32[2,512,512]{1,2,0:T(8,128)}), f32[2,512,512]{1,2,0:T(8,128)}) %all-reduce.18.cloned.1.call-update) | async-done | bytes 2097168 | tf_op jit(solution)/shard_map/psum | solution.py:12
  1473.2 18.9 %subtract_bitcast_fusion = f32[4,1,512,2,1,512]{2,5,3,0,4,1:T(8,128)} fusion(f32[4,512,2,512]{1,3,2,0:T(8,128)} %bitcast_dynamic-update-slice_fusion.3, pred[4,2]{1,0:T(4,128)(4,1)S(1)} %get-tuple-element.770, f32[4,512,512]{1,2,0:T(8,128)} %all-reduce.16.cloned.1.call-done, f32[2,512,512]{1,2,0:T(8,128)} %all-reduce.18.cloned.1.call-done), kind=kOutput, calls=%fused_computation.154 | convolution fusion | flops 12889096192 | bytes 23068680 | tf_op jit(solution)/shard_map/iab,jcb->iajc/dot_general | solution.py:122
  1492.1 20.5 %copy.302 = f32[4,1,512,2,1,512]{5,4,3,2,1,0:T(1,128)} copy(f32[4,1,512,2,1,512]{2,5,3,0,4,1:T(8,128)} %subtract_bitcast_fusion) | data formatting | bytes 16777216 | tf_op jit(solution)/shard_map/reshape | solution.py:127
  (506 shorter events, 103.3 us)
Async XLA Ops:
  230.1 137.6 %all-to-all-start = ((f32[16,4,32,2,512]{4,2,3,1,0:T(8,128)}), f32[16,4,32,2,512]{4,2,3,1,0:T(8,128)}, u32[]{:S(2)}, u32[]{:S(2)}) async-start(f32[16,4,32,2,512]{4,2,3,1,0:T(8,128)} %get-tuple-element.463), calls=%async_computation | async-start | bytes 16777216 | tf_op jit(solution)/shard_map/all_to_all | solution.py:96
  236.1 230.4 %all-reduce.8.cloned.1.call-start = ((), (), s32[]{:S(2)}) async-start(), calls=%async_computation.1 | async-start | bytes 2097152 | tf_op jit(solution)/shard_map/psum | solution.py:12
  388.6 475.2 %all-reduce.10.cloned.1.call-start = ((), (), s32[]{:S(2)}) async-start(), calls=%async_computation.2 | async-start | bytes 8388608 | tf_op jit(solution)/shard_map/psum | solution.py:12
  578.2 1.1 copy-start.8
  737.3 2.7 copy-start.5
  737.3 7.3 copy-start.1
  742.4 4.7 copy-start.6
  748.2 4.9 copy-start.3
  753.1 1.0 copy-start.4
  756.9 176.4 %all-reduce.12.cloned.1.call-start = ((), (), s32[]{:S(2)}) async-start(), calls=%async_computation.3 | async-start | bytes 4194304 | tf_op jit(solution)/shard_map/psum | solution.py:12
  871.3 147.3 %all-reduce.14.cloned.1.call-start = ((), (), s32[]{:S(2)}) async-start(), calls=%async_computation.4 | async-start | bytes 2097152 | tf_op jit(solution)/shard_map/psum | solution.py:12
  951.8 3.4 copy-start
  956.3 450.2 %all-reduce.16.cloned.1.call-start = ((), (), s32[]{:S(2)}) async-start(), calls=%async_computation.5 | async-start | bytes 8388608 | tf_op jit(solution)/shard_map/psum | solution.py:12
  1121.6 1.1 copy-start.7
  1280.7 5.9 copy-start.2
  1286.6 8.5 slice-start
  1290.4 4.7 slice-start.1
  1299.6 173.6 %all-reduce.18.cloned.1.call-start = ((), (), s32[]{:S(2)}) async-start(), calls=%async_computation.6 | async-start | bytes 4194304 | tf_op jit(solution)/shard_map/psum | solution.py:12
Sparse Core Ops, SparseCore 0:
  388.7 77.7 all-reduce.7
  757.0 106.7 all-reduce.9
  871.4 61.8 all-reduce.11
  956.4 62.1 all-reduce.13
  1299.7 106.7 all-reduce.15
  1411.3 61.8 all-reduce.17
where the time goes:
time: 1530 us; the launch traced here: 1520 us
  waiting for transfers between devices  584 us (38%)
  other arithmetic  562 us (37%)
  blocking collectives  161 us (11%)
  local copies, waits for them, and re-layouts  113 us (7%)
  matrix products  71.2 us (5%)
  between operations  19.7 us (1%)
    psum x6, waiting for transfers between devices, broadcast(): return lax.psum(kept, axis)  452 us
    another operation x6, other arithmetic, shards(): lax.linalg.triangular_solve(repeated, column, left_side=False, lower=True...  321 us
    another operation x29, other arithmetic, shards(): diagonal_factor = jnp.linalg.cholesky(diagonal)  167 us
    all_to_all x1, waiting for transfers between devices, shards(): lax.all_to_all(outgoing, 'col', split_axis=0, concat_axis=2, tiled=True)  132 us
    all_gather x1, blocking collectives, shards(): lax.all_gather(points, ('row', 'col'), axis=2, tiled=True)  60.4 us
    all_gather x1, blocking collectives, shards(): lax.all_gather(weights, ('row', 'col'), axis=1, tiled=True)  58.3 us
    all_gather x1, blocking collectives, shards(): lax.all_gather(shift, ('row', 'col'), axis=0, tiled=True)  42.7 us
    dynamic_update_slice x16, other arithmetic, add_group(): return lax.dynamic_update_slice(buffer, placed, starts)  42 us
  transfers between devices with their start and end apart: 7, of which 7 were waited for; matrix products, arithmetic and copies ran while one was open for 2% of the time, Pallas kernels for 0%

commit v1 on v0

v1 whole, which is shorter than its diff:
```python
import functools

import jax
import jax.numpy as jnp
from jax import lax
from jax.experimental import pallas as pl
from jax.experimental.pallas import tpu as pltpu
from jax.sharding import PartitionSpec as P

SOFTENING_SQUARED = 0.0004
F32 = jnp.float32
BF16 = jnp.bfloat16
QUAD = 4
TILE = 512
FEAT = 48
LEAD = 1024
BASE = 128
STEP = 16
WINDOW = LEAD + BASE
HIGHEST = lax.Precision.HIGHEST


def split(value):
    high = value.astype(BF16)
    return high, (value - high.astype(F32)).astype(BF16)


def dot3(a_high, a_low, b_high, b_low):
    dot = functools.partial(jnp.dot, preferred_element_type=F32)
    return dot(a_high, b_high) + (dot(a_high, b_low) + dot(a_low, b_high))


def gather_shards(shard):
    rows, cols = lax.axis_size("row"), lax.axis_size("col")
    ys, xs = rows // 2, 4
    zs = cols // xs

    def send(value, move):
        pairs = []
        for source in range(rows * cols):
            row, col = divmod(source, cols)
            y, core, x, z = move(row // 2, row % 2, col // zs, col % zs)
            pairs.append((source, ((y % ys) * 2 + core % 2) * cols + (x % xs) * zs + z % zs))
        return lax.ppermute(value, ("row", "col"), pairs)

    held = shard[None]
    moves = [lambda y, c, x, z, k=k: (y, c, x, z + k) for k in range(1, zs)]
    held = jnp.concatenate([held] + [send(held, move) for move in moves], 0)
    moves = [lambda y, c, x, z, k=k: (y, c, x + k, z) for k in range(1, xs)]
    held = jnp.concatenate([held] + [send(held, move) for move in moves], 0)
    held = jnp.concatenate([held, send(held, lambda y, c, x, z: (y, c + 1, x, z))], 0)
    moves = [lambda y, c, x, z, k=k: (y + k, c, x, z) for k in range(1, ys)]
    return jnp.concatenate([held] + [send(held, move) for move in moves], 0)


def prep_kernel(where_ref, g0, g1, g2, g3, u_ref, v_ref, wr_ref, wc_ref, pad):
    geometry = jnp.concatenate([g0[...], g1[...], g2[...], g3[...]], axis=1)
    centred = geometry[0:12] - 0.5
    coarse = jnp.floor(centred * 256.0 + 0.5) * (1.0 / 256.0)
    fine = centred - coarse
    fine_high = fine.astype(BF16).astype(F32)
    fine_low = fine - fine_high
    per = lambda value: [value[4 * c : 4 * c + 4] for c in range(3)]
    coarse, fine, fine_high, fine_low = per(coarse), per(fine), per(fine_high), per(fine_low)
    norm = sum(c * c for c in coarse)
    norm_high = jnp.floor(norm * 256.0) * (1.0 / 256.0)
    norm_low = norm - norm_high
    mixed = sum(2.0 * c * f + f * f for c, f in zip(coarse, fine))

    def pieces(value):
        first = value.astype(BF16).astype(F32)
        second = (value - first).astype(BF16).astype(F32)
        return [first, second, value - first - second]

    one = jnp.ones_like(norm)
    twice = lambda values: [-2.0 * value for value in values]
    left = twice(coarse) + [norm_high, norm_low, one, one]
    left += twice(coarse) + twice(coarse) + twice(fine_high) + twice(fine_low)
    left += twice(fine_high) + twice(fine_high) + twice(fine_low)
    left += pieces(mixed) + [one] * 3
    right = coarse + [one, one, norm_high, norm_low]
    right += fine_high + fine_low + coarse + coarse
    right += fine_high + fine_low + fine_high
    right += [one] * 3 + pieces(mixed + SOFTENING_SQUARED)
    pad[...] = jnp.zeros_like(pad)
    for quad in range(QUAD):
        for k, value in enumerate(left):
            pad[k : k + 1, :] = value[quad : quad + 1, :]
        u_ref[quad] = jnp.transpose(pad[...])[:, :FEAT].astype(BF16)
        for k, value in enumerate(right):
            pad[k : k + 1, :] = value[quad : quad + 1, :]
        v_ref[quad] = pad[0:FEAT, :].astype(BF16)
    pad[0:8, :] = geometry[12:20]
    wr_ref[...] = jnp.transpose(pad[...])
    wc_ref[...] = geometry[12:20]


def assemble(u_ref, v_ref, wr_ref, wc_ref, left, right, start, count):
    rows = pl.ds(start, count)
    total = None
    for first in range(QUAD):
        part = None
        for second in range(QUAD):
            squared = jnp.dot(u_ref[left, first, rows, :], v_ref[right, second], preferred_element_type=F32)
            term = lax.rsqrt(squared) * wc_ref[right, second : second + 1, :]
            part = term if part is None else part + term
        part = part * wr_ref[left, rows, first : first + 1]
        total = part if total is None else total + part
    return total


def with_shift(values, wr_ref, tile, start, count):
    row = start + lax.broadcasted_iota(jnp.int32, (count, TILE), 0)
    col = lax.broadcasted_iota(jnp.int32, (count, TILE), 1)
    return values + jnp.where(row == col, wr_ref[tile, pl.ds(start, count), 4:5], 0.0)


def eliminate_base(work):
    for step in range(BASE // STEP):
        low = step * STEP
        block = work[low : low + STEP, :]
        left, right = block[:, :BASE], block[:, BASE:]
        spread = [jnp.broadcast_to(left[:, low + j : low + j + 1], (STEP, BASE)) for j in range(STEP)]
        full = lambda value, i: jnp.broadcast_to(value[i : i + 1, :], (8, BASE))
        m = [[full(spread[j], i) for j in range(i + 1)] for i in range(STEP)]
        a = [full(left, i) for i in range(STEP)]
        g = [full(right, i) for i in range(STEP)]
        for j in range(STEP):
            scale = lax.rsqrt(m[j][j])
            a[j] = a[j] * scale
            g[j] = g[j] * scale
            for i in range(j + 1, STEP):
                m[i][j] = m[i][j] * scale
            for i in range(j + 1, STEP):
                for k in range(j + 1, i + 1):
                    m[i][k] = m[i][k] - m[i][j] * m[k][j]
                a[i] = a[i] - m[i][j] * a[j]
                g[i] = g[i] - m[i][j] * g[j]
        for i in range(STEP):
            work[low + i : low + i + 1, :BASE] = a[i][0:1]
            work[low + i : low + i + 1, BASE:] = g[i][0:1]
        if low + STEP < BASE:
            done = work[low : low + STEP, :]
            rest = done[:, low + STEP : BASE]
            work[low + STEP :, :] = work[low + STEP :, :] - lax.dot_general(
                rest, done, (((0,), (0,)), ((), ())), precision=HIGHEST, preferred_element_type=F32
            )


def chain_kernel(u_ref, v_ref, wr_ref, wc_ref, ft_ref, hh_ref, hl_ref, th_ref, tl_ref, state, work):
    state[:, LEAD:] = jnp.zeros((LEAD, LEAD), F32)
    eye = (
        lax.broadcasted_iota(jnp.int32, (BASE, BASE), 0) == lax.broadcasted_iota(jnp.int32, (BASE, BASE), 1)
    ).astype(F32)
    for left, right in ((0, 0), (0, 1), (1, 1)):
        @pl.loop(0, TILE // 256)
        def _(chunk):
            start = pl.multiple_of(chunk * 256, 256)
            values = assemble(u_ref, v_ref, wr_ref, wc_ref, left, right, start, 256)
            if left == right:
                values = with_shift(values, wr_ref, left, start, 256)
            state[pl.ds(left * TILE + start, 256), right * TILE : (right + 1) * TILE] = values

    blocks = LEAD // BASE

    @pl.loop(0, blocks)
    def _(k):
        here = pl.multiple_of(k * BASE, BASE)
        rows = pl.ds(here, BASE)
        state[rows, pl.ds(pl.multiple_of(LEAD + here, BASE), BASE)] = eye
        work[:, :BASE] = state[rows, pl.ds(here, BASE)]
        work[:, BASE:] = eye
        eliminate_base(work)
        inverse = work[:, BASE:]
        window = pl.ds(here, WINDOW)
        state[rows, window] = jnp.dot(inverse, state[rows, window], precision=HIGHEST, preferred_element_type=F32)

        @pl.loop(k + 1, blocks)
        def _(i):
            below = pl.multiple_of(i * BASE, BASE)
            state[pl.ds(below, BASE), window] = state[pl.ds(below, BASE), window] - lax.dot_general(
                state[rows, pl.ds(below, BASE)],
                state[rows, window],
                (((0,), (0,)), ((), ())),
                precision=HIGHEST,
                preferred_element_type=F32,
            )

    ft_ref[...] = state[:, :LEAD]

    @pl.loop(0, blocks)
    def _(k):
        rows = pl.ds(pl.multiple_of(k * BASE, BASE), BASE)
        slab = state[rows, LEAD:]
        hh_ref[rows, :], hl_ref[rows, :] = split(slab)
        th_ref[:, rows], tl_ref[:, rows] = split(jnp.transpose(slab))


def weights_kernel(info, u_ref, v_ref, wr_ref, wc_ref, hh, hl, th, tl, yh_ref, yl_ref, ah, al, zh, zl):
    slot = pl.program_id(0)
    column = info[slot]
    panel = column < 2
    top, low = pl.ds(0, TILE), pl.ds(TILE, TILE)

    @pl.when(jnp.logical_not(panel))
    def _():
        for half in range(2):
            @pl.loop(0, TILE // 256)
            def _(chunk):
                start = pl.multiple_of(chunk * 256, 256)
                values = assemble(u_ref, v_ref, wr_ref, wc_ref, half, 6 + slot, start, 256)
                rows = pl.ds(half * TILE + start, 256)
                ah[rows, :], al[rows, :] = split(values)
        zh[top, :], zl[top, :] = split(dot3(hh[top, top], hl[top, top], ah[top, :], al[top, :]))
        zh[low, :], zl[low, :] = split(dot3(hh[low, :], hl[low, :], ah[...], al[...]))

    @pl.when(panel)
    def _():
        row = lax.broadcasted_iota(jnp.int32, (LEAD, TILE), 0)
        col = lax.broadcasted_iota(jnp.int32, (LEAD, TILE), 1)
        zh[...] = jnp.where(row == col + column * TILE, -1.0, 0.0).astype(BF16)
        zl[...] = jnp.zeros((LEAD, TILE), BF16)

    yh_ref[top, :], yl_ref[top, :] = split(dot3(th[top, :], tl[top, :], zh[...], zl[...]))
    yh_ref[low, :], yl_ref[low, :] = split(dot3(th[low, low], tl[low, low], zh[low, :], zl[low, :]))


CHUNK = 256
ZERO, UPDATE, DIAGONAL, PANEL, FACTOR = range(5)


def final_kernel(info, u_ref, v_ref, wr_ref, wc_ref, yh, yl, ft_ref, out_ref, ah, al):
    slot, chunk = pl.program_id(0), pl.program_id(1)
    start = pl.multiple_of(chunk * CHUNK, CHUNK)
    kinds = [info[2 + slot * 2], info[3 + slot * 2]]

    def store(j, values):
        for q in range(TILE // 128):
            out_ref[pl.ds(j * 4 + q, CHUNK, stride=8), :] = values[:, q * 128 : (q + 1) * 128]

    needed = lambda kind: (kind != ZERO) & (kind != FACTOR)

    @pl.when(needed(kinds[0]) | needed(kinds[1]))
    def _():
        for half in range(2):
            values = assemble(u_ref, v_ref, wr_ref, wc_ref, 2 + slot, half, start, CHUNK)
            cols = pl.ds(half * TILE, TILE)
            ah[:, cols], al[:, cols] = split(values)

    for j in range(2):
        kind = kinds[j]

        @pl.when(kind == ZERO)
        def _():
            store(j, jnp.zeros((CHUNK, TILE), F32))

        @pl.when(kind == PANEL)
        def _():
            store(j, -dot3(ah[...], al[...], yh[j], yl[j]))

        @pl.when((kind == UPDATE) | (kind == DIAGONAL))
        def _():
            values = assemble(u_ref, v_ref, wr_ref, wc_ref, 2 + slot, 6 + j, start, CHUNK)
            row = start + lax.broadcasted_iota(jnp.int32, (CHUNK, TILE), 0)
            col = lax.broadcasted_iota(jnp.int32, (CHUNK, TILE), 1)
            shift = wr_ref[2 + slot, pl.ds(start, CHUNK), 4:5]
            values = values + jnp.where((row == col) & (kind == DIAGONAL), shift, 0.0)
            store(j, values - dot3(ah[...], al[...], yh[j], yl[j]))

        if j == 0:
            @pl.when(kind == FACTOR)
            def _():
                which = info[10]
                lanes = pl.ds(pl.multiple_of(which // 2 * TILE + start, CHUNK), CHUNK)
                rows = pl.ds(pl.multiple_of(which % 2 * TILE, TILE), TILE)
                values = jnp.transpose(ft_ref[rows, lanes])
                row = start + lax.broadcasted_iota(jnp.int32, (CHUNK, TILE), 0)
                col = lax.broadcasted_iota(jnp.int32, (CHUNK, TILE), 1)
                keep = (row >= col) | (which // 2 != which % 2)
                store(j, jnp.where(keep, values, 0.0))


def whole(count):
    return [pl.BlockSpec(memory_space=pltpu.VMEM)] * count


def shards(points, weights, shift, cluster_rank):
    rows, cols = lax.axis_size("row"), lax.axis_size("col")
    row, col = lax.axis_index("row"), lax.axis_index("col")
    width = shift.shape[0]
    fill = jnp.zeros((7, width), F32)
    shard = jnp.concatenate([points.reshape(12, width), weights, shift[None], fill], 0)
    gathered = gather_shards(shard)

    slots = jnp.arange(4, dtype=jnp.int32)
    tile_rows = row + rows * slots
    tile_cols = col + cols * slots[:2]
    wanted = jnp.concatenate([slots[:2], tile_rows, tile_cols])
    clusters = jnp.arange(cluster_rank.shape[0], dtype=jnp.int32)
    found = jnp.sum(jnp.where(cluster_rank[None, :] == wanted[:, None], clusters[None, :], 0), axis=1)
    from_row, from_x = found // 4, found % 4
    dy = (row // 2 - from_row // 2) % 4
    dc = (row % 2 - from_row % 2) % 2
    dx = (col // 4 - from_x) % 4
    dz = (col % 4 - slots) % 4
    where = ((((dy * 2 + dc) * 4 + dx) * 4)[:, None] + dz[None, :]).reshape(-1).astype(jnp.int32)

    part = lambda z: pl.BlockSpec((None, 24, width), lambda t, at: (at[4 * t + z], 0, 0))
    u, v, wr, wc = pl.pallas_call(
        prep_kernel,
        grid_spec=pltpu.PrefetchScalarGridSpec(
            num_scalar_prefetch=1,
            grid=(8,),
            in_specs=[part(z) for z in range(4)],
            out_specs=[
                pl.BlockSpec((None, QUAD, TILE, FEAT), lambda t, at: (t, 0, 0, 0)),
                pl.BlockSpec((None, QUAD, FEAT, TILE), lambda t, at: (t, 0, 0, 0)),
                pl.BlockSpec((None, TILE, 128), lambda t, at: (t, 0, 0)),
                pl.BlockSpec((None, 8, TILE), lambda t, at: (t, 0, 0)),
            ],
            scratch_shapes=[pltpu.VMEM((128, TILE), F32)],
        ),
        out_shape=[
            jax.ShapeDtypeStruct((8, QUAD, TILE, FEAT), BF16),
            jax.ShapeDtypeStruct((8, QUAD, FEAT, TILE), BF16),
            jax.ShapeDtypeStruct((8, TILE, 128), F32),
            jax.ShapeDtypeStruct((8, 8, TILE), F32),
        ],
        name="prep",
    )(where, *[gathered] * 4)

    square = jax.ShapeDtypeStruct((LEAD, LEAD), BF16)
    ft, hh, hl, th, tl = pl.pallas_call(
        chain_kernel,
        in_specs=whole(4),
        out_specs=whole(5),
        out_shape=[jax.ShapeDtypeStruct((LEAD, LEAD), F32)] + [square] * 4,
        scratch_shapes=[pltpu.VMEM((LEAD, 2 * LEAD), F32), pltpu.VMEM((BASE, 2 * BASE), F32)],
        name="chain",
    )(u, v, wr, wc)

    block_rows, block_cols = tile_rows[:, None], tile_cols[None, :]
    kinds = jnp.where(
        block_rows < block_cols,
        ZERO,
        jnp.where(
            block_cols >= 2,
            jnp.where(block_rows == block_cols, DIAGONAL, UPDATE),
            jnp.where(block_rows < 2, FACTOR, PANEL),
        ),
    )
    info = jnp.concatenate([tile_cols, kinds.reshape(-1), (row * 2 + col)[None]]).astype(jnp.int32)

    half = jax.ShapeDtypeStruct((2, LEAD, TILE), BF16)
    yh, yl = pl.pallas_call(
        weights_kernel,
        grid_spec=pltpu.PrefetchScalarGridSpec(
            num_scalar_prefetch=1,
            grid=(2,),
            in_specs=whole(8),
            out_specs=[pl.BlockSpec((None, LEAD, TILE), lambda j, info: (j, 0, 0))] * 2,
            scratch_shapes=[pltpu.VMEM((LEAD, TILE), BF16)] * 4,
        ),
        out_shape=[half, half],
        name="weights",
    )(info, u, v, wr, wc, hh, hl, th, tl)

    lines = CHUNK * 8
    out = pl.pallas_call(
        final_kernel,
        grid_spec=pltpu.PrefetchScalarGridSpec(
            num_scalar_prefetch=1,
            grid=(4, TILE // CHUNK),
            in_specs=whole(7),
            out_specs=pl.BlockSpec((lines, 128), lambda i, h, info: (i * (TILE // CHUNK) + h, 0)),
            scratch_shapes=[pltpu.VMEM((CHUNK, LEAD), BF16)] * 2,
        ),
        out_shape=jax.ShapeDtypeStruct((4 * TILE * 8, 128), F32),
        name="final",
    )(info, u, v, wr, wc, yh, yl, ft)
    return out.reshape(4, 1, TILE, 2, 1, TILE)


def solution(mesh):
    return jax.shard_map(
        shards,
        mesh=mesh,
        in_specs=(P(None, None, ("row", "col")), P(None, ("row", "col")), P(("row", "col")), P()),
        out_specs=P(None, "row", None, None, "col", None),
        check_vma=False,
    )
```

time: 1530 us -> 227 us (0.15)
  waiting for transfers between devices: 584 us -> 21.1 us
  other arithmetic: 562 us -> 3.3 us
  Pallas kernels: 0 us -> 184 us
  blocking collectives: 161 us -> 0 us
  local copies, waits for them, and re-layouts: 113 us -> 2.82 us
  matrix products: 71.2 us -> 0 us
  between operations: 19.7 us -> 0.17 us
    another operation x35 -> x0, other arithmetic: 488 us -> none  [the longest x6 321 us: shards(): lax.linalg.triangular_solve(repeated, column, left_side=False, lower=True...]
    psum x6 -> x0, waiting for transfers between devices: 452 us -> none  [broadcast(): return lax.psum(kept, axis)]
    pallas_call x0 -> x4, Pallas kernels: none -> 184 us  [the longest x1 90.3 us: shards(): pl.pallas_call(chain_kernel, in_specs=whole(4), out_specs=whole(5), out_s...]
    all_gather x3 -> x0, blocking collectives: 161 us -> none  [the longest x1 60.4 us: shards(): lax.all_gather(points, ('row', 'col'), axis=2, tiled=True)]
    all_to_all x1 -> x0, waiting for transfers between devices: 132 us -> none  [shards(): lax.all_to_all(outgoing, 'col', split_axis=0, concat_axis=2, tiled=True)]
    dynamic_update_slice x16 -> x0, other arithmetic: 42 us -> none  [add_group(): return lax.dynamic_update_slice(buffer, placed, starts)]
    dot_general x2 -> x0, matrix products: 37.4 us -> none  [shards(): jnp.einsum('iab,jcb->iajc', row_factors, col_factors, precision=lax.Preci...]
    another operation x26 -> x0, matrix products: 33.8 us -> none  [the longest x14 30.1 us: shards(): lax.linalg.triangular_solve(repeated, column, left_side=False, lower=True...]
  transfers between devices with their start and end apart: 7 -> 10, of which waited for: 7 -> 5; matrix products, arithmetic and copies ran while one was open for 2% -> 1% of each run, Pallas kernels for 0% -> 0%
where the time goes in v1:
time: 227 us; the launch traced here: 226 us
  Pallas kernels  184 us (81%)
  waiting for transfers between devices  21.1 us (9%)
  starting transfers between devices  14.2 us (6%)
  other arithmetic  3.3 us (1%)
  local copies, waits for them, and re-layouts  2.82 us (1%)
    pallas_call x1, Pallas kernels, shards(): pl.pallas_call(chain_kernel, in_specs=whole(4), out_specs=whole(5), out_s...  90.3 us
    pallas_call x1, Pallas kernels, shards(): pl.pallas_call(final_kernel, grid_spec=pltpu.PrefetchScalarGridSpec(num_s...  56.8 us
    pallas_call x1, Pallas kernels, shards(): pl.pallas_call(weights_kernel, grid_spec=pltpu.PrefetchScalarGridSpec(num...  29.6 us
    ppermute x10, waiting for transfers between devices, send(): return lax.ppermute(value, ('row', 'col'), pairs)  21.1 us
    ppermute x10, starting transfers between devices, send(): return lax.ppermute(value, ('row', 'col'), pairs)  14.2 us
    pallas_call x1, Pallas kernels, shards(): pl.pallas_call(prep_kernel, grid_spec=pltpu.PrefetchScalarGridSpec(num_sc...  7.58 us
  transfers between devices with their start and end apart: 10, of which 5 were waited for; matrix products, arithmetic and copies ran while one was open for 1% of the time, Pallas kernels for 0%

profile of v1, /device:TPU:73, one launch (start us, length us, event | category | flops | bytes accessed | tf_op | source)
XLA Modules:
  0.0 225.9 jit_solution(14681395161605345205)
XLA Ops:
  0.0 0.7 reshape.151
  0.7 0.1 pad.7.clone
  0.8 0.8 maximum_bitcast_fusion
  1.5 0.0 collective-permute-start.2
  1.6 3.1 %collective-permute-start.1 = (f32[1,24,128]{2,1,0:T(8,128)S(1)}, f32[1,24,128]{2,1,0:T(8,128)S(1)}, u32[]{:S(2)}, u32[]{:S(2)}) collective-permute-start(f32[1,24,128]{2,1,0:T(8,128)S(1)} %maximum_bitcast_fusion), channel_id=1, source_target_pairs={{0,2},{1,3},{2,0},{3,1},{4,6},{5,7},{6,4},{7,5},{8,10},{9,11},{10,... | collective-permute-start | bytes 36872 | tf_op jit(solution)/shard_map/ppermute | solution.py:44
  4.7 0.0 collective-permute-start
  4.7 0.8 constant_dynamic-update-slice_fusion.14
  5.5 0.1 pad_add_fusion.1
  5.6 0.8 select_reduce_fusion
  6.5 0.0 collective-permute-done.2
  6.5 0.0 collective-permute-done.1
  6.5 0.8 collective-permute-done
  7.2 2.5 %collective-permute-start.5 = (f32[4,24,128]{2,1,0:T(8,128)S(1)}, f32[4,24,128]{2,1,0:T(8,128)S(1)}, u32[]{:S(2)}, u32[]{:S(2)}) collective-permute-start(f32[4,24,128]{2,1,0:T(8,128)S(1)} %pad_maximum_fusion), channel_id=1, source_target_pairs={{0,12},{1,13},{2,14},{3,15},{4,0},{5,1},{6,2},{7,3},{8,4},{9,5},{1... | collective-permute-start | bytes 147464 | tf_op jit(solution)/shard_map/ppermute | solution.py:44
  9.7 0.5 collective-permute-start.4
  10.2 0.6 collective-permute-start.3
  10.9 3.8 %collective-permute-done.3 = f32[4,24,128]{2,1,0:T(8,128)S(1)} collective-permute-done((f32[4,24,128]{2,1,0:T(8,128)S(1)}, f32[4,24,128]{2,1,0:T(8,128)S(1)}, u32[]{:S(2)}, u32[]{:S(2)}) %collective-permute-start.3) | collective-permute-done | bytes 49184 | tf_op jit(solution)/shard_map/ppermute | solution.py:44
  14.7 0.0 collective-permute-done.4
  14.7 0.0 collective-permute-done.5
  14.8 3.9 %collective-permute-start.6 = (f32[16,24,128]{2,1,0:T(8,128)S(1)}, f32[16,24,128]{2,1,0:T(8,128)S(1)}, u32[]{:S(2)}, u32[]{:S(2)}) collective-permute-start(f32[16,24,128]{2,1,0:T(8,128)S(1)} %get-tuple-element.33), channel_id=1, source_target_pairs={{0,16},{1,17},{2,18},{3,19},{4,20},{5,21},{6,22},{7,23},{8,24},{9,... | collective-permute-start | bytes 589832 | tf_op jit(solution)/shard_map/ppermute | solution.py:44
  18.7 1.0 collective-permute-done.6
  19.8 1.4 collective-permute-start.7
  21.1 0.1 broadcast_add_fusion
  21.2 0.2 collective-permute-start.9
  21.4 2.0 collective-permute-start.8
  23.4 0.1 select_select_fusion
  23.5 0.1 select_n.123
  23.5 0.7 add.142.where_ref
  24.2 0.6 pad_add_fusion.info
  24.8 5.3 %collective-permute-done.7 = f32[32,24,128]{2,1,0:T(8,128)S(1)} collective-permute-done((f32[32,24,128]{2,1,0:T(8,128)S(1)}, f32[32,24,128]{2,1,0:T(8,128)S(1)}, u32[]{:S(2)}, u32[]{:S(2)}) %collective-permute-start.7) | collective-permute-done | bytes 393248 | tf_op jit(solution)/shard_map/ppermute | solution.py:44
  30.2 10.2 %collective-permute-done.8 = f32[32,24,128]{2,1,0:T(8,128)S(1)} collective-permute-done((f32[32,24,128]{2,1,0:T(8,128)S(1)}, f32[32,24,128]{2,1,0:T(8,128)S(1)}, u32[]{:S(2)}, u32[]{:S(2)}) %collective-permute-start.8) | collective-permute-done | bytes 393248 | tf_op jit(solution)/shard_map/ppermute | solution.py:44
  40.4 0.0 collective-permute-done.9
  40.4 0.0 copy-start
  40.5 1.1 copy-done
  41.6 7.6 %prep.1 = (bf16[8,4,512,48]{3,2,1,0:T(8,128)(2,1)}, bf16[8,4,48,512]{3,2,1,0:T(8,128)(2,1)}, f32[8,512,128]{2,1,0:T(8,128)}, f32[8,8,512]{2,1,0:T(8,128)}) custom-call(s32[32]{0:T(128)} %add.142.where_ref, f32[128,24,128]{2,1,0:T(8,128)} %copy-done, f32[128,24,128]{2,1,0:T(8,128)} %copy-done, f32[128,24,128]{2,1,0:T(8,128)} %copy-done, f32[128,24,128]{2,1,0:T(8,128)} %copy-done), custom_call_target="tpu_custom_call" | custom-call | tf_op jit(solution)/shard_map/prep/pallas_call | solution.py:309
  49.2 90.3 %chain.1 = (f32[1024,1024]{1,0:T(8,128)}, bf16[1024,1024]{1,0:T(8,128)(2,1)}, bf16[1024,1024]{1,0:T(8,128)(2,1)}, bf16[1024,1024]{1,0:T(8,128)(2,1)}, bf16[1024,1024]{1,0:T(8,128)(2,1)}) custom-call(bf16[8,4,512,48]{3,2,1,0:T(8,128)(2,1)} %get-tuple-element.16.u_ref, bf16[8,4,48,512]{3,2,1,0:T(8,128)(2,1)} %get-tuple-element.17.v_ref, ...), custom_call_target="tpu_custom_call" | custom-call | tf_op jit(solution)/shard_map/chain/pallas_call | solution.py:333
  139.5 29.6 %weights.1 = (bf16[2,1024,512]{2,1,0:T(8,128)(2,1)}, bf16[2,1024,512]{2,1,0:T(8,128)(2,1)}) custom-call(s32[11]{0:T(128)} %pad_add_fusion.info, bf16[8,4,512,48]{3,2,1,0:T(8,128)(2,1)} %get-tuple-element.16.u_ref, bf16[8,4,48,512]{3,2,1,0:T(8,128)(2,1)} %get-tuple-element.17.v_ref, f32[8,512,128]{2,1,0:T(8,128)} %get-tuple-element.18.wr_ref, ...), custom_call_target="tpu_custom_call" | custom-call | tf_op jit(solution)/shard_map/weights/pallas_call | solution.py:355
  169.1 56.8 %final.1 = f32[16384,128]{1,0:T(8,128)} custom-call(s32[11]{0:T(128)} %pad_add_fusion.info, bf16[8,4,512,48]{3,2,1,0:T(8,128)(2,1)} %get-tuple-element.16.u_ref, bf16[8,4,48,512]{3,2,1,0:T(8,128)(2,1)} %get-tuple-element.17.v_ref, f32[8,512,128]{2,1,0:T(8,128)} %get-tuple-element.18.wr_ref, f32[8,8,512]{2,1,0:T(8,128)} %get-tuple-element.19.wc_ref, ...), custom_call_target="tpu_custom_call" | custom-call | tf_op jit(solution)/shard_map/final/pallas_call | solution.py:369
  (17 shorter events, 0.2 us)
Async XLA Ops:
  1.5 4.9 %collective-permute-start.2 = (f32[1,24,128]{2,1,0:T(8,128)S(1)}, f32[1,24,128]{2,1,0:T(8,128)S(1)}, u32[]{:S(2)}, u32[]{:S(2)}) collective-permute-start(f32[1,24,128]{2,1,0:T(8,128)S(1)} %maximum_bitcast_fusion), channel_id=1, source_target_pairs={{0,3},{1,0},{2,1},{3,2},{4,7},{5,4},{6,5},{7,6},{8,11},{9,8},{10,9... | collective-permute-start | bytes 36872 | tf_op jit(solution)/shard_map/ppermute | solution.py:44
  1.6 4.9 %collective-permute-start.1 = (f32[1,24,128]{2,1,0:T(8,128)S(1)}, f32[1,24,128]{2,1,0:T(8,128)S(1)}, u32[]{:S(2)}, u32[]{:S(2)}) collective-permute-start(f32[1,24,128]{2,1,0:T(8,128)S(1)} %maximum_bitcast_fusion), channel_id=1, source_target_pairs={{0,2},{1,3},{2,0},{3,1},{4,6},{5,7},{6,4},{7,5},{8,10},{9,11},{10,... | collective-permute-start | bytes 36872 | tf_op jit(solution)/shard_map/ppermute | solution.py:44
  4.7 2.5 %collective-permute-start = (f32[1,24,128]{2,1,0:T(8,128)S(1)}, f32[1,24,128]{2,1,0:T(8,128)S(1)}, u32[]{:S(2)}, u32[]{:S(2)}) collective-permute-start(f32[1,24,128]{2,1,0:T(8,128)S(1)} %maximum_bitcast_fusion), channel_id=1, source_target_pairs={{0,1},{1,2},{2,3},{3,0},{4,5},{5,6},{6,7},{7,4},{8,9},{9,10},{10,1... | collective-permute-start | bytes 36872 | tf_op jit(solution)/shard_map/ppermute | solution.py:44
  7.2 7.5 %collective-permute-start.5 = (f32[4,24,128]{2,1,0:T(8,128)S(1)}, f32[4,24,128]{2,1,0:T(8,128)S(1)}, u32[]{:S(2)}, u32[]{:S(2)}) collective-permute-start(f32[4,24,128]{2,1,0:T(8,128)S(1)} %pad_maximum_fusion), channel_id=1, source_target_pairs={{0,12},{1,13},{2,14},{3,15},{4,0},{5,1},{6,2},{7,3},{8,4},{9,5},{1... | collective-permute-start | bytes 147464 | tf_op jit(solution)/shard_map/ppermute | solution.py:44
  9.7 5.0 %collective-permute-start.4 = (f32[4,24,128]{2,1,0:T(8,128)S(1)}, f32[4,24,128]{2,1,0:T(8,128)S(1)}, u32[]{:S(2)}, u32[]{:S(2)}) collective-permute-start(f32[4,24,128]{2,1,0:T(8,128)S(1)} %pad_maximum_fusion), channel_id=1, source_target_pairs={{0,8},{1,9},{2,10},{3,11},{4,12},{5,13},{6,14},{7,15},{8,0},{9,1},... | collective-permute-start | bytes 147464 | tf_op jit(solution)/shard_map/ppermute | solution.py:44
  10.2 4.5 %collective-permute-start.3 = (f32[4,24,128]{2,1,0:T(8,128)S(1)}, f32[4,24,128]{2,1,0:T(8,128)S(1)}, u32[]{:S(2)}, u32[]{:S(2)}) collective-permute-start(f32[4,24,128]{2,1,0:T(8,128)S(1)} %pad_maximum_fusion), channel_id=1, source_target_pairs={{0,4},{1,5},{2,6},{3,7},{4,8},{5,9},{6,10},{7,11},{8,12},{9,13},{1... | collective-permute-start | bytes 147464 | tf_op jit(solution)/shard_map/ppermute | solution.py:44
  14.8 5.0 %collective-permute-start.6 = (f32[16,24,128]{2,1,0:T(8,128)S(1)}, f32[16,24,128]{2,1,0:T(8,128)S(1)}, u32[]{:S(2)}, u32[]{:S(2)}) collective-permute-start(f32[16,24,128]{2,1,0:T(8,128)S(1)} %get-tuple-element.33), channel_id=1, source_target_pairs={{0,16},{1,17},{2,18},{3,19},{4,20},{5,21},{6,22},{7,23},{8,24},{9,... | collective-permute-start | bytes 589832 | tf_op jit(solution)/shard_map/ppermute | solution.py:44
  19.8 10.4 %collective-permute-start.7 = (f32[32,24,128]{2,1,0:T(8,128)S(1)}, f32[32,24,128]{2,1,0:T(8,128)S(1)}, u32[]{:S(2)}, u32[]{:S(2)}) collective-permute-start(f32[32,24,128]{2,1,0:T(8,128)S(1)} %get-tuple-element.29), channel_id=1, source_target_pairs={{0,32},{1,33},{2,34},{3,35},{4,36},{5,37},{6,38},{7,39},{8,40},{9,... | collective-permute-start | bytes 1179656 | tf_op jit(solution)/shard_map/ppermute | solution.py:44
  21.2 19.2 %collective-permute-start.9 = (f32[32,24,128]{2,1,0:T(8,128)S(1)}, f32[32,24,128]{2,1,0:T(8,128)S(1)}, u32[]{:S(2)}, u32[]{:S(2)}) collective-permute-start(f32[32,24,128]{2,1,0:T(8,128)S(1)} %get-tuple-element.29), channel_id=1, source_target_pairs={{0,96},{1,97},{2,98},{3,99},{4,100},{5,101},{6,102},{7,103},{8,104... | collective-permute-start | bytes 1179656 | tf_op jit(solution)/shard_map/ppermute | solution.py:44
  21.4 19.0 %collective-permute-start.8 = (f32[32,24,128]{2,1,0:T(8,128)S(1)}, f32[32,24,128]{2,1,0:T(8,128)S(1)}, u32[]{:S(2)}, u32[]{:S(2)}) collective-permute-start(f32[32,24,128]{2,1,0:T(8,128)S(1)} %get-tuple-element.29), channel_id=1, source_target_pairs={{0,64},{1,65},{2,66},{3,67},{4,68},{5,69},{6,70},{7,71},{8,72},{9,... | collective-permute-start | bytes 1179656 | tf_op jit(solution)/shard_map/ppermute | solution.py:44
  40.4 1.1 copy-start

commit v2 on v1

--- a/solution.py
+++ b/solution.py
@@ -48,9 +48,9 @@
     held = jnp.concatenate([held] + [send(held, move) for move in moves], 0)
     moves = [lambda y, c, x, z, k=k: (y, c, x + k, z) for k in range(1, xs)]
     held = jnp.concatenate([held] + [send(held, move) for move in moves], 0)
-    held = jnp.concatenate([held, send(held, lambda y, c, x, z: (y, c + 1, x, z))], 0)
     moves = [lambda y, c, x, z, k=k: (y + k, c, x, z) for k in range(1, ys)]
-    return jnp.concatenate([held] + [send(held, move) for move in moves], 0)
+    held = jnp.concatenate([held] + [send(held, move) for move in moves], 0)
+    return jnp.concatenate([held, send(held, lambda y, c, x, z: (y, c + 1, x, z))], 0)
 
 
 def prep_kernel(where_ref, g0, g1, g2, g3, u_ref, v_ref, wr_ref, wc_ref, pad):
@@ -95,14 +95,14 @@
     wc_ref[...] = geometry[12:20]
 
 
-def assemble(u_ref, v_ref, wr_ref, wc_ref, left, right, start, count):
+def assemble(u_ref, v_ref, wr_ref, wc_ref, left, right, start, count, cols=slice(0, TILE)):
     rows = pl.ds(start, count)
     total = None
     for first in range(QUAD):
         part = None
         for second in range(QUAD):
-            squared = jnp.dot(u_ref[left, first, rows, :], v_ref[right, second], preferred_element_type=F32)
-            term = lax.rsqrt(squared) * wc_ref[right, second : second + 1, :]
+            squared = jnp.dot(u_ref[left, first, rows, :], v_ref[right, second, :, cols], preferred_element_type=F32)
+            term = lax.rsqrt(squared) * wc_ref[right, second : second + 1, cols]
             part = term if part is None else part + term
         part = part * wr_ref[left, rows, first : first + 1]
         total = part if total is None else total + part
@@ -115,43 +115,85 @@
     return values + jnp.where(row == col, wr_ref[tile, pl.ds(start, count), 4:5], 0.0)
 
 
-def eliminate_base(work):
+def split3(value):
+    first = value.astype(BF16)
+    rest = value - first.astype(F32)
+    second = rest.astype(BF16)
+    return first, second, (rest - second.astype(F32)).astype(BF16)
+
+
+def dot_rows(left, right):
+    return lax.dot_general(left, right, (((0,), (0,)), ((), ())), preferred_element_type=F32)
+
+
+def eliminate_base(work, spread, solved, lines):
+    lane = lax.broadcasted_iota(jnp.int32, (8, BASE), 1)
+    sub = lax.broadcasted_iota(jnp.int32, (8, BASE), 0)
+    repeat = lambda ref, i: ref[pl.ds(i, 8, stride=0), :]
     for step in range(BASE // STEP):
         low = step * STEP
-        block = work[low : low + STEP, :]
-        left, right = block[:, :BASE], block[:, BASE:]
-        spread = [jnp.broadcast_to(left[:, low + j : low + j + 1], (STEP, BASE)) for j in range(STEP)]
-        full = lambda value, i: jnp.broadcast_to(value[i : i + 1, :], (8, BASE))
-        m = [[full(spread[j], i) for j in range(i + 1)] for i in range(STEP)]
-        a = [full(left, i) for i in range(STEP)]
-        g = [full(right, i) for i in range(STEP)]
+        high = low + STEP
+        a, c = [], [[], []]
+        for half in range(2):
+            left = work[low + 8 * half : low + 8 * half + 8, :]
+            for j in range(STEP):
+                column = jnp.broadcast_to(left[:, low + j : low + j + 1], (8, BASE))
+                c[half].append(column)
+            inside = (lane >= low) & (lane < high)
+            a.append(jnp.where(inside, jnp.where(lane == sub + (low + 8 * half), 1.0, 0.0), left))
+            lines[8 * half : 8 * half + 8, :] = a[half]
+        d = []
+        for half in range(2):
+            diagonal = c[half][8 * half]
+            for j in range(8 * half + 1, 8 * half + 8):
+                diagonal = jnp.where(sub == j % 8, c[half][j], diagonal)
+            d.append(diagonal)
+            spread[0, 8 * half : 8 * half + 8, :] = diagonal
+        pivot = repeat(spread.at[0], 0)
         for j in range(STEP):
-            scale = lax.rsqrt(m[j][j])
-            a[j] = a[j] * scale
-            g[j] = g[j] * scale
-            for i in range(j + 1, STEP):
-                m[i][j] = m[i][j] * scale
-            for i in range(j + 1, STEP):
-                for k in range(j + 1, i + 1):
-                    m[i][k] = m[i][k] - m[i][j] * m[k][j]
-                a[i] = a[i] - m[i][j] * a[j]
-                g[i] = g[i] - m[i][j] * g[j]
-        for i in range(STEP):
-            work[low + i : low + i + 1, :BASE] = a[i][0:1]
-            work[low + i : low + i + 1, BASE:] = g[i][0:1]
-        if low + STEP < BASE:
-            done = work[low : low + STEP, :]
-            rest = done[:, low + STEP : BASE]
-            work[low + STEP :, :] = work[low + STEP :, :] - lax.dot_general(
-                rest, done, (((0,), (0,)), ((), ())), precision=HIGHEST, preferred_element_type=F32
+            scale = lax.rsqrt(pivot)
+            first = j // 8
+            line = repeat(lines, j) * scale
+            for half in range(first, 2):
+                c[half][j] = c[half][j] * scale
+                solved[j, 8 * half : 8 * half + 8, :] = c[half][j]
+                if j + 2 < STEP:
+                    d[half] = d[half] - c[half][j] * c[half][j]
+                    spread[j + 1, 8 * half : 8 * half + 8, :] = d[half]
+            for k in range(j + 1, STEP):
+                factor = repeat(solved.at[j], k)
+                if k == j + 1:
+                    pivot = repeat(spread.at[j], k) - factor * factor
+                for half in range(k // 8, 2):
+                    c[half][k] = c[half][k] - c[half][j] * factor
+            for half in range(first, 2):
+                update = a[half] - c[half][j] * line
+                if half == first:
+                    update = jnp.where(sub > j % 8, update, jnp.where(sub == j % 8, line, a[half]))
+                a[half] = update
+                lines[8 * half : 8 * half + 8, :] = update
+        for half in range(2):
+            work[low + 8 * half : low + 8 * half + 8, :] = a[half]
+        if high < BASE:
+            w0, w1, w2 = split3(jnp.concatenate(a, 0))
+            product = dot_rows(
+                jnp.concatenate([w0, w0, w1, w0, w1, w2], 0), jnp.concatenate([w0, w1, w0, w2, w1, w0], 0)
             )
-
-
-def chain_kernel(u_ref, v_ref, wr_ref, wc_ref, ft_ref, hh_ref, hl_ref, th_ref, tl_ref, state, work):
-    state[:, LEAD:] = jnp.zeros((LEAD, LEAD), F32)
-    eye = (
-        lax.broadcasted_iota(jnp.int32, (BASE, BASE), 0) == lax.broadcasted_iota(jnp.int32, (BASE, BASE), 1)
-    ).astype(F32)
+            rest = lax.broadcasted_iota(jnp.int32, (BASE - high, BASE), 1)
+            kept = jnp.where((rest >= low) & (rest < high), 0.0, work[high:, :])
+            work[high:, :] = kept - product[high:, :]
+
+
+def chain_kernel(
+    u_ref, v_ref, wr_ref, wc_ref,
+    ft_ref, hh_ref, hl_ref, th_ref, tl_ref,
+    state, work, spread, solved, lines, stack, tall,
+):
+    state[:, LEAD:] = jnp.zeros((LEAD + BASE, LEAD), F32)
+    state[LEAD:, :LEAD] = jnp.zeros((BASE, LEAD), F32)
+    lane = lax.broadcasted_iota(jnp.int32, (BASE, BASE), 1)
+    row = lax.broadcasted_iota(jnp.int32, (BASE, BASE), 0)
+    eye = (row == lane).astype(F32)
     for left, right in ((0, 0), (0, 1), (1, 1)):
         @pl.loop(0, TILE // 256)
         def _(chunk):
@@ -168,25 +210,52 @@
         here = pl.multiple_of(k * BASE, BASE)
         rows = pl.ds(here, BASE)
         state[rows, pl.ds(pl.multiple_of(LEAD + here, BASE), BASE)] = eye
-        work[:, :BASE] = state[rows, pl.ds(here, BASE)]
-        work[:, BASE:] = eye
-        eliminate_base(work)
-        inverse = work[:, BASE:]
+        work[...] = state[rows, pl.ds(here, BASE)]
+
+        eliminate_base(work, spread, solved, lines)
+        l0, l1, l2 = split3(jnp.where(row >= lane, work[...], 0.0))
         window = pl.ds(here, WINDOW)
-        state[rows, window] = jnp.dot(inverse, state[rows, window], precision=HIGHEST, preferred_element_type=F32)
-
-        @pl.loop(k + 1, blocks)
+
+        def load(values):
+            first, second, third = split3(values)
+            stack[0:128, :] = first
+            stack[128:256, :] = second
+            stack[256:384, :] = third
+            stack[384:512, :] = first
+
+        load(state[rows, window])
+        both = jnp.concatenate
+        two = jnp.dot(
+            both([both([l0, l0], 1), both([l1, l1], 1)], 0), stack[0:256, :], preferred_element_type=F32
+        )
+        one = jnp.dot(both([l0, l2], 1), stack[256:512, :], preferred_element_type=F32)
+        done = two[:BASE] + (two[BASE:] + one)
+        state[rows, window] = done
+        load(done)
+
+        @pl.loop(0, blocks - 1 - k)
         def _(i):
-            below = pl.multiple_of(i * BASE, BASE)
-            state[pl.ds(below, BASE), window] = state[pl.ds(below, BASE), window] - lax.dot_general(
-                state[rows, pl.ds(below, BASE)],
-                state[rows, window],
-                (((0,), (0,)), ((), ())),
-                precision=HIGHEST,
-                preferred_element_type=F32,
-            )
-
-    ft_ref[...] = state[:, :LEAD]
+            there = pl.multiple_of((i + 1) * BASE, BASE)
+            first, second, third = split3(jnp.transpose(state[rows, pl.ds(pl.multiple_of(here + there, BASE), BASE)]))
+            part = pl.ds(pl.multiple_of(i * BASE, BASE), BASE)
+            tall[part, 0:128] = first
+            tall[part, 128:256] = first
+            tall[part, 256:384] = second
+            tall[part, 384:512] = second
+            tall[part, 512:640] = first
+            tall[part, 640:768] = third
+
+        @pl.loop(0, (blocks - k) // 2)
+        def _(pair):
+            part = pl.ds(pl.multiple_of(pair * 256, 256), 256)
+            below = pl.ds(pl.multiple_of(here + BASE + pair * 256, BASE), 256)
+            dot = functools.partial(jnp.dot, preferred_element_type=F32)
+            update = dot(tall[part, 0:256], stack[0:256, :])
+            update += dot(tall[part, 256:512], stack[0:256, :])
+            update += dot(tall[part, 512:768], stack[256:512, :])
+            state[below, window] = state[below, window] - update
+
+    ft_ref[...] = state[:LEAD, :LEAD]
 
     @pl.loop(0, blocks)
     def _(k):
@@ -303,7 +372,7 @@
     dc = (row % 2 - from_row % 2) % 2
     dx = (col // 4 - from_x) % 4
     dz = (col % 4 - slots) % 4
-    where = ((((dy * 2 + dc) * 4 + dx) * 4)[:, None] + dz[None, :]).reshape(-1).astype(jnp.int32)
+    where = ((((dc * 4 + dy) * 4 + dx) * 4)[:, None] + dz[None, :]).reshape(-1).astype(jnp.int32)
 
     part = lambda z: pl.BlockSpec((None, 24, width), lambda t, at: (at[4 * t + z], 0, 0))
     u, v, wr, wc = pl.pallas_call(
@@ -335,7 +404,15 @@
         in_specs=whole(4),
         out_specs=whole(5),
         out_shape=[jax.ShapeDtypeStruct((LEAD, LEAD), F32)] + [square] * 4,
-        scratch_shapes=[pltpu.VMEM((LEAD, 2 * LEAD), F32), pltpu.VMEM((BASE, 2 * BASE), F32)],
+        scratch_shapes=[
+            pltpu.VMEM((LEAD + BASE, 2 * LEAD), F32),
+            pltpu.VMEM((BASE, BASE), F32),
+            pltpu.VMEM((STEP, STEP, BASE), F32),
+            pltpu.VMEM((STEP, STEP, BASE), F32),
+            pltpu.VMEM((STEP, BASE), F32),
+            pltpu.VMEM((4 * BASE, WINDOW), BF16),
+            pltpu.VMEM((LEAD, 6 * BASE), BF16),
+        ],
         name="chain",
     )(u, v, wr, wc)
 

time: 227 us -> 194 us (0.85)
  Pallas kernels: 184 us -> 161 us
  waiting for transfers between devices: 21.1 us -> 10.6 us
    pallas_call x1, Pallas kernels: 90.3 us -> 66.8 us  [shards(): pl.pallas_call(chain_kernel, in_specs=whole(4), out_specs=whole(5), out_s...]
    ppermute x10, waiting for transfers between devices: 21.1 us -> 10.6 us  [send(): return lax.ppermute(value, ('row', 'col'), pairs)]
  transfers between devices with their start and end apart: 10 -> 10, of which waited for: 5 -> 7; matrix products, arithmetic and copies ran while one was open for 1% -> 1% of each run, Pallas kernels for 0% -> 0%
where the time goes in v2:
time: 194 us; the launch traced here: 193 us
  Pallas kernels  161 us (83%)
  starting transfers between devices  16.1 us (8%)
  waiting for transfers between devices  10.6 us (5%)
  local copies, waits for them, and re-layouts  2.86 us (1%)
  other arithmetic  2.59 us (1%)
    pallas_call x1, Pallas kernels, shards(): pl.pallas_call(chain_kernel, in_specs=whole(4), out_specs=whole(5), out_s...  66.8 us
    pallas_call x1, Pallas kernels, shards(): pl.pallas_call(final_kernel, grid_spec=pltpu.PrefetchScalarGridSpec(num_s...  56.6 us
    pallas_call x1, Pallas kernels, shards(): pl.pallas_call(weights_kernel, grid_spec=pltpu.PrefetchScalarGridSpec(num...  29.6 us
    ppermute x10, starting transfers between devices, send(): return lax.ppermute(value, ('row', 'col'), pairs)  16.1 us
    ppermute x10, waiting for transfers between devices, send(): return lax.ppermute(value, ('row', 'col'), pairs)  10.6 us
    pallas_call x1, Pallas kernels, shards(): pl.pallas_call(prep_kernel, grid_spec=pltpu.PrefetchScalarGridSpec(num_sc...  7.62 us
  transfers between devices with their start and end apart: 10, of which 7 were waited for; matrix products, arithmetic and copies ran while one was open for 1% of the time, Pallas kernels for 0%

profile of v2, /device:TPU:73, one launch (start us, length us, event | category | flops | bytes accessed | tf_op | source)
XLA Modules:
  0.0 192.9 jit_solution(13817624466478979570)
XLA Ops:
  0.0 0.0 copy-start.1
  0.0 0.7 reshape.151
  0.7 0.1 pad.7.clone
  0.8 0.8 maximum_bitcast_fusion
  1.6 0.0 collective-permute-start.2
  1.6 3.1 %collective-permute-start.1 = (f32[1,24,128]{2,1,0:T(8,128)S(1)}, f32[1,24,128]{2,1,0:T(8,128)S(1)}, u32[]{:S(2)}, u32[]{:S(2)}) collective-permute-start(f32[1,24,128]{2,1,0:T(8,128)S(1)} %maximum_bitcast_fusion), channel_id=1, source_target_pairs={{0,2},{1,3},{2,0},{3,1},{4,6},{5,7},{6,4},{7,5},{8,10},{9,11},{10,... | collective-permute-start | bytes 36872 | tf_op jit(solution)/shard_map/ppermute | solution.py:44
  4.7 0.0 collective-permute-start
  4.7 0.8 constant_dynamic-update-slice_fusion.16
  5.5 0.0 collective-permute-done.2
  5.5 0.3 collective-permute-done.1
  5.8 1.5 collective-permute-done
  7.3 2.5 %collective-permute-start.5 = (f32[4,24,128]{2,1,0:T(8,128)S(1)}, f32[4,24,128]{2,1,0:T(8,128)S(1)}, u32[]{:S(2)}, u32[]{:S(2)}) collective-permute-start(f32[4,24,128]{2,1,0:T(8,128)S(1)} %pad_maximum_fusion), channel_id=1, source_target_pairs={{0,12},{1,13},{2,14},{3,15},{4,0},{5,1},{6,2},{7,3},{8,4},{9,5},{1... | collective-permute-start | bytes 147464 | tf_op jit(solution)/shard_map/ppermute | solution.py:44
  9.7 0.5 collective-permute-start.4
  10.3 0.6 collective-permute-start.3
  10.9 3.8 %collective-permute-done.3 = f32[4,24,128]{2,1,0:T(8,128)S(1)} collective-permute-done((f32[4,24,128]{2,1,0:T(8,128)S(1)}, f32[4,24,128]{2,1,0:T(8,128)S(1)}, u32[]{:S(2)}, u32[]{:S(2)}) %collective-permute-start.3) | collective-permute-done | bytes 49184 | tf_op jit(solution)/shard_map/ppermute | solution.py:44
  14.7 0.0 collective-permute-done.4
  14.8 0.0 collective-permute-done.5
  14.8 1.4 collective-permute-start.6
  16.2 0.1 select_select_fusion
  16.2 0.8 collective-permute-start.7
  17.0 2.0 %collective-permute-start.8 = (f32[16,24,128]{2,1,0:T(8,128)S(1)}, f32[16,24,128]{2,1,0:T(8,128)S(1)}, u32[]{:S(2)}, u32[]{:S(2)}) collective-permute-start(f32[16,24,128]{2,1,0:T(8,128)S(1)} %get-tuple-element.37), channel_id=1, source_target_pairs={{0,96},{1,97},{2,98},{3,99},{4,100},{5,101},{6,102},{7,103},{8,104... | collective-permute-start | bytes 589832 | tf_op jit(solution)/shard_map/ppermute | solution.py:44
  19.0 0.3 collective-permute-done.6
  19.4 3.0 %collective-permute-done.7 = f32[16,24,128]{2,1,0:T(8,128)S(1)} collective-permute-done((f32[16,24,128]{2,1,0:T(8,128)S(1)}, f32[16,24,128]{2,1,0:T(8,128)S(1)}, u32[]{:S(2)}, u32[]{:S(2)}) %collective-permute-start.7) | collective-permute-done | bytes 196640 | tf_op jit(solution)/shard_map/ppermute | solution.py:44
  22.4 1.6 collective-permute-done.8
  24.0 5.2 %collective-permute-start.9 = (f32[64,24,128]{2,1,0:T(8,128)S(1)}, f32[64,24,128]{2,1,0:T(8,128)S(1)}, u32[]{:S(2)}, u32[]{:S(2)}) collective-permute-start(f32[64,24,128]{2,1,0:T(8,128)S(1)} %get-tuple-element.29), channel_id=1, source_target_pairs={{0,16},{1,17},{2,18},{3,19},{4,20},{5,21},{6,22},{7,23},{8,24},{9,... | collective-permute-start | bytes 2359304 | tf_op jit(solution)/shard_map/ppermute | solution.py:44
  29.2 0.1 select_n.123
  29.3 0.1 pad_add_fusion.1
  29.3 0.0 copy-done.1
  29.3 0.2 select_reduce_fusion
  29.5 0.1 broadcast_add_fusion
  29.6 0.7 add.142.where_ref
  30.3 0.6 pad_add_fusion.info
  30.9 0.2 collective-permute-done.9
  31.1 0.1 constant_dynamic-update-slice_fusion.17.g0.g1.g2.g3
  31.1 0.0 copy-start
  31.1 1.1 copy-done
  32.3 7.6 %prep.1 = (bf16[8,4,512,48]{3,2,1,0:T(8,128)(2,1)}, bf16[8,4,48,512]{3,2,1,0:T(8,128)(2,1)}, f32[8,512,128]{2,1,0:T(8,128)}, f32[8,8,512]{2,1,0:T(8,128)}) custom-call(s32[32]{0:T(128)} %add.142.where_ref, f32[128,24,128]{2,1,0:T(8,128)} %copy-done, f32[128,24,128]{2,1,0:T(8,128)} %copy-done, f32[128,24,128]{2,1,0:T(8,128)} %copy-done, f32[128,24,128]{2,1,0:T(8,128)} %copy-done), custom_call_target="tpu_custom_call" | custom-call | tf_op jit(solution)/shard_map/prep/pallas_call | solution.py:378
  39.9 66.8 %chain.1 = (f32[1024,1024]{1,0:T(8,128)}, bf16[1024,1024]{1,0:T(8,128)(2,1)}, bf16[1024,1024]{1,0:T(8,128)(2,1)}, bf16[1024,1024]{1,0:T(8,128)(2,1)}, bf16[1024,1024]{1,0:T(8,128)(2,1)}) custom-call(bf16[8,4,512,48]{3,2,1,0:T(8,128)(2,1)} %get-tuple-element.16.u_ref, bf16[8,4,48,512]{3,2,1,0:T(8,128)(2,1)} %get-tuple-element.17.v_ref, ...), custom_call_target="tpu_custom_call" | custom-call | tf_op jit(solution)/shard_map/chain/pallas_call | solution.py:402
  106.7 29.6 %weights.1 = (bf16[2,1024,512]{2,1,0:T(8,128)(2,1)}, bf16[2,1024,512]{2,1,0:T(8,128)(2,1)}) custom-call(s32[11]{0:T(128)} %pad_add_fusion.info, bf16[8,4,512,48]{3,2,1,0:T(8,128)(2,1)} %get-tuple-element.16.u_ref, bf16[8,4,48,512]{3,2,1,0:T(8,128)(2,1)} %get-tuple-element.17.v_ref, f32[8,512,128]{2,1,0:T(8,128)} %get-tuple-element.18.wr_ref, ...), custom_call_target="tpu_custom_call" | custom-call | tf_op jit(solution)/shard_map/weights/pallas_call | solution.py:432
  136.3 56.6 %final.1 = f32[16384,128]{1,0:T(8,128)} custom-call(s32[11]{0:T(128)} %pad_add_fusion.info, bf16[8,4,512,48]{3,2,1,0:T(8,128)(2,1)} %get-tuple-element.16.u_ref, bf16[8,4,48,512]{3,2,1,0:T(8,128)(2,1)} %get-tuple-element.17.v_ref, f32[8,512,128]{2,1,0:T(8,128)} %get-tuple-element.18.wr_ref, f32[8,8,512]{2,1,0:T(8,128)} %get-tuple-element.19.wc_ref, ...), custom_call_target="tpu_custom_call" | custom-call | tf_op jit(solution)/shard_map/final/pallas_call | solution.py:446
  (16 shorter events, 0.2 us)
Async XLA Ops:
  0.0 29.3 %copy-start.1 = (s32[32]{0:T(128)S(1)}, s32[32]{0:T(128)}, u32[]{:S(2)}) copy-start(s32[32]{0:T(128)} %param.7) | copy-start | bytes 388
  1.6 3.9 %collective-permute-start.2 = (f32[1,24,128]{2,1,0:T(8,128)S(1)}, f32[1,24,128]{2,1,0:T(8,128)S(1)}, u32[]{:S(2)}, u32[]{:S(2)}) collective-permute-start(f32[1,24,128]{2,1,0:T(8,128)S(1)} %maximum_bitcast_fusion), channel_id=1, source_target_pairs={{0,3},{1,0},{2,1},{3,2},{4,7},{5,4},{6,5},{7,6},{8,11},{9,8},{10,9... | collective-permute-start | bytes 36872 | tf_op jit(solution)/shard_map/ppermute | solution.py:44
  1.6 4.2 %collective-permute-start.1 = (f32[1,24,128]{2,1,0:T(8,128)S(1)}, f32[1,24,128]{2,1,0:T(8,128)S(1)}, u32[]{:S(2)}, u32[]{:S(2)}) collective-permute-start(f32[1,24,128]{2,1,0:T(8,128)S(1)} %maximum_bitcast_fusion), channel_id=1, source_target_pairs={{0,2},{1,3},{2,0},{3,1},{4,6},{5,7},{6,4},{7,5},{8,10},{9,11},{10,... | collective-permute-start | bytes 36872 | tf_op jit(solution)/shard_map/ppermute | solution.py:44
  4.7 2.5 %collective-permute-start = (f32[1,24,128]{2,1,0:T(8,128)S(1)}, f32[1,24,128]{2,1,0:T(8,128)S(1)}, u32[]{:S(2)}, u32[]{:S(2)}) collective-permute-start(f32[1,24,128]{2,1,0:T(8,128)S(1)} %maximum_bitcast_fusion), channel_id=1, source_target_pairs={{0,1},{1,2},{2,3},{3,0},{4,5},{5,6},{6,7},{7,4},{8,9},{9,10},{10,1... | collective-permute-start | bytes 36872 | tf_op jit(solution)/shard_map/ppermute | solution.py:44
  7.3 7.5 %collective-permute-start.5 = (f32[4,24,128]{2,1,0:T(8,128)S(1)}, f32[4,24,128]{2,1,0:T(8,128)S(1)}, u32[]{:S(2)}, u32[]{:S(2)}) collective-permute-start(f32[4,24,128]{2,1,0:T(8,128)S(1)} %pad_maximum_fusion), channel_id=1, source_target_pairs={{0,12},{1,13},{2,14},{3,15},{4,0},{5,1},{6,2},{7,3},{8,4},{9,5},{1... | collective-permute-start | bytes 147464 | tf_op jit(solution)/shard_map/ppermute | solution.py:44
  9.7 5.0 %collective-permute-start.4 = (f32[4,24,128]{2,1,0:T(8,128)S(1)}, f32[4,24,128]{2,1,0:T(8,128)S(1)}, u32[]{:S(2)}, u32[]{:S(2)}) collective-permute-start(f32[4,24,128]{2,1,0:T(8,128)S(1)} %pad_maximum_fusion), channel_id=1, source_target_pairs={{0,8},{1,9},{2,10},{3,11},{4,12},{5,13},{6,14},{7,15},{8,0},{9,1},... | collective-permute-start | bytes 147464 | tf_op jit(solution)/shard_map/ppermute | solution.py:44
  10.3 4.5 %collective-permute-start.3 = (f32[4,24,128]{2,1,0:T(8,128)S(1)}, f32[4,24,128]{2,1,0:T(8,128)S(1)}, u32[]{:S(2)}, u32[]{:S(2)}) collective-permute-start(f32[4,24,128]{2,1,0:T(8,128)S(1)} %pad_maximum_fusion), channel_id=1, source_target_pairs={{0,4},{1,5},{2,6},{3,7},{4,8},{5,9},{6,10},{7,11},{8,12},{9,13},{1... | collective-permute-start | bytes 147464 | tf_op jit(solution)/shard_map/ppermute | solution.py:44
  14.8 4.6 %collective-permute-start.6 = (f32[16,24,128]{2,1,0:T(8,128)S(1)}, f32[16,24,128]{2,1,0:T(8,128)S(1)}, u32[]{:S(2)}, u32[]{:S(2)}) collective-permute-start(f32[16,24,128]{2,1,0:T(8,128)S(1)} %get-tuple-element.37), channel_id=1, source_target_pairs={{0,32},{1,33},{2,34},{3,35},{4,36},{5,37},{6,38},{7,39},{8,40},{9,... | collective-permute-start | bytes 589832 | tf_op jit(solution)/shard_map/ppermute | solution.py:44
  16.2 6.1 %collective-permute-start.7 = (f32[16,24,128]{2,1,0:T(8,128)S(1)}, f32[16,24,128]{2,1,0:T(8,128)S(1)}, u32[]{:S(2)}, u32[]{:S(2)}) collective-permute-start(f32[16,24,128]{2,1,0:T(8,128)S(1)} %get-tuple-element.37), channel_id=1, source_target_pairs={{0,64},{1,65},{2,66},{3,67},{4,68},{5,69},{6,70},{7,71},{8,72},{9,... | collective-permute-start | bytes 589832 | tf_op jit(solution)/shard_map/ppermute | solution.py:44
  17.0 6.9 %collective-permute-start.8 = (f32[16,24,128]{2,1,0:T(8,128)S(1)}, f32[16,24,128]{2,1,0:T(8,128)S(1)}, u32[]{:S(2)}, u32[]{:S(2)}) collective-permute-start(f32[16,24,128]{2,1,0:T(8,128)S(1)} %get-tuple-element.37), channel_id=1, source_target_pairs={{0,96},{1,97},{2,98},{3,99},{4,100},{5,101},{6,102},{7,103},{8,104... | collective-permute-start | bytes 589832 | tf_op jit(solution)/shard_map/ppermute | solution.py:44
  24.0 7.1 %collective-permute-start.9 = (f32[64,24,128]{2,1,0:T(8,128)S(1)}, f32[64,24,128]{2,1,0:T(8,128)S(1)}, u32[]{:S(2)}, u32[]{:S(2)}) collective-permute-start(f32[64,24,128]{2,1,0:T(8,128)S(1)} %get-tuple-element.29), channel_id=1, source_target_pairs={{0,16},{1,17},{2,18},{3,19},{4,20},{5,21},{6,22},{7,23},{8,24},{9,... | collective-permute-start | bytes 2359304 | tf_op jit(solution)/shard_map/ppermute | solution.py:44
  31.1 1.1 copy-start

commit v3 on v2

--- a/solution.py
+++ b/solution.py
@@ -30,27 +30,27 @@
     return dot(a_high, b_high) + (dot(a_high, b_low) + dot(a_low, b_high))
 
 
+def send(value, move, rows, cols):
+    ys, xs = rows // 2, 4
+    zs = cols // xs
+    pairs = []
+    for source in range(rows * cols):
+        row, col = divmod(source, cols)
+        y, core, x, z = move(row // 2, row % 2, col // zs, col % zs)
+        pairs.append((source, ((y % ys) * 2 + core % 2) * cols + (x % xs) * zs + z % zs))
+    return lax.ppermute(value, ("row", "col"), pairs)
+
+
 def gather_shards(shard):
     rows, cols = lax.axis_size("row"), lax.axis_size("col")
-    ys, xs = rows // 2, 4
-    zs = cols // xs
-
-    def send(value, move):
-        pairs = []
-        for source in range(rows * cols):
-            row, col = divmod(source, cols)
-            y, core, x, z = move(row // 2, row % 2, col // zs, col % zs)
-            pairs.append((source, ((y % ys) * 2 + core % 2) * cols + (x % xs) * zs + z % zs))
-        return lax.ppermute(value, ("row", "col"), pairs)
-
     held = shard[None]
-    moves = [lambda y, c, x, z, k=k: (y, c, x, z + k) for k in range(1, zs)]
-    held = jnp.concatenate([held] + [send(held, move) for move in moves], 0)
-    moves = [lambda y, c, x, z, k=k: (y, c, x + k, z) for k in range(1, xs)]
-    held = jnp.concatenate([held] + [send(held, move) for move in moves], 0)
-    moves = [lambda y, c, x, z, k=k: (y + k, c, x, z) for k in range(1, ys)]
-    held = jnp.concatenate([held] + [send(held, move) for move in moves], 0)
-    return jnp.concatenate([held, send(held, lambda y, c, x, z: (y, c + 1, x, z))], 0)
+    for axis in (3, 2, 0):
+        moved = [held]
+        for k in range(1, 4):
+            move = lambda *at, k=k: [part + k * (i == axis) for i, part in enumerate(at)]
+            moved.append(send(held, move, rows, cols))
+        held = jnp.concatenate(moved, 0)
+    return jnp.concatenate([held, send(held, lambda y, c, x, z: (y, c + 1, x, z), rows, cols)], 0)
 
 
 def prep_kernel(where_ref, g0, g1, g2, g3, u_ref, v_ref, wr_ref, wc_ref, pad):
@@ -83,13 +83,22 @@
     right += fine_high + fine_low + fine_high
     right += [one] * 3 + pieces(mixed + SOFTENING_SQUARED)
     pad[...] = jnp.zeros_like(pad)
-    for quad in range(QUAD):
-        for k, value in enumerate(left):
-            pad[k : k + 1, :] = value[quad : quad + 1, :]
-        u_ref[quad] = jnp.transpose(pad[...])[:, :FEAT].astype(BF16)
-        for k, value in enumerate(right):
-            pad[k : k + 1, :] = value[quad : quad + 1, :]
-        v_ref[quad] = pad[0:FEAT, :].astype(BF16)
+    tile = pl.program_id(0)
+
+    @pl.when(tile < 6)
+    def _():
+        for quad in range(QUAD):
+            for k, value in enumerate(left):
+                pad[k : k + 1, :] = value[quad : quad + 1, :]
+            u_ref[quad] = jnp.transpose(pad[...])[:, :FEAT].astype(BF16)
+
+    @pl.when((tile < 2) | (tile >= 6))
+    def _():
+        for quad in range(QUAD):
+            for k, value in enumerate(right):
+                pad[k : k + 1, :] = value[quad : quad + 1, :]
+            v_ref[quad] = pad[0:FEAT, :].astype(BF16)
+
     pad[0:8, :] = geometry[12:20]
     wr_ref[...] = jnp.transpose(pad[...])
     wc_ref[...] = geometry[12:20]
@@ -107,12 +116,6 @@
         part = part * wr_ref[left, rows, first : first + 1]
         total = part if total is None else total + part
     return total
-
-
-def with_shift(values, wr_ref, tile, start, count):
-    row = start + lax.broadcasted_iota(jnp.int32, (count, TILE), 0)
-    col = lax.broadcasted_iota(jnp.int32, (count, TILE), 1)
-    return values + jnp.where(row == col, wr_ref[tile, pl.ds(start, count), 4:5], 0.0)
 
 
 def split3(value):
@@ -185,25 +188,45 @@
 
 
 def chain_kernel(
-    u_ref, v_ref, wr_ref, wc_ref,
-    ft_ref, hh_ref, hl_ref, th_ref, tl_ref,
-    state, work, spread, solved, lines, stack, tall,
+    info, u_ref, v_ref, wr_ref, wc_ref,
+    ft_ref, y_ref,
+    state, side, work, spread, solved, lines, stack, tall,
 ):
     state[:, LEAD:] = jnp.zeros((LEAD + BASE, LEAD), F32)
     state[LEAD:, :LEAD] = jnp.zeros((BASE, LEAD), F32)
+    side[LEAD:, :] = jnp.zeros((BASE, BASE), F32)
     lane = lax.broadcasted_iota(jnp.int32, (BASE, BASE), 1)
     row = lax.broadcasted_iota(jnp.int32, (BASE, BASE), 0)
     eye = (row == lane).astype(F32)
-    for left, right in ((0, 0), (0, 1), (1, 1)):
-        @pl.loop(0, TILE // 256)
-        def _(chunk):
-            start = pl.multiple_of(chunk * 256, 256)
-            values = assemble(u_ref, v_ref, wr_ref, wc_ref, left, right, start, 256)
-            if left == right:
-                values = with_shift(values, wr_ref, left, start, 256)
-            state[pl.ds(left * TILE + start, 256), right * TILE : (right + 1) * TILE] = values
+    geometry = (u_ref, v_ref, wr_ref, wc_ref)
+    slot, column = info[0], info[1]
+    offset = pl.multiple_of(info[2], BASE)
+
+    @pl.loop(0, TILE // 256)
+    def _(chunk):
+        start = pl.multiple_of(chunk * 256, 256)
+        rows = pl.ds(start, 256)
+        for tile in range(2):
+            here = pl.ds(pl.multiple_of(tile * TILE + start, 256), 256)
+            low = tile * TILE
+            values = assemble(*geometry, tile, tile, start, 256, slice(256, TILE))
+            line = start + lax.broadcasted_iota(jnp.int32, (256, 256), 0)
+            across = 256 + lax.broadcasted_iota(jnp.int32, (256, 256), 1)
+            values = values + jnp.where(line == across, wr_ref[tile, rows, 4:5], 0.0)
+            state[here, low + 256 : low + TILE] = values
+            side[here, :] = assemble(*geometry, tile, 6 + slot, start, 256, pl.ds(offset, BASE))
+        state[rows, TILE : 2 * TILE] = assemble(*geometry, 0, 1, start, 256)
+
+    for tile in range(2):
+        values = assemble(*geometry, tile, tile, 0, 256, slice(0, 256))
+        line = lax.broadcasted_iota(jnp.int32, (256, 256), 0)
+        across = lax.broadcasted_iota(jnp.int32, (256, 256), 1)
+        values = values + jnp.where(line == across, wr_ref[tile, 0:256, 4:5], 0.0)
+        state[tile * TILE : tile * TILE + 256, tile * TILE : tile * TILE + 256] = values
 
     blocks = LEAD // BASE
+    both = jnp.concatenate
+    dot = functools.partial(jnp.dot, preferred_element_type=F32)
 
     @pl.loop(0, blocks)
     def _(k):
@@ -211,7 +234,6 @@
         rows = pl.ds(here, BASE)
         state[rows, pl.ds(pl.multiple_of(LEAD + here, BASE), BASE)] = eye
         work[...] = state[rows, pl.ds(here, BASE)]
-
         eliminate_base(work, spread, solved, lines)
         l0, l1, l2 = split3(jnp.where(row >= lane, work[...], 0.0))
         window = pl.ds(here, WINDOW)
@@ -223,14 +245,11 @@
             stack[256:384, :] = third
             stack[384:512, :] = first
 
-        load(state[rows, window])
-        both = jnp.concatenate
-        two = jnp.dot(
-            both([both([l0, l0], 1), both([l1, l1], 1)], 0), stack[0:256, :], preferred_element_type=F32
-        )
-        one = jnp.dot(both([l0, l2], 1), stack[256:512, :], preferred_element_type=F32)
-        done = two[:BASE] + (two[BASE:] + one)
-        state[rows, window] = done
+        load(both([state[rows, window], side[rows, :]], 1))
+        two = dot(both([both([l0, l0], 1), both([l1, l1], 1)], 0), stack[0:256, :])
+        done = two[:BASE] + (two[BASE:] + dot(both([l0, l2], 1), stack[256:512, :]))
+        state[rows, window] = done[:, :WINDOW]
+        side[rows, :] = done[:, WINDOW:]
         load(done)
 
         @pl.loop(0, blocks - 1 - k)
@@ -249,72 +268,67 @@
         def _(pair):
             part = pl.ds(pl.multiple_of(pair * 256, 256), 256)
             below = pl.ds(pl.multiple_of(here + BASE + pair * 256, BASE), 256)
-            dot = functools.partial(jnp.dot, preferred_element_type=F32)
             update = dot(tall[part, 0:256], stack[0:256, :])
             update += dot(tall[part, 256:512], stack[0:256, :])
             update += dot(tall[part, 512:768], stack[256:512, :])
-            state[below, window] = state[below, window] - update
+            state[below, window] = state[below, window] - update[:, :WINDOW]
+            side[below, :] = side[below, :] - update[:, WINDOW:]
 
     ft_ref[...] = state[:LEAD, :LEAD]
 
-    @pl.loop(0, blocks)
-    def _(k):
-        rows = pl.ds(pl.multiple_of(k * BASE, BASE), BASE)
-        slab = state[rows, LEAD:]
-        hh_ref[rows, :], hl_ref[rows, :] = split(slab)
-        th_ref[:, rows], tl_ref[:, rows] = split(jnp.transpose(slab))
-
-
-def weights_kernel(info, u_ref, v_ref, wr_ref, wc_ref, hh, hl, th, tl, yh_ref, yl_ref, ah, al, zh, zl):
-    slot = pl.program_id(0)
-    column = info[slot]
-    panel = column < 2
-    top, low = pl.ds(0, TILE), pl.ds(TILE, TILE)
-
-    @pl.when(jnp.logical_not(panel))
+    @pl.when(column < 2)
     def _():
-        for half in range(2):
-            @pl.loop(0, TILE // 256)
-            def _(chunk):
-                start = pl.multiple_of(chunk * 256, 256)
-                values = assemble(u_ref, v_ref, wr_ref, wc_ref, half, 6 + slot, start, 256)
-                rows = pl.ds(half * TILE + start, 256)
-                ah[rows, :], al[rows, :] = split(values)
-        zh[top, :], zl[top, :] = split(dot3(hh[top, top], hl[top, top], ah[top, :], al[top, :]))
-        zh[low, :], zl[low, :] = split(dot3(hh[low, :], hl[low, :], ah[...], al[...]))
-
-    @pl.when(panel)
-    def _():
-        row = lax.broadcasted_iota(jnp.int32, (LEAD, TILE), 0)
-        col = lax.broadcasted_iota(jnp.int32, (LEAD, TILE), 1)
-        zh[...] = jnp.where(row == col + column * TILE, -1.0, 0.0).astype(BF16)
-        zl[...] = jnp.zeros((LEAD, TILE), BF16)
-
-    yh_ref[top, :], yl_ref[top, :] = split(dot3(th[top, :], tl[top, :], zh[...], zl[...]))
-    yh_ref[low, :], yl_ref[low, :] = split(dot3(th[low, low], tl[low, low], zh[low, :], zl[low, :]))
-
-
-CHUNK = 256
-ZERO, UPDATE, DIAGONAL, PANEL, FACTOR = range(5)
-
-
-def final_kernel(info, u_ref, v_ref, wr_ref, wc_ref, yh, yl, ft_ref, out_ref, ah, al):
-    slot, chunk = pl.program_id(0), pl.program_id(1)
+        line = lax.broadcasted_iota(jnp.int32, (LEAD, BASE), 0)
+        across = lax.broadcasted_iota(jnp.int32, (LEAD, BASE), 1)
+        side[:LEAD, :] = jnp.where(line == across + (column * TILE + offset), -1.0, 0.0)
+
+    for out in range(4):
+        total = jnp.zeros((256, BASE), F32)
+        for part in range(out, 4):
+            rows = slice(part * 256, part * 256 + 256)
+            factor = jnp.transpose(state[rows, LEAD + out * 256 : LEAD + out * 256 + 256])
+            high, low = split(factor)
+            z_high, z_low = split(side[rows, :])
+            wide = dot(high, both([z_high, z_low], 1))
+            total = total + (wide[:, :BASE] + (wide[:, BASE:] + dot(low, z_high)))
+        y_ref[out * 256 : out * 256 + 256, :] = total
+
+
+def panel_kernel(base, info, u_ref, v_ref, wr_ref, wc_ref, *refs):
+    ah_ref, al_ref = refs[-2:]
+    slot, chunk = base + pl.program_id(0), pl.program_id(1)
     start = pl.multiple_of(chunk * CHUNK, CHUNK)
-    kinds = [info[2 + slot * 2], info[3 + slot * 2]]
-
-    def store(j, values):
-        for q in range(TILE // 128):
-            out_ref[pl.ds(j * 4 + q, CHUNK, stride=8), :] = values[:, q * 128 : (q + 1) * 128]
-
+    kinds = [info[3 + slot * 2], info[4 + slot * 2]]
     needed = lambda kind: (kind != ZERO) & (kind != FACTOR)
 
     @pl.when(needed(kinds[0]) | needed(kinds[1]))
     def _():
         for half in range(2):
             values = assemble(u_ref, v_ref, wr_ref, wc_ref, 2 + slot, half, start, CHUNK)
-            cols = pl.ds(half * TILE, TILE)
-            ah[:, cols], al[:, cols] = split(values)
+            cols = slice(half * TILE, half * TILE + TILE)
+            ah_ref[:, cols], al_ref[:, cols] = split(values)
+
+
+CHUNK = 256
+ZERO, UPDATE, DIAGONAL, PANEL, FACTOR = range(5)
+
+
+def final_kernel(info, u_ref, v_ref, wr_ref, wc_ref, ft_ref, *rest):
+    parts, (ah, al, out_ref, yh, yl) = rest[:8], rest[8:]
+    slot, chunk = pl.program_id(0), pl.program_id(1)
+    start = pl.multiple_of(chunk * CHUNK, CHUNK)
+    kinds = [info[3 + slot * 2], info[4 + slot * 2]]
+
+    @pl.when((slot == 0) & (chunk == 0))
+    def _():
+        for p, part in enumerate(parts):
+            source = info[12 + p]
+            lanes = pl.ds(pl.multiple_of(source % 4 * 128, 128), 128)
+            yh[source // 4, :, lanes], yl[source // 4, :, lanes] = split(part[...])
+
+    def store(j, values):
+        for q in range(TILE // 128):
+            out_ref[pl.ds(j * 4 + q, CHUNK, stride=8), :] = values[:, q * 128 : (q + 1) * 128]
 
     for j in range(2):
         kind = kinds[j]
@@ -339,7 +353,7 @@
         if j == 0:
             @pl.when(kind == FACTOR)
             def _():
-                which = info[10]
+                which = info[11]
                 lanes = pl.ds(pl.multiple_of(which // 2 * TILE + start, CHUNK), CHUNK)
                 rows = pl.ds(pl.multiple_of(which % 2 * TILE, TILE), TILE)
                 values = jnp.transpose(ft_ref[rows, lanes])
@@ -398,24 +412,6 @@
         name="prep",
     )(where, *[gathered] * 4)
 
-    square = jax.ShapeDtypeStruct((LEAD, LEAD), BF16)
-    ft, hh, hl, th, tl = pl.pallas_call(
-        chain_kernel,
-        in_specs=whole(4),
-        out_specs=whole(5),
-        out_shape=[jax.ShapeDtypeStruct((LEAD, LEAD), F32)] + [square] * 4,
-        scratch_shapes=[
-            pltpu.VMEM((LEAD + BASE, 2 * LEAD), F32),
-            pltpu.VMEM((BASE, BASE), F32),
-            pltpu.VMEM((STEP, STEP, BASE), F32),
-            pltpu.VMEM((STEP, STEP, BASE), F32),
-            pltpu.VMEM((STEP, BASE), F32),
-            pltpu.VMEM((4 * BASE, WINDOW), BF16),
-            pltpu.VMEM((LEAD, 6 * BASE), BF16),
-        ],
-        name="chain",
-    )(u, v, wr, wc)
-
     block_rows, block_cols = tile_rows[:, None], tile_cols[None, :]
     kinds = jnp.where(
         block_rows < block_cols,
@@ -426,35 +422,72 @@
             jnp.where(block_rows < 2, FACTOR, PANEL),
         ),
     )
-    info = jnp.concatenate([tile_cols, kinds.reshape(-1), (row * 2 + col)[None]]).astype(jnp.int32)
-
-    half = jax.ShapeDtypeStruct((2, LEAD, TILE), BF16)
-    yh, yl = pl.pallas_call(
-        weights_kernel,
-        grid_spec=pltpu.PrefetchScalarGridSpec(
-            num_scalar_prefetch=1,
-            grid=(2,),
-            in_specs=whole(8),
-            out_specs=[pl.BlockSpec((None, LEAD, TILE), lambda j, info: (j, 0, 0))] * 2,
-            scratch_shapes=[pltpu.VMEM((LEAD, TILE), BF16)] * 4,
-        ),
-        out_shape=[half, half],
-        name="weights",
-    )(info, u, v, wr, wc, hh, hl, th, tl)
+    mine = row // 4
+    order = jnp.arange(8, dtype=jnp.int32)
+    sources = (row // 2 - order % 4) % 4 * 2 + (row % 2 - order // 4) % 2
+    head = jnp.stack([mine, col + cols * mine, row % 4 * BASE])
+    info = jnp.concatenate([head, kinds.reshape(-1), (row * 2 + col)[None], sources]).astype(jnp.int32)
+
+    smem = [pl.BlockSpec(memory_space=pltpu.SMEM)]
+    ft, weights_part = pl.pallas_call(
+        chain_kernel,
+        in_specs=smem + whole(4),
+        out_specs=whole(2),
+        out_shape=[jax.ShapeDtypeStruct((LEAD, LEAD), F32), jax.ShapeDtypeStruct((LEAD, BASE), F32)],
+        scratch_shapes=[
+            pltpu.VMEM((LEAD + BASE, 2 * LEAD), F32),
+            pltpu.VMEM((LEAD + BASE, BASE), F32),
+            pltpu.VMEM((BASE, BASE), F32),
+            pltpu.VMEM((STEP, STEP, BASE), F32),
+            pltpu.VMEM((STEP, STEP, BASE), F32),
+            pltpu.VMEM((STEP, BASE), F32),
+            pltpu.VMEM((4 * BASE, WINDOW + BASE), BF16),
+            pltpu.VMEM((LEAD, 6 * BASE), BF16),
+        ],
+        name="chain",
+    )(info, u, v, wr, wc)
+
+    tall = jax.ShapeDtypeStruct((4 * TILE, LEAD), BF16)
+    chunks = TILE // CHUNK
+
+    def panel(base, held):
+        blocked = pl.BlockSpec((CHUNK, LEAD), lambda i, h, info: ((base + i) * chunks + h, 0))
+        return pl.pallas_call(
+            functools.partial(panel_kernel, base),
+            grid_spec=pltpu.PrefetchScalarGridSpec(
+                num_scalar_prefetch=1,
+                grid=(2, chunks),
+                in_specs=whole(4) + [pl.BlockSpec(memory_space=pl.ANY)] * len(held),
+                out_specs=[blocked] * 2,
+            ),
+            out_shape=[tall] * 2,
+            input_output_aliases={5 + i: i for i in range(len(held))},
+            cost_estimate=pl.CostEstimate(
+                flops=30_000_000_000, bytes_accessed=8_000_000, transcendentals=17_000_000
+            ),
+            name=f"panel{base}",
+        )(info, u, v, wr, wc, *held)
+
+    near = [send(weights_part, lambda y, c, x, z, k=k: (y + k, c, x, z), rows, cols) for k in range(1, 4)]
+    *near, ah, al = lax.optimization_barrier((*near, *panel(0, [])))
+    parts = [weights_part] + near
+    parts = parts + [send(part, lambda y, c, x, z: (y, c + 1, x, z), rows, cols) for part in parts]
+    *parts, ah, al = lax.optimization_barrier((*parts, *panel(2, [ah, al])))
 
     lines = CHUNK * 8
     out = pl.pallas_call(
         final_kernel,
         grid_spec=pltpu.PrefetchScalarGridSpec(
             num_scalar_prefetch=1,
-            grid=(4, TILE // CHUNK),
-            in_specs=whole(7),
-            out_specs=pl.BlockSpec((lines, 128), lambda i, h, info: (i * (TILE // CHUNK) + h, 0)),
-            scratch_shapes=[pltpu.VMEM((CHUNK, LEAD), BF16)] * 2,
+            grid=(4, chunks),
+            in_specs=whole(13)
+            + [pl.BlockSpec((CHUNK, LEAD), lambda i, h, info: (i * chunks + h, 0))] * 2,
+            out_specs=pl.BlockSpec((lines, 128), lambda i, h, info: (i * chunks + h, 0)),
+            scratch_shapes=[pltpu.VMEM((2, LEAD, TILE), BF16)] * 2,
         ),
         out_shape=jax.ShapeDtypeStruct((4 * TILE * 8, 128), F32),
         name="final",
-    )(info, u, v, wr, wc, yh, yl, ft)
+    )(info, u, v, wr, wc, ft, *parts, ah, al)
     return out.reshape(4, 1, TILE, 2, 1, TILE)
 
 

time: 194 us -> 185 us (0.954)
  Pallas kernels: 161 us -> 138 us
  waiting for transfers between devices: 10.6 us -> 17.2 us
  starting transfers between devices: 16.1 us -> 22 us
    pallas_call x1, Pallas kernels: 56.6 us -> 35.7 us  [shards(): pl.pallas_call(final_kernel, grid_spec=pltpu.PrefetchScalarGridSpec(num_s...]
    ppermute x10 -> x17, waiting for transfers between devices: 10.6 us -> 17.2 us  [send(): return lax.ppermute(value, ('row', 'col'), pairs)]
    ppermute x10 -> x17, starting transfers between devices: 16.1 us -> 22 us  [send(): return lax.ppermute(value, ('row', 'col'), pairs)]
    pallas_call x2 -> x3, Pallas kernels: 96.4 us -> 95.2 us  [the longest x1 62.7 us: shards(): pl.pallas_call(chain_kernel, in_specs=smem + whole(4), out_specs=whole(2)...]
  transfers between devices with their start and end apart: 10 -> 17, of which waited for: 7 -> 9; matrix products, arithmetic and copies ran while one was open for 1% -> 1% of each run, Pallas kernels for 0% -> 18%
where the time goes in v3:
time: 185 us; the launch traced here: 184 us
  Pallas kernels  138 us (75%)
  starting transfers between devices  22 us (12%)
  waiting for transfers between devices  17.2 us (9%)
  local copies, waits for them, and re-layouts  4.63 us (3%)
  other arithmetic  2.02 us (1%)
    pallas_call x1, Pallas kernels, shards(): pl.pallas_call(chain_kernel, in_specs=smem + whole(4), out_specs=whole(2)...  62.7 us
    pallas_call x1, Pallas kernels, shards(): pl.pallas_call(final_kernel, grid_spec=pltpu.PrefetchScalarGridSpec(num_s...  35.7 us
    pallas_call x2, Pallas kernels, panel(): pl.pallas_call(functools.partial(panel_kernel, base), grid_spec=pltpu.Pre...  32.6 us
    ppermute x17, starting transfers between devices, send(): return lax.ppermute(value, ('row', 'col'), pairs)  22 us
    ppermute x17, waiting for transfers between devices, send(): return lax.ppermute(value, ('row', 'col'), pairs)  17.2 us
    pallas_call x1, Pallas kernels, shards(): pl.pallas_call(prep_kernel, grid_spec=pltpu.PrefetchScalarGridSpec(num_sc...  7.39 us
  transfers between devices with their start and end apart: 17, of which 9 were waited for; matrix products, arithmetic and copies ran while one was open for 1% of the time, Pallas kernels for 18%

profile of v3, /device:TPU:73, one launch (start us, length us, event | category | flops | bytes accessed | tf_op | source)
XLA Modules:
  0.0 184.3 jit_solution(5722110799611122043)
XLA Ops:
  0.0 0.0 copy-start.7
  0.0 0.7 reshape.151
  0.7 0.1 pad.7.clone
  0.8 0.8 maximum_bitcast_fusion
  1.6 0.0 collective-permute-start.2
  1.6 3.1 %collective-permute-start.1 = (f32[1,24,128]{2,1,0:T(8,128)S(1)}, f32[1,24,128]{2,1,0:T(8,128)S(1)}, u32[]{:S(2)}, u32[]{:S(2)}) collective-permute-start(f32[1,24,128]{2,1,0:T(8,128)S(1)} %maximum_bitcast_fusion), channel_id=1, source_target_pairs={{0,2},{1,3},{2,0},{3,1},{4,6},{5,7},{6,4},{7,5},{8,10},{9,11},{10,... | collective-permute-start | bytes 36872 | tf_op jit(solution)/shard_map/ppermute | solution.py:41
  4.7 0.0 collective-permute-start
  4.7 0.8 constant_dynamic-update-slice_fusion.16
  5.5 0.0 collective-permute-done.2
  5.5 0.3 collective-permute-done.1
  5.8 1.5 collective-permute-done
  7.3 2.5 %collective-permute-start.5 = (f32[4,24,128]{2,1,0:T(8,128)S(1)}, f32[4,24,128]{2,1,0:T(8,128)S(1)}, u32[]{:S(2)}, u32[]{:S(2)}) collective-permute-start(f32[4,24,128]{2,1,0:T(8,128)S(1)} %pad_maximum_fusion), channel_id=1, source_target_pairs={{0,12},{1,13},{2,14},{3,15},{4,0},{5,1},{6,2},{7,3},{8,4},{9,5},{1... | collective-permute-start | bytes 147464 | tf_op jit(solution)/shard_map/ppermute | solution.py:41
  9.7 0.5 collective-permute-start.4
  10.3 0.6 collective-permute-start.3
  10.9 3.8 %collective-permute-done.3 = f32[4,24,128]{2,1,0:T(8,128)S(1)} collective-permute-done((f32[4,24,128]{2,1,0:T(8,128)S(1)}, f32[4,24,128]{2,1,0:T(8,128)S(1)}, u32[]{:S(2)}, u32[]{:S(2)}) %collective-permute-start.3) | collective-permute-done | bytes 49184 | tf_op jit(solution)/shard_map/ppermute | solution.py:41
  14.7 0.0 collective-permute-done.4
  14.8 0.0 collective-permute-done.5
  14.8 1.4 collective-permute-start.6
  16.2 0.1 select_select_fusion
  16.2 0.1 select_n.150
  16.3 0.8 collective-permute-start.7
  17.1 2.1 %collective-permute-start.8 = (f32[16,24,128]{2,1,0:T(8,128)S(1)}, f32[16,24,128]{2,1,0:T(8,128)S(1)}, u32[]{:S(2)}, u32[]{:S(2)}) collective-permute-start(f32[16,24,128]{2,1,0:T(8,128)S(1)} %get-tuple-element.65), channel_id=1, source_target_pairs={{0,96},{1,97},{2,98},{3,99},{4,100},{5,101},{6,102},{7,103},{8,104... | collective-permute-start | bytes 589832 | tf_op jit(solution)/shard_map/ppermute | solution.py:41
  19.1 0.2 collective-permute-done.6
  19.4 3.1 %collective-permute-done.7 = f32[16,24,128]{2,1,0:T(8,128)S(1)} collective-permute-done((f32[16,24,128]{2,1,0:T(8,128)S(1)}, f32[16,24,128]{2,1,0:T(8,128)S(1)}, u32[]{:S(2)}, u32[]{:S(2)}) %collective-permute-start.7) | collective-permute-done | bytes 196640 | tf_op jit(solution)/shard_map/ppermute | solution.py:41
  22.5 1.5 collective-permute-done.8
  24.0 5.4 %collective-permute-start.9 = (f32[64,24,128]{2,1,0:T(8,128)S(1)}, f32[64,24,128]{2,1,0:T(8,128)S(1)}, u32[]{:S(2)}, u32[]{:S(2)}) collective-permute-start(f32[64,24,128]{2,1,0:T(8,128)S(1)} %get-tuple-element.57), channel_id=1, source_target_pairs={{0,16},{1,17},{2,18},{3,19},{4,20},{5,21},{6,22},{7,23},{8,24},{9,... | collective-permute-start | bytes 2359304 | tf_op jit(solution)/shard_map/ppermute | solution.py:41
  29.5 0.1 pad_add_fusion
  29.5 0.0 copy-done.7
  29.5 0.2 select_reduce_fusion
  29.8 0.1 broadcast_add_fusion
  29.8 0.6 add.172.where_ref
  30.5 0.7 concatenate.24.info
  31.1 0.2 collective-permute-done.9
  31.4 0.1 constant_dynamic-update-slice_fusion.17.g0.g1.g2.g3
  31.4 0.0 copy-start
  31.4 1.1 copy-done
  32.6 7.4 %prep.1 = (bf16[8,4,512,48]{3,2,1,0:T(8,128)(2,1)}, bf16[8,4,48,512]{3,2,1,0:T(8,128)(2,1)}, f32[8,512,128]{2,1,0:T(8,128)}, f32[8,8,512]{2,1,0:T(8,128)}) custom-call(s32[32]{0:T(128)} %add.172.where_ref, f32[128,24,128]{2,1,0:T(8,128)} %copy-done, f32[128,24,128]{2,1,0:T(8,128)} %copy-done, f32[128,24,128]{2,1,0:T(8,128)} %copy-done, f32[128,24,128]{2,1,0:T(8,128)} %copy-done), custom_call_target="tpu_custom_call" | custom-call | tf_op jit(solution)/shard_map/prep/pallas_call | solution.py:392
  40.0 62.7 %chain.1 = (f32[1024,1024]{1,0:T(8,128)}, f32[1024,128]{1,0:T(8,128)}) custom-call(s32[20]{0:T(128)} %concatenate.24.info, bf16[8,4,512,48]{3,2,1,0:T(8,128)(2,1)} %get-tuple-element.30.u_ref, bf16[8,4,48,512]{3,2,1,0:T(8,128)(2,1)} %get-tuple-element.31.v_ref, f32[8,512,128]{2,1,0:T(8,128)} %get-tuple-element.32.wr_ref, f32[8,8,512]{2,1,0:T(8,128)} %get-tuple-element.33.wc_ref), custom_call_target="tpu_custom_call" | custom-call | tf_op jit(solution)/shard_map/chain/pallas_call | solution.py:432
  102.6 0.3 collective-permute-start.13
  103.0 0.0 collective-permute-start.12
  103.0 2.0 %collective-permute-start.11 = (f32[1024,128]{1,0:T(8,128)}, f32[1024,128]{1,0:T(8,128)S(1)}, u32[]{:S(2)}, u32[]{:S(2)}) collective-permute-start(f32[1024,128]{1,0:T(8,128)} %get-tuple-element.45.rest_0_), channel_id=1, source_target_pairs={{0,64},{1,65},{2,66},{3,67},{4,68},{5,69},{6,70},{7,71},{8,72},{9,... | collective-permute-start | bytes 1572872 | tf_op jit(solution)/shard_map/ppermute | solution.py:41
  105.0 1.5 collective-permute-start.10
  106.5 16.3 %panel0.1 = (bf16[2048,1024]{1,0:T(8,128)(2,1)}, bf16[2048,1024]{1,0:T(8,128)(2,1)}) custom-call(s32[20]{0:T(128)} %concatenate.24.info, bf16[8,4,512,48]{3,2,1,0:T(8,128)(2,1)} %get-tuple-element.30.u_ref, bf16[8,4,48,512]{3,2,1,0:T(8,128)(2,1)} %get-tuple-element.31.v_ref, f32[8,512,128]{2,1,0:T(8,128)} %get-tuple-element.32.wr_ref, ...), custom_call_target="tpu_custom_call" | custom-call | flops 30000001024 | bytes 8000000 | tf_op jit(solution)/shard_map/panel0/pallas_call | solution.py:455
  122.7 0.0 collective-permute-done.12.rest_3_
  122.7 5.5 %collective-permute-done.11.rest_2_ = f32[1024,128]{1,0:T(8,128)S(1)} collective-permute-done((f32[1024,128]{1,0:T(8,128)}, f32[1024,128]{1,0:T(8,128)S(1)}, u32[]{:S(2)}, u32[]{:S(2)}) %collective-permute-start.11) | collective-permute-done | bytes 524320 | tf_op jit(solution)/shard_map/ppermute | solution.py:41
  128.3 1.0 collective-permute-done.10.rest_1_
  129.3 1.3 collective-permute-start.14
  130.6 0.0 collective-permute-start.15
  130.6 0.5 collective-permute-start.16
  131.1 16.3 %panel2.1 = (bf16[2048,1024]{1,0:T(8,128)(2,1)}, bf16[2048,1024]{1,0:T(8,128)(2,1)}) custom-call(s32[20]{0:T(128)} %concatenate.24.info, bf16[8,4,512,48]{3,2,1,0:T(8,128)(2,1)} %get-tuple-element.30.u_ref, bf16[8,4,48,512]{3,2,1,0:T(8,128)(2,1)} %get-tuple-element.31.v_ref, ...), custom_call_target="tpu_custom_call", output_to_operand_aliasing={{0}: (5, {}), {1}: (6, {})} | custom-call | flops 30000001024 | bytes 8000000 | tf_op jit(solution)/shard_map/panel2/pallas_call | solution.py:455
  147.4 0.0 copy-done.2
  147.4 0.0 copy-done.3
  147.4 0.0 copy-done.4
  147.4 0.0 collective-permute-done.13.rest_4_
  147.5 0.0 copy-start.1
  147.5 0.0 collective-permute-done.14.rest_5_
  147.5 0.0 copy-start.5
  147.5 0.0 collective-permute-done.15.rest_6_
  147.5 0.0 copy-start.6
  147.5 0.0 collective-permute-done.16.rest_7_
  147.5 0.7 copy-done.1
  148.3 0.2 copy-done.5
  148.4 0.2 copy-done.6
  148.6 35.7 %final.1 = f32[16384,128]{1,0:T(8,128)} custom-call(s32[20]{0:T(128)} %concatenate.24.info, bf16[8,4,512,48]{3,2,1,0:T(8,128)(2,1)} %get-tuple-element.30.u_ref, bf16[8,4,48,512]{3,2,1,0:T(8,128)(2,1)} %get-tuple-element.31.v_ref, f32[8,512,128]{2,1,0:T(8,128)} %get-tuple-element.32.wr_ref, f32[8,8,512]{2,1,0:T(8,128)} %get-tuple-element.33.wc_ref, ...), custom_call_target="tpu_custom_call" | custom-call | tf_op jit(solution)/shard_map/final/pallas_call | solution.py:478
  (20 shorter events, 0.2 us)
Async XLA Ops:
  0.0 29.5 %copy-start.7 = (s32[32]{0:T(128)S(1)}, s32[32]{0:T(128)}, u32[]{:S(2)}) copy-start(s32[32]{0:T(128)} %param.7) | copy-start | bytes 388
  1.6 3.9 %collective-permute-start.2 = (f32[1,24,128]{2,1,0:T(8,128)S(1)}, f32[1,24,128]{2,1,0:T(8,128)S(1)}, u32[]{:S(2)}, u32[]{:S(2)}) collective-permute-start(f32[1,24,128]{2,1,0:T(8,128)S(1)} %maximum_bitcast_fusion), channel_id=1, source_target_pairs={{0,3},{1,0},{2,1},{3,2},{4,7},{5,4},{6,5},{7,6},{8,11},{9,8},{10,9... | collective-permute-start | bytes 36872 | tf_op jit(solution)/shard_map/ppermute | solution.py:41
  1.6 4.2 %collective-permute-start.1 = (f32[1,24,128]{2,1,0:T(8,128)S(1)}, f32[1,24,128]{2,1,0:T(8,128)S(1)}, u32[]{:S(2)}, u32[]{:S(2)}) collective-permute-start(f32[1,24,128]{2,1,0:T(8,128)S(1)} %maximum_bitcast_fusion), channel_id=1, source_target_pairs={{0,2},{1,3},{2,0},{3,1},{4,6},{5,7},{6,4},{7,5},{8,10},{9,11},{10,... | collective-permute-start | bytes 36872 | tf_op jit(solution)/shard_map/ppermute | solution.py:41
  4.7 2.5 %collective-permute-start = (f32[1,24,128]{2,1,0:T(8,128)S(1)}, f32[1,24,128]{2,1,0:T(8,128)S(1)}, u32[]{:S(2)}, u32[]{:S(2)}) collective-permute-start(f32[1,24,128]{2,1,0:T(8,128)S(1)} %maximum_bitcast_fusion), channel_id=1, source_target_pairs={{0,1},{1,2},{2,3},{3,0},{4,5},{5,6},{6,7},{7,4},{8,9},{9,10},{10,1... | collective-permute-start | bytes 36872 | tf_op jit(solution)/shard_map/ppermute | solution.py:41
  7.3 7.5 %collective-permute-start.5 = (f32[4,24,128]{2,1,0:T(8,128)S(1)}, f32[4,24,128]{2,1,0:T(8,128)S(1)}, u32[]{:S(2)}, u32[]{:S(2)}) collective-permute-start(f32[4,24,128]{2,1,0:T(8,128)S(1)} %pad_maximum_fusion), channel_id=1, source_target_pairs={{0,12},{1,13},{2,14},{3,15},{4,0},{5,1},{6,2},{7,3},{8,4},{9,5},{1... | collective-permute-start | bytes 147464 | tf_op jit(solution)/shard_map/ppermute | solution.py:41
  9.7 5.0 %collective-permute-start.4 = (f32[4,24,128]{2,1,0:T(8,128)S(1)}, f32[4,24,128]{2,1,0:T(8,128)S(1)}, u32[]{:S(2)}, u32[]{:S(2)}) collective-permute-start(f32[4,24,128]{2,1,0:T(8,128)S(1)} %pad_maximum_fusion), channel_id=1, source_target_pairs={{0,8},{1,9},{2,10},{3,11},{4,12},{5,13},{6,14},{7,15},{8,0},{9,1},... | collective-permute-start | bytes 147464 | tf_op jit(solution)/shard_map/ppermute | solution.py:41
  10.3 4.5 %collective-permute-start.3 = (f32[4,24,128]{2,1,0:T(8,128)S(1)}, f32[4,24,128]{2,1,0:T(8,128)S(1)}, u32[]{:S(2)}, u32[]{:S(2)}) collective-permute-start(f32[4,24,128]{2,1,0:T(8,128)S(1)} %pad_maximum_fusion), channel_id=1, source_target_pairs={{0,4},{1,5},{2,6},{3,7},{4,8},{5,9},{6,10},{7,11},{8,12},{9,13},{1... | collective-permute-start | bytes 147464 | tf_op jit(solution)/shard_map/ppermute | solution.py:41
  14.8 4.6 %collective-permute-start.6 = (f32[16,24,128]{2,1,0:T(8,128)S(1)}, f32[16,24,128]{2,1,0:T(8,128)S(1)}, u32[]{:S(2)}, u32[]{:S(2)}) collective-permute-start(f32[16,24,128]{2,1,0:T(8,128)S(1)} %get-tuple-element.65), channel_id=1, source_target_pairs={{0,32},{1,33},{2,34},{3,35},{4,36},{5,37},{6,38},{7,39},{8,40},{9,... | collective-permute-start | bytes 589832 | tf_op jit(solution)/shard_map/ppermute | solution.py:41
  16.3 6.2 %collective-permute-start.7 = (f32[16,24,128]{2,1,0:T(8,128)S(1)}, f32[16,24,128]{2,1,0:T(8,128)S(1)}, u32[]{:S(2)}, u32[]{:S(2)}) collective-permute-start(f32[16,24,128]{2,1,0:T(8,128)S(1)} %get-tuple-element.65), channel_id=1, source_target_pairs={{0,64},{1,65},{2,66},{3,67},{4,68},{5,69},{6,70},{7,71},{8,72},{9,... | collective-permute-start | bytes 589832 | tf_op jit(solution)/shard_map/ppermute | solution.py:41
  17.1 6.9 %collective-permute-start.8 = (f32[16,24,128]{2,1,0:T(8,128)S(1)}, f32[16,24,128]{2,1,0:T(8,128)S(1)}, u32[]{:S(2)}, u32[]{:S(2)}) collective-permute-start(f32[16,24,128]{2,1,0:T(8,128)S(1)} %get-tuple-element.65), channel_id=1, source_target_pairs={{0,96},{1,97},{2,98},{3,99},{4,100},{5,101},{6,102},{7,103},{8,104... | collective-permute-start | bytes 589832 | tf_op jit(solution)/shard_map/ppermute | solution.py:41
  24.0 7.3 %collective-permute-start.9 = (f32[64,24,128]{2,1,0:T(8,128)S(1)}, f32[64,24,128]{2,1,0:T(8,128)S(1)}, u32[]{:S(2)}, u32[]{:S(2)}) collective-permute-start(f32[64,24,128]{2,1,0:T(8,128)S(1)} %get-tuple-element.57), channel_id=1, source_target_pairs={{0,16},{1,17},{2,18},{3,19},{4,20},{5,21},{6,22},{7,23},{8,24},{9,... | collective-permute-start | bytes 2359304 | tf_op jit(solution)/shard_map/ppermute | solution.py:41
  31.4 1.1 copy-start
  102.6 44.8 %collective-permute-start.13 = (f32[1024,128]{1,0:T(8,128)}, f32[1024,128]{1,0:T(8,128)S(1)}, u32[]{:S(2)}, u32[]{:S(2)}) collective-permute-start(f32[1024,128]{1,0:T(8,128)} %get-tuple-element.45.rest_0_), channel_id=1, source_target_pairs={{0,16},{1,17},{2,18},{3,19},{4,20},{5,21},{6,22},{7,23},{8,24},{9,... | collective-permute-start | bytes 1572872 | tf_op jit(solution)/shard_map/ppermute | solution.py:41
  103.0 19.8 %collective-permute-start.12 = (f32[1024,128]{1,0:T(8,128)}, f32[1024,128]{1,0:T(8,128)S(1)}, u32[]{:S(2)}, u32[]{:S(2)}) collective-permute-start(f32[1024,128]{1,0:T(8,128)} %get-tuple-element.45.rest_0_), channel_id=1, source_target_pairs={{0,96},{1,97},{2,98},{3,99},{4,100},{5,101},{6,102},{7,103},{8,104... | collective-permute-start | bytes 1572872 | tf_op jit(solution)/shard_map/ppermute | solution.py:41
  103.0 25.3 %collective-permute-start.11 = (f32[1024,128]{1,0:T(8,128)}, f32[1024,128]{1,0:T(8,128)S(1)}, u32[]{:S(2)}, u32[]{:S(2)}) collective-permute-start(f32[1024,128]{1,0:T(8,128)} %get-tuple-element.45.rest_0_), channel_id=1, source_target_pairs={{0,64},{1,65},{2,66},{3,67},{4,68},{5,69},{6,70},{7,71},{8,72},{9,... | collective-permute-start | bytes 1572872 | tf_op jit(solution)/shard_map/ppermute | solution.py:41
  105.0 24.3 %collective-permute-start.10 = (f32[1024,128]{1,0:T(8,128)}, f32[1024,128]{1,0:T(8,128)S(1)}, u32[]{:S(2)}, u32[]{:S(2)}) collective-permute-start(f32[1024,128]{1,0:T(8,128)} %get-tuple-element.45.rest_0_), channel_id=1, source_target_pairs={{0,32},{1,33},{2,34},{3,35},{4,36},{5,37},{6,38},{7,39},{8,40},{9,... | collective-permute-start | bytes 1572872 | tf_op jit(solution)/shard_map/ppermute | solution.py:41
  122.7 24.7 %copy-start.2 = (f32[1024,128]{1,0:T(8,128)}, f32[1024,128]{1,0:T(8,128)S(1)}, u32[]{:S(2)}) copy-start(f32[1024,128]{1,0:T(8,128)S(1)} %collective-permute-done.12.rest_3_) | copy-start | bytes 1572868
  128.3 19.1 %copy-start.3 = (f32[1024,128]{1,0:T(8,128)}, f32[1024,128]{1,0:T(8,128)S(1)}, u32[]{:S(2)}) copy-start(f32[1024,128]{1,0:T(8,128)S(1)} %collective-permute-done.11.rest_2_) | copy-start | bytes 1572868
  129.3 18.2 %copy-start.4 = (f32[1024,128]{1,0:T(8,128)}, f32[1024,128]{1,0:T(8,128)S(1)}, u32[]{:S(2)}) copy-start(f32[1024,128]{1,0:T(8,128)S(1)} %collective-permute-done.10.rest_1_) | copy-start | bytes 1572868
  129.3 18.2 %collective-permute-start.14 = (f32[1024,128]{1,0:T(8,128)S(1)}, f32[1024,128]{1,0:T(8,128)S(1)}, u32[]{:S(2)}, u32[]{:S(2)}) collective-permute-start(f32[1024,128]{1,0:T(8,128)S(1)} %collective-permute-done.10.rest_1_), channel_id=1, source_target_pairs={{0,16},{1,17},{2,18},{3,19},{4,20},{5,21},{6,22},{7,23},{8,24},{9,... | collective-permute-start | bytes 1572872 | tf_op jit(solution)/shard_map/ppermute | solution.py:41
  130.6 16.9 %collective-permute-start.15 = (f32[1024,128]{1,0:T(8,128)S(1)}, f32[1024,128]{1,0:T(8,128)S(1)}, u32[]{:S(2)}, u32[]{:S(2)}) collective-permute-start(f32[1024,128]{1,0:T(8,128)S(1)} %collective-permute-done.11.rest_2_), channel_id=1, source_target_pairs={{0,16},{1,17},{2,18},{3,19},{4,20},{5,21},{6,22},{7,23},{8,24},{9,... | collective-permute-start | bytes 1572872 | tf_op jit(solution)/shard_map/ppermute | solution.py:41
  130.6 16.9 %collective-permute-start.16 = (f32[1024,128]{1,0:T(8,128)S(1)}, f32[1024,128]{1,0:T(8,128)}, u32[]{:S(2)}, u32[]{:S(2)}) collective-permute-start(f32[1024,128]{1,0:T(8,128)S(1)} %collective-permute-done.12.rest_3_), channel_id=1, source_target_pairs={{0,16},{1,17},{2,18},{3,19},{4,20},{5,21},{6,22},{7,23},{8,24},{9,... | collective-permute-start | bytes 1572872 | tf_op jit(solution)/shard_map/ppermute | solution.py:41
  147.5 0.8 copy-start.1
  147.5 1.0 copy-start.5
  147.5 1.1 copy-start.6

commit v4 on v3

--- a/solution.py
+++ b/solution.py
@@ -188,8 +188,8 @@
 
 
 def chain_kernel(
-    info, u_ref, v_ref, wr_ref, wc_ref,
-    ft_ref, y_ref,
+    info, u_ref, v_ref, wr_ref, wc_ref, vj_ref, wj_ref,
+    f_ref, y_ref,
     state, side, work, spread, solved, lines, stack, tall,
 ):
     state[:, LEAD:] = jnp.zeros((LEAD + BASE, LEAD), F32)
@@ -199,7 +199,7 @@
     row = lax.broadcasted_iota(jnp.int32, (BASE, BASE), 0)
     eye = (row == lane).astype(F32)
     geometry = (u_ref, v_ref, wr_ref, wc_ref)
-    slot, column = info[0], info[1]
+    column = info[1]
     offset = pl.multiple_of(info[2], BASE)
 
     @pl.loop(0, TILE // 256)
@@ -214,7 +214,7 @@
             across = 256 + lax.broadcasted_iota(jnp.int32, (256, 256), 1)
             values = values + jnp.where(line == across, wr_ref[tile, rows, 4:5], 0.0)
             state[here, low + 256 : low + TILE] = values
-            side[here, :] = assemble(*geometry, tile, 6 + slot, start, 256, pl.ds(offset, BASE))
+            side[here, :] = assemble(u_ref, vj_ref, wr_ref, wj_ref, tile, 0, start, 256, pl.ds(offset, BASE))
         state[rows, TILE : 2 * TILE] = assemble(*geometry, 0, 1, start, 256)
 
     for tile in range(2):
@@ -274,7 +274,18 @@
             state[below, window] = state[below, window] - update[:, :WINDOW]
             side[below, :] = side[below, :] - update[:, WINDOW:]
 
-    ft_ref[...] = state[:LEAD, :LEAD]
+    which = info[11]
+
+    @pl.when((which == 0) | (which == 2) | (which == 3))
+    def _():
+        from_rows = pl.ds(pl.multiple_of(which % 2 * TILE, TILE), TILE)
+        for chunk in range(TILE // BASE):
+            from_cols = pl.ds(pl.multiple_of(which // 2 * TILE + chunk * BASE, BASE), BASE)
+            values = jnp.transpose(state[from_rows, from_cols])
+            line = chunk * BASE + lax.broadcasted_iota(jnp.int32, (BASE, TILE), 0)
+            across = lax.broadcasted_iota(jnp.int32, (BASE, TILE), 1)
+            keep = (line >= across) | (which == 2)
+            f_ref[chunk * BASE : chunk * BASE + BASE, :] = jnp.where(keep, values, 0.0)
 
     @pl.when(column < 2)
     def _():
@@ -304,7 +315,7 @@
     @pl.when(needed(kinds[0]) | needed(kinds[1]))
     def _():
         for half in range(2):
-            values = assemble(u_ref, v_ref, wr_ref, wc_ref, 2 + slot, half, start, CHUNK)
+            values = assemble(u_ref, v_ref, wr_ref, wc_ref, 0, half, start, CHUNK)
             cols = slice(half * TILE, half * TILE + TILE)
             ah_ref[:, cols], al_ref[:, cols] = split(values)
 
@@ -313,7 +324,7 @@
 ZERO, UPDATE, DIAGONAL, PANEL, FACTOR = range(5)
 
 
-def final_kernel(info, u_ref, v_ref, wr_ref, wc_ref, ft_ref, *rest):
+def final_kernel(info, u_ref, v_ref, wr_ref, wc_ref, f_ref, *rest):
     parts, (ah, al, out_ref, yh, yl) = rest[:8], rest[8:]
     slot, chunk = pl.program_id(0), pl.program_id(1)
     start = pl.multiple_of(chunk * CHUNK, CHUNK)
@@ -343,24 +354,17 @@
 
         @pl.when((kind == UPDATE) | (kind == DIAGONAL))
         def _():
-            values = assemble(u_ref, v_ref, wr_ref, wc_ref, 2 + slot, 6 + j, start, CHUNK)
+            values = assemble(u_ref, v_ref, wr_ref, wc_ref, 0, j, start, CHUNK)
             row = start + lax.broadcasted_iota(jnp.int32, (CHUNK, TILE), 0)
             col = lax.broadcasted_iota(jnp.int32, (CHUNK, TILE), 1)
-            shift = wr_ref[2 + slot, pl.ds(start, CHUNK), 4:5]
+            shift = wr_ref[0, pl.ds(start, CHUNK), 4:5]
             values = values + jnp.where((row == col) & (kind == DIAGONAL), shift, 0.0)
             store(j, values - dot3(ah[...], al[...], yh[j], yl[j]))
 
         if j == 0:
             @pl.when(kind == FACTOR)
             def _():
-                which = info[11]
-                lanes = pl.ds(pl.multiple_of(which // 2 * TILE + start, CHUNK), CHUNK)
-                rows = pl.ds(pl.multiple_of(which % 2 * TILE, TILE), TILE)
-                values = jnp.transpose(ft_ref[rows, lanes])
-                row = start + lax.broadcasted_iota(jnp.int32, (CHUNK, TILE), 0)
-                col = lax.broadcasted_iota(jnp.int32, (CHUNK, TILE), 1)
-                keep = (row >= col) | (which // 2 != which % 2)
-                store(j, jnp.where(keep, values, 0.0))
+                store(j, f_ref[pl.ds(start, CHUNK), :])
 
 
 def whole(count):
@@ -426,53 +430,72 @@
     order = jnp.arange(8, dtype=jnp.int32)
     sources = (row // 2 - order % 4) % 4 * 2 + (row % 2 - order // 4) % 2
     head = jnp.stack([mine, col + cols * mine, row % 4 * BASE])
-    info = jnp.concatenate([head, kinds.reshape(-1), (row * 2 + col)[None], sources]).astype(jnp.int32)
-
-    smem = [pl.BlockSpec(memory_space=pltpu.SMEM)]
-    ft, weights_part = pl.pallas_call(
+    info = jnp.concatenate([head, kinds.reshape(-1), jnp.where((row < 2) & (col < 2), row * 2 + col, 1)[None], sources]).astype(jnp.int32)
+
+    def geometry(left, right, held):
+        return [
+            pl.BlockSpec((held, QUAD, TILE, FEAT), lambda *at: (left(*at), 0, 0, 0)),
+            pl.BlockSpec((2, QUAD, FEAT, TILE), lambda *at: (right, 0, 0, 0)),
+            pl.BlockSpec((held, TILE, 128), lambda *at: (left(*at), 0, 0)),
+            pl.BlockSpec((2, 8, TILE), lambda *at: (right, 0, 0)),
+        ]
+
+    factor, weights_part = pl.pallas_call(
         chain_kernel,
-        in_specs=smem + whole(4),
-        out_specs=whole(2),
-        out_shape=[jax.ShapeDtypeStruct((LEAD, LEAD), F32), jax.ShapeDtypeStruct((LEAD, BASE), F32)],
-        scratch_shapes=[
-            pltpu.VMEM((LEAD + BASE, 2 * LEAD), F32),
-            pltpu.VMEM((LEAD + BASE, BASE), F32),
-            pltpu.VMEM((BASE, BASE), F32),
-            pltpu.VMEM((STEP, STEP, BASE), F32),
-            pltpu.VMEM((STEP, STEP, BASE), F32),
-            pltpu.VMEM((STEP, BASE), F32),
-            pltpu.VMEM((4 * BASE, WINDOW + BASE), BF16),
-            pltpu.VMEM((LEAD, 6 * BASE), BF16),
-        ],
+        grid_spec=pltpu.PrefetchScalarGridSpec(
+            num_scalar_prefetch=1,
+            grid=(1,),
+            in_specs=geometry(lambda *at: 0, 0, 2)
+            + [
+                pl.BlockSpec((1, QUAD, FEAT, TILE), lambda i, info: (6 + info[0], 0, 0, 0)),
+                pl.BlockSpec((1, 8, TILE), lambda i, info: (6 + info[0], 0, 0)),
+            ],
+            out_specs=[
+                pl.BlockSpec((TILE, TILE), lambda i, info: (0, 0)),
+                pl.BlockSpec((LEAD, BASE), lambda i, info: (0, 0)),
+            ],
+            scratch_shapes=[
+                pltpu.VMEM((LEAD + BASE, 2 * LEAD), F32),
+                pltpu.VMEM((LEAD + BASE, BASE), F32),
+                pltpu.VMEM((BASE, BASE), F32),
+                pltpu.VMEM((STEP, STEP, BASE), F32),
+                pltpu.VMEM((STEP, STEP, BASE), F32),
+                pltpu.VMEM((STEP, BASE), F32),
+                pltpu.VMEM((4 * BASE, WINDOW + BASE), BF16),
+                pltpu.VMEM((LEAD, 6 * BASE), BF16),
+            ],
+        ),
+        out_shape=[jax.ShapeDtypeStruct((TILE, TILE), F32), jax.ShapeDtypeStruct((LEAD, BASE), F32)],
         name="chain",
-    )(info, u, v, wr, wc)
+    )(info, u, v, wr, wc, v, wc)
 
     tall = jax.ShapeDtypeStruct((4 * TILE, LEAD), BF16)
     chunks = TILE // CHUNK
 
-    def panel(base, held):
+    def panel(base, count, held):
         blocked = pl.BlockSpec((CHUNK, LEAD), lambda i, h, info: ((base + i) * chunks + h, 0))
         return pl.pallas_call(
             functools.partial(panel_kernel, base),
             grid_spec=pltpu.PrefetchScalarGridSpec(
                 num_scalar_prefetch=1,
-                grid=(2, chunks),
-                in_specs=whole(4) + [pl.BlockSpec(memory_space=pl.ANY)] * len(held),
+                grid=(count, chunks),
+                in_specs=geometry(lambda i, h, info: 2 + base + i, 0, 1)
+                + [pl.BlockSpec(memory_space=pl.ANY)] * len(held),
                 out_specs=[blocked] * 2,
             ),
             out_shape=[tall] * 2,
             input_output_aliases={5 + i: i for i in range(len(held))},
             cost_estimate=pl.CostEstimate(
-                flops=30_000_000_000, bytes_accessed=8_000_000, transcendentals=17_000_000
+                flops=count * 15_000_000_000, bytes_accessed=count * 4_000_000, transcendentals=count * 8_000_000
             ),
             name=f"panel{base}",
         )(info, u, v, wr, wc, *held)
 
     near = [send(weights_part, lambda y, c, x, z, k=k: (y + k, c, x, z), rows, cols) for k in range(1, 4)]
-    *near, ah, al = lax.optimization_barrier((*near, *panel(0, [])))
+    *near, ah, al = lax.optimization_barrier((*near, *panel(0, 3, [])))
     parts = [weights_part] + near
     parts = parts + [send(part, lambda y, c, x, z: (y, c + 1, x, z), rows, cols) for part in parts]
-    *parts, ah, al = lax.optimization_barrier((*parts, *panel(2, [ah, al])))
+    *parts, ah, al = lax.optimization_barrier((*parts, *panel(3, 1, [ah, al])))
 
     lines = CHUNK * 8
     out = pl.pallas_call(
@@ -480,14 +503,15 @@
         grid_spec=pltpu.PrefetchScalarGridSpec(
             num_scalar_prefetch=1,
             grid=(4, chunks),
-            in_specs=whole(13)
+            in_specs=geometry(lambda i, h, info: 2 + i, 3, 1)
+            + whole(9)
             + [pl.BlockSpec((CHUNK, LEAD), lambda i, h, info: (i * chunks + h, 0))] * 2,
             out_specs=pl.BlockSpec((lines, 128), lambda i, h, info: (i * chunks + h, 0)),
             scratch_shapes=[pltpu.VMEM((2, LEAD, TILE), BF16)] * 2,
         ),
         out_shape=jax.ShapeDtypeStruct((4 * TILE * 8, 128), F32),
         name="final",
-    )(info, u, v, wr, wc, ft, *parts, ah, al)
+    )(info, u, v, wr, wc, factor, *parts, ah, al)
     return out.reshape(4, 1, TILE, 2, 1, TILE)
 
 

time: 185 us -> 173 us (0.935)
  Pallas kernels: 138 us -> 129 us
  waiting for transfers between devices: 17.2 us -> 13.7 us
    pallas_call x2, Pallas kernels: 32.6 us -> 28.3 us  [panel(): pl.pallas_call(functools.partial(panel_kernel, base), grid_spec=pltpu.Pre...]
    ppermute x17, waiting for transfers between devices: 17.2 us -> 13.7 us  [send(): return lax.ppermute(value, ('row', 'col'), pairs)]
    pallas_call x1, Pallas kernels: 35.7 us -> 32.9 us  [shards(): pl.pallas_call(final_kernel, grid_spec=pltpu.PrefetchScalarGridSpec(num_s...]
    pallas_call x1, Pallas kernels: 62.7 us -> 60.7 us  [shards(): pl.pallas_call(chain_kernel, grid_spec=pltpu.PrefetchScalarGridSpec(num_s...]
  transfers between devices with their start and end apart: 17 -> 17, of which waited for: 9 -> 9; matrix products, arithmetic and copies ran while one was open for 1% -> 2% of each run, Pallas kernels for 18% -> 16%
where the time goes in v4:
time: 173 us; the launch traced here: 172 us
  Pallas kernels  129 us (75%)
  starting transfers between devices  22 us (13%)
  waiting for transfers between devices  13.7 us (8%)
  local copies, waits for them, and re-layouts  4.56 us (3%)
  other arithmetic  2.02 us (1%)
    pallas_call x1, Pallas kernels, shards(): pl.pallas_call(chain_kernel, grid_spec=pltpu.PrefetchScalarGridSpec(num_s...  60.7 us
    pallas_call x1, Pallas kernels, shards(): pl.pallas_call(final_kernel, grid_spec=pltpu.PrefetchScalarGridSpec(num_s...  32.9 us
    pallas_call x2, Pallas kernels, panel(): pl.pallas_call(functools.partial(panel_kernel, base), grid_spec=pltpu.Pre...  28.3 us
    ppermute x17, starting transfers between devices, send(): return lax.ppermute(value, ('row', 'col'), pairs)  22 us
    ppermute x17, waiting for transfers between devices, send(): return lax.ppermute(value, ('row', 'col'), pairs)  13.7 us
    pallas_call x1, Pallas kernels, shards(): pl.pallas_call(prep_kernel, grid_spec=pltpu.PrefetchScalarGridSpec(num_sc...  7.4 us
  transfers between devices with their start and end apart: 17, of which 9 were waited for; matrix products, arithmetic and copies ran while one was open for 2% of the time, Pallas kernels for 16%

profile of v4, /device:TPU:73, one launch (start us, length us, event | category | flops | bytes accessed | tf_op | source)
XLA Modules:
  0.0 171.7 jit_solution(12115541304259601268)
XLA Ops:
  0.0 0.0 copy-start.7
  0.0 0.7 reshape.151
  0.7 0.1 pad.7.clone
  0.8 0.8 maximum_bitcast_fusion
  1.6 0.0 collective-permute-start.2
  1.6 3.1 %collective-permute-start.1 = (f32[1,24,128]{2,1,0:T(8,128)S(1)}, f32[1,24,128]{2,1,0:T(8,128)S(1)}, u32[]{:S(2)}, u32[]{:S(2)}) collective-permute-start(f32[1,24,128]{2,1,0:T(8,128)S(1)} %maximum_bitcast_fusion), channel_id=1, source_target_pairs={{0,2},{1,3},{2,0},{3,1},{4,6},{5,7},{6,4},{7,5},{8,10},{9,11},{10,... | collective-permute-start | bytes 36872 | tf_op jit(solution)/shard_map/ppermute | solution.py:41
  4.7 0.0 collective-permute-start
  4.7 0.8 constant_dynamic-update-slice_fusion.16
  5.5 0.0 collective-permute-done.2
  5.5 0.3 collective-permute-done.1
  5.8 1.5 collective-permute-done
  7.3 2.5 %collective-permute-start.5 = (f32[4,24,128]{2,1,0:T(8,128)S(1)}, f32[4,24,128]{2,1,0:T(8,128)S(1)}, u32[]{:S(2)}, u32[]{:S(2)}) collective-permute-start(f32[4,24,128]{2,1,0:T(8,128)S(1)} %pad_maximum_fusion), channel_id=1, source_target_pairs={{0,12},{1,13},{2,14},{3,15},{4,0},{5,1},{6,2},{7,3},{8,4},{9,5},{1... | collective-permute-start | bytes 147464 | tf_op jit(solution)/shard_map/ppermute | solution.py:41
  9.7 0.5 collective-permute-start.4
  10.3 0.6 collective-permute-start.3
  10.9 3.8 %collective-permute-done.3 = f32[4,24,128]{2,1,0:T(8,128)S(1)} collective-permute-done((f32[4,24,128]{2,1,0:T(8,128)S(1)}, f32[4,24,128]{2,1,0:T(8,128)S(1)}, u32[]{:S(2)}, u32[]{:S(2)}) %collective-permute-start.3) | collective-permute-done | bytes 49184 | tf_op jit(solution)/shard_map/ppermute | solution.py:41
  14.7 0.0 collective-permute-done.4
  14.8 0.0 collective-permute-done.5
  14.8 1.4 collective-permute-start.6
  16.2 0.1 select_select_fusion
  16.2 0.1 select_n.154
  16.3 0.8 collective-permute-start.7
  17.1 2.0 %collective-permute-start.8 = (f32[16,24,128]{2,1,0:T(8,128)S(1)}, f32[16,24,128]{2,1,0:T(8,128)S(1)}, u32[]{:S(2)}, u32[]{:S(2)}) collective-permute-start(f32[16,24,128]{2,1,0:T(8,128)S(1)} %get-tuple-element.65), channel_id=1, source_target_pairs={{0,96},{1,97},{2,98},{3,99},{4,100},{5,101},{6,102},{7,103},{8,104... | collective-permute-start | bytes 589832 | tf_op jit(solution)/shard_map/ppermute | solution.py:41
  19.1 0.2 collective-permute-done.6
  19.4 3.1 %collective-permute-done.7 = f32[16,24,128]{2,1,0:T(8,128)S(1)} collective-permute-done((f32[16,24,128]{2,1,0:T(8,128)S(1)}, f32[16,24,128]{2,1,0:T(8,128)S(1)}, u32[]{:S(2)}, u32[]{:S(2)}) %collective-permute-start.7) | collective-permute-done | bytes 196640 | tf_op jit(solution)/shard_map/ppermute | solution.py:41
  22.5 1.5 collective-permute-done.8
  24.0 5.4 %collective-permute-start.9 = (f32[64,24,128]{2,1,0:T(8,128)S(1)}, f32[64,24,128]{2,1,0:T(8,128)S(1)}, u32[]{:S(2)}, u32[]{:S(2)}) collective-permute-start(f32[64,24,128]{2,1,0:T(8,128)S(1)} %get-tuple-element.57), channel_id=1, source_target_pairs={{0,16},{1,17},{2,18},{3,19},{4,20},{5,21},{6,22},{7,23},{8,24},{9,... | collective-permute-start | bytes 2359304 | tf_op jit(solution)/shard_map/ppermute | solution.py:41
  29.5 0.1 pad_add_fusion
  29.5 0.0 copy-done.7
  29.5 0.2 select_reduce_fusion
  29.8 0.1 broadcast_add_fusion
  29.8 0.6 add.172.where_ref
  30.4 0.7 concatenate.24.info
  31.1 0.3 collective-permute-done.9
  31.4 0.1 constant_dynamic-update-slice_fusion.17.g0.g1.g2.g3
  31.4 0.0 copy-start
  31.4 1.1 copy-done
  32.6 7.4 %prep.1 = (bf16[8,4,512,48]{3,2,1,0:T(8,128)(2,1)}, bf16[8,4,48,512]{3,2,1,0:T(8,128)(2,1)}, f32[8,512,128]{2,1,0:T(8,128)}, f32[8,8,512]{2,1,0:T(8,128)}) custom-call(s32[32]{0:T(128)} %add.172.where_ref, f32[128,24,128]{2,1,0:T(8,128)} %copy-done, f32[128,24,128]{2,1,0:T(8,128)} %copy-done, f32[128,24,128]{2,1,0:T(8,128)} %copy-done, f32[128,24,128]{2,1,0:T(8,128)} %copy-done), custom_call_target="tpu_custom_call" | custom-call | tf_op jit(solution)/shard_map/prep/pallas_call | solution.py:396
  40.0 60.7 %chain.1 = (f32[512,512]{1,0:T(8,128)}, f32[1024,128]{1,0:T(8,128)}) custom-call(s32[20]{0:T(128)} %concatenate.24.info, bf16[8,4,512,48]{3,2,1,0:T(8,128)(2,1)} %get-tuple-element.30.u_ref, bf16[8,4,48,512]{3,2,1,0:T(8,128)(2,1)} %get-tuple-element.31.v_ref.vj_ref, f32[8,512,128]{2,1,0:T(8,128)} %get-tuple-element.32.wr_ref, ...), custom_call_target="tpu_custom_call" | custom-call | tf_op jit(solution)/shard_map/chain/pallas_call | solution.py:443
  100.7 0.4 collective-permute-start.13
  101.1 0.0 collective-permute-start.12
  101.1 2.0 %collective-permute-start.11 = (f32[1024,128]{1,0:T(8,128)}, f32[1024,128]{1,0:T(8,128)S(1)}, u32[]{:S(2)}, u32[]{:S(2)}) collective-permute-start(f32[1024,128]{1,0:T(8,128)} %get-tuple-element.45.rest_0_), channel_id=1, source_target_pairs={{0,64},{1,65},{2,66},{3,67},{4,68},{5,69},{6,70},{7,71},{8,72},{9,... | collective-permute-start | bytes 1572872 | tf_op jit(solution)/shard_map/ppermute | solution.py:41
  103.1 1.4 collective-permute-start.10
  104.5 19.8 %panel0.1 = (bf16[2048,1024]{1,0:T(8,128)(2,1)}, bf16[2048,1024]{1,0:T(8,128)(2,1)}) custom-call(s32[20]{0:T(128)} %concatenate.24.info, bf16[8,4,512,48]{3,2,1,0:T(8,128)(2,1)} %get-tuple-element.30.u_ref, bf16[8,4,48,512]{3,2,1,0:T(8,128)(2,1)} %get-tuple-element.31.v_ref.vj_ref, f32[8,512,128]{2,1,0:T(8,128)} %get-tuple-element.32.wr_ref, ...), custom_call_target="tpu_custom_call" | custom-call | flops 44999999488 | bytes 12000000 | tf_op jit(solution)/shard_map/panel0/pallas_call | solution.py:477
  124.3 0.0 collective-permute-done.12.rest_3_
  124.3 2.1 %collective-permute-done.11.rest_2_ = f32[1024,128]{1,0:T(8,128)S(1)} collective-permute-done((f32[1024,128]{1,0:T(8,128)}, f32[1024,128]{1,0:T(8,128)S(1)}, u32[]{:S(2)}, u32[]{:S(2)}) %collective-permute-start.11) | collective-permute-done | bytes 524320 | tf_op jit(solution)/shard_map/ppermute | solution.py:41
  126.4 1.0 collective-permute-done.10.rest_1_
  127.4 1.3 collective-permute-start.14
  128.7 0.0 collective-permute-start.15
  128.7 0.5 collective-permute-start.16
  129.2 8.5 %panel3.1 = (bf16[2048,1024]{1,0:T(8,128)(2,1)}, bf16[2048,1024]{1,0:T(8,128)(2,1)}) custom-call(s32[20]{0:T(128)} %concatenate.24.info, bf16[8,4,512,48]{3,2,1,0:T(8,128)(2,1)} %get-tuple-element.30.u_ref, bf16[8,4,48,512]{3,2,1,0:T(8,128)(2,1)} %get-tuple-element.31.v_ref.vj_ref, ...), custom_call_target="tpu_custom_call", output_to_operand_aliasing={{0}: (5, {}), {1}: (6, {})} | custom-call | flops 15000000512 | bytes 4000000 | tf_op jit(solution)/shard_map/panel3/pallas_call | solution.py:477
  137.7 0.0 copy-done.2
  137.7 0.0 copy-done.3
  137.7 0.0 copy-done.4
  137.7 0.0 collective-permute-done.13.rest_4_
  137.7 0.0 copy-start.1
  137.7 0.0 collective-permute-done.14.rest_5_
  137.7 0.0 copy-start.5
  137.8 0.0 collective-permute-done.15.rest_6_
  137.8 0.0 copy-start.6
  137.8 0.0 collective-permute-done.16.rest_7_
  137.8 0.7 copy-done.1
  138.5 0.2 copy-done.5
  138.7 0.2 copy-done.6
  138.9 32.9 %final.1 = f32[16384,128]{1,0:T(8,128)} custom-call(s32[20]{0:T(128)} %concatenate.24.info, bf16[8,4,512,48]{3,2,1,0:T(8,128)(2,1)} %get-tuple-element.30.u_ref, bf16[8,4,48,512]{3,2,1,0:T(8,128)(2,1)} %get-tuple-element.31.v_ref.vj_ref, f32[8,512,128]{2,1,0:T(8,128)} %get-tuple-element.32.wr_ref, f32[8,8,512]{2,1,0:T(8,128)} %get-tuple-element.33.wc_ref.wj_ref, ...), custom_call_target="tpu_custom_call" | custom-call | tf_op jit(solution)/shard_map/final/pallas_call | solution.py:501
  (20 shorter events, 0.2 us)
Async XLA Ops:
  0.0 29.5 %copy-start.7 = (s32[32]{0:T(128)S(1)}, s32[32]{0:T(128)}, u32[]{:S(2)}) copy-start(s32[32]{0:T(128)} %param.7) | copy-start | bytes 388
  1.6 3.9 %collective-permute-start.2 = (f32[1,24,128]{2,1,0:T(8,128)S(1)}, f32[1,24,128]{2,1,0:T(8,128)S(1)}, u32[]{:S(2)}, u32[]{:S(2)}) collective-permute-start(f32[1,24,128]{2,1,0:T(8,128)S(1)} %maximum_bitcast_fusion), channel_id=1, source_target_pairs={{0,3},{1,0},{2,1},{3,2},{4,7},{5,4},{6,5},{7,6},{8,11},{9,8},{10,9... | collective-permute-start | bytes 36872 | tf_op jit(solution)/shard_map/ppermute | solution.py:41
  1.6 4.2 %collective-permute-start.1 = (f32[1,24,128]{2,1,0:T(8,128)S(1)}, f32[1,24,128]{2,1,0:T(8,128)S(1)}, u32[]{:S(2)}, u32[]{:S(2)}) collective-permute-start(f32[1,24,128]{2,1,0:T(8,128)S(1)} %maximum_bitcast_fusion), channel_id=1, source_target_pairs={{0,2},{1,3},{2,0},{3,1},{4,6},{5,7},{6,4},{7,5},{8,10},{9,11},{10,... | collective-permute-start | bytes 36872 | tf_op jit(solution)/shard_map/ppermute | solution.py:41
  4.7 2.5 %collective-permute-start = (f32[1,24,128]{2,1,0:T(8,128)S(1)}, f32[1,24,128]{2,1,0:T(8,128)S(1)}, u32[]{:S(2)}, u32[]{:S(2)}) collective-permute-start(f32[1,24,128]{2,1,0:T(8,128)S(1)} %maximum_bitcast_fusion), channel_id=1, source_target_pairs={{0,1},{1,2},{2,3},{3,0},{4,5},{5,6},{6,7},{7,4},{8,9},{9,10},{10,1... | collective-permute-start | bytes 36872 | tf_op jit(solution)/shard_map/ppermute | solution.py:41
  7.3 7.5 %collective-permute-start.5 = (f32[4,24,128]{2,1,0:T(8,128)S(1)}, f32[4,24,128]{2,1,0:T(8,128)S(1)}, u32[]{:S(2)}, u32[]{:S(2)}) collective-permute-start(f32[4,24,128]{2,1,0:T(8,128)S(1)} %pad_maximum_fusion), channel_id=1, source_target_pairs={{0,12},{1,13},{2,14},{3,15},{4,0},{5,1},{6,2},{7,3},{8,4},{9,5},{1... | collective-permute-start | bytes 147464 | tf_op jit(solution)/shard_map/ppermute | solution.py:41
  9.7 5.0 %collective-permute-start.4 = (f32[4,24,128]{2,1,0:T(8,128)S(1)}, f32[4,24,128]{2,1,0:T(8,128)S(1)}, u32[]{:S(2)}, u32[]{:S(2)}) collective-permute-start(f32[4,24,128]{2,1,0:T(8,128)S(1)} %pad_maximum_fusion), channel_id=1, source_target_pairs={{0,8},{1,9},{2,10},{3,11},{4,12},{5,13},{6,14},{7,15},{8,0},{9,1},... | collective-permute-start | bytes 147464 | tf_op jit(solution)/shard_map/ppermute | solution.py:41
  10.3 4.5 %collective-permute-start.3 = (f32[4,24,128]{2,1,0:T(8,128)S(1)}, f32[4,24,128]{2,1,0:T(8,128)S(1)}, u32[]{:S(2)}, u32[]{:S(2)}) collective-permute-start(f32[4,24,128]{2,1,0:T(8,128)S(1)} %pad_maximum_fusion), channel_id=1, source_target_pairs={{0,4},{1,5},{2,6},{3,7},{4,8},{5,9},{6,10},{7,11},{8,12},{9,13},{1... | collective-permute-start | bytes 147464 | tf_op jit(solution)/shard_map/ppermute | solution.py:41
  14.8 4.6 %collective-permute-start.6 = (f32[16,24,128]{2,1,0:T(8,128)S(1)}, f32[16,24,128]{2,1,0:T(8,128)S(1)}, u32[]{:S(2)}, u32[]{:S(2)}) collective-permute-start(f32[16,24,128]{2,1,0:T(8,128)S(1)} %get-tuple-element.65), channel_id=1, source_target_pairs={{0,32},{1,33},{2,34},{3,35},{4,36},{5,37},{6,38},{7,39},{8,40},{9,... | collective-permute-start | bytes 589832 | tf_op jit(solution)/shard_map/ppermute | solution.py:41
  16.3 6.2 %collective-permute-start.7 = (f32[16,24,128]{2,1,0:T(8,128)S(1)}, f32[16,24,128]{2,1,0:T(8,128)S(1)}, u32[]{:S(2)}, u32[]{:S(2)}) collective-permute-start(f32[16,24,128]{2,1,0:T(8,128)S(1)} %get-tuple-element.65), channel_id=1, source_target_pairs={{0,64},{1,65},{2,66},{3,67},{4,68},{5,69},{6,70},{7,71},{8,72},{9,... | collective-permute-start | bytes 589832 | tf_op jit(solution)/shard_map/ppermute | solution.py:41
  17.1 6.9 %collective-permute-start.8 = (f32[16,24,128]{2,1,0:T(8,128)S(1)}, f32[16,24,128]{2,1,0:T(8,128)S(1)}, u32[]{:S(2)}, u32[]{:S(2)}) collective-permute-start(f32[16,24,128]{2,1,0:T(8,128)S(1)} %get-tuple-element.65), channel_id=1, source_target_pairs={{0,96},{1,97},{2,98},{3,99},{4,100},{5,101},{6,102},{7,103},{8,104... | collective-permute-start | bytes 589832 | tf_op jit(solution)/shard_map/ppermute | solution.py:41
  24.0 7.3 %collective-permute-start.9 = (f32[64,24,128]{2,1,0:T(8,128)S(1)}, f32[64,24,128]{2,1,0:T(8,128)S(1)}, u32[]{:S(2)}, u32[]{:S(2)}) collective-permute-start(f32[64,24,128]{2,1,0:T(8,128)S(1)} %get-tuple-element.57), channel_id=1, source_target_pairs={{0,16},{1,17},{2,18},{3,19},{4,20},{5,21},{6,22},{7,23},{8,24},{9,... | collective-permute-start | bytes 2359304 | tf_op jit(solution)/shard_map/ppermute | solution.py:41
  31.4 1.1 copy-start
  100.7 37.0 %collective-permute-start.13 = (f32[1024,128]{1,0:T(8,128)}, f32[1024,128]{1,0:T(8,128)S(1)}, u32[]{:S(2)}, u32[]{:S(2)}) collective-permute-start(f32[1024,128]{1,0:T(8,128)} %get-tuple-element.45.rest_0_), channel_id=1, source_target_pairs={{0,16},{1,17},{2,18},{3,19},{4,20},{5,21},{6,22},{7,23},{8,24},{9,... | collective-permute-start | bytes 1572872 | tf_op jit(solution)/shard_map/ppermute | solution.py:41
  101.1 23.2 %collective-permute-start.12 = (f32[1024,128]{1,0:T(8,128)}, f32[1024,128]{1,0:T(8,128)S(1)}, u32[]{:S(2)}, u32[]{:S(2)}) collective-permute-start(f32[1024,128]{1,0:T(8,128)} %get-tuple-element.45.rest_0_), channel_id=1, source_target_pairs={{0,96},{1,97},{2,98},{3,99},{4,100},{5,101},{6,102},{7,103},{8,104... | collective-permute-start | bytes 1572872 | tf_op jit(solution)/shard_map/ppermute | solution.py:41
  101.1 25.3 %collective-permute-start.11 = (f32[1024,128]{1,0:T(8,128)}, f32[1024,128]{1,0:T(8,128)S(1)}, u32[]{:S(2)}, u32[]{:S(2)}) collective-permute-start(f32[1024,128]{1,0:T(8,128)} %get-tuple-element.45.rest_0_), channel_id=1, source_target_pairs={{0,64},{1,65},{2,66},{3,67},{4,68},{5,69},{6,70},{7,71},{8,72},{9,... | collective-permute-start | bytes 1572872 | tf_op jit(solution)/shard_map/ppermute | solution.py:41
  103.1 24.3 %collective-permute-start.10 = (f32[1024,128]{1,0:T(8,128)}, f32[1024,128]{1,0:T(8,128)S(1)}, u32[]{:S(2)}, u32[]{:S(2)}) collective-permute-start(f32[1024,128]{1,0:T(8,128)} %get-tuple-element.45.rest_0_), channel_id=1, source_target_pairs={{0,32},{1,33},{2,34},{3,35},{4,36},{5,37},{6,38},{7,39},{8,40},{9,... | collective-permute-start | bytes 1572872 | tf_op jit(solution)/shard_map/ppermute | solution.py:41
  124.3 13.4 %copy-start.2 = (f32[1024,128]{1,0:T(8,128)}, f32[1024,128]{1,0:T(8,128)S(1)}, u32[]{:S(2)}) copy-start(f32[1024,128]{1,0:T(8,128)S(1)} %collective-permute-done.12.rest_3_) | copy-start | bytes 1572868
  126.4 11.3 %copy-start.3 = (f32[1024,128]{1,0:T(8,128)}, f32[1024,128]{1,0:T(8,128)S(1)}, u32[]{:S(2)}) copy-start(f32[1024,128]{1,0:T(8,128)S(1)} %collective-permute-done.11.rest_2_) | copy-start | bytes 1572868
  127.4 10.3 %copy-start.4 = (f32[1024,128]{1,0:T(8,128)}, f32[1024,128]{1,0:T(8,128)S(1)}, u32[]{:S(2)}) copy-start(f32[1024,128]{1,0:T(8,128)S(1)} %collective-permute-done.10.rest_1_) | copy-start | bytes 1572868
  127.4 10.3 %collective-permute-start.14 = (f32[1024,128]{1,0:T(8,128)S(1)}, f32[1024,128]{1,0:T(8,128)S(1)}, u32[]{:S(2)}, u32[]{:S(2)}) collective-permute-start(f32[1024,128]{1,0:T(8,128)S(1)} %collective-permute-done.10.rest_1_), channel_id=1, source_target_pairs={{0,16},{1,17},{2,18},{3,19},{4,20},{5,21},{6,22},{7,23},{8,24},{9,... | collective-permute-start | bytes 1572872 | tf_op jit(solution)/shard_map/ppermute | solution.py:41
  128.7 9.1 %collective-permute-start.15 = (f32[1024,128]{1,0:T(8,128)S(1)}, f32[1024,128]{1,0:T(8,128)S(1)}, u32[]{:S(2)}, u32[]{:S(2)}) collective-permute-start(f32[1024,128]{1,0:T(8,128)S(1)} %collective-permute-done.11.rest_2_), channel_id=1, source_target_pairs={{0,16},{1,17},{2,18},{3,19},{4,20},{5,21},{6,22},{7,23},{8,24},{9,... | collective-permute-start | bytes 1572872 | tf_op jit(solution)/shard_map/ppermute | solution.py:41
  128.7 9.1 %collective-permute-start.16 = (f32[1024,128]{1,0:T(8,128)S(1)}, f32[1024,128]{1,0:T(8,128)}, u32[]{:S(2)}, u32[]{:S(2)}) collective-permute-start(f32[1024,128]{1,0:T(8,128)S(1)} %collective-permute-done.12.rest_3_), channel_id=1, source_target_pairs={{0,16},{1,17},{2,18},{3,19},{4,20},{5,21},{6,22},{7,23},{8,24},{9,... | collective-permute-start | bytes 1572872 | tf_op jit(solution)/shard_map/ppermute | solution.py:41
  137.7 0.8 copy-start.1
  137.7 1.0 copy-start.5
  137.8 1.1 copy-start.6

commit v5 on v4

--- a/solution.py
+++ b/solution.py
@@ -15,7 +15,8 @@
 FEAT = 48
 LEAD = 1024
 BASE = 128
-STEP = 16
+STEP = 32
+HALVES = STEP // 8
 WINDOW = LEAD + BASE
 HIGHEST = lax.Precision.HIGHEST
 
@@ -53,8 +54,9 @@
     return jnp.concatenate([held, send(held, lambda y, c, x, z: (y, c + 1, x, z), rows, cols)], 0)
 
 
-def prep_kernel(where_ref, g0, g1, g2, g3, u_ref, v_ref, wr_ref, wc_ref, pad):
-    geometry = jnp.concatenate([g0[...], g1[...], g2[...], g3[...]], axis=1)
+def prep_kernel(where_ref, g_ref, u_ref, v_ref, wr_ref, wc_ref, pad):
+    tile = pl.program_id(0)
+    geometry = jnp.concatenate([g_ref[where_ref[4 * tile + z], :, 0, :] for z in range(4)], axis=1)
     centred = geometry[0:12] - 0.5
     coarse = jnp.floor(centred * 256.0 + 0.5) * (1.0 / 256.0)
     fine = centred - coarse
@@ -83,8 +85,6 @@
     right += fine_high + fine_low + fine_high
     right += [one] * 3 + pieces(mixed + SOFTENING_SQUARED)
     pad[...] = jnp.zeros_like(pad)
-    tile = pl.program_id(0)
-
     @pl.when(tile < 6)
     def _():
         for quad in range(QUAD):
@@ -99,9 +99,9 @@
                 pad[k : k + 1, :] = value[quad : quad + 1, :]
             v_ref[quad] = pad[0:FEAT, :].astype(BF16)
 
-    pad[0:8, :] = geometry[12:20]
+    pad[0:5, :] = geometry[12:17]
     wr_ref[...] = jnp.transpose(pad[...])
-    wc_ref[...] = geometry[12:20]
+    wc_ref[0:5, :] = geometry[12:17]
 
 
 def assemble(u_ref, v_ref, wr_ref, wc_ref, left, right, start, count, cols=slice(0, TILE)):
@@ -136,8 +136,8 @@
     for step in range(BASE // STEP):
         low = step * STEP
         high = low + STEP
-        a, c = [], [[], []]
-        for half in range(2):
+        a, c = [], [[] for _ in range(HALVES)]
+        for half in range(HALVES):
             left = work[low + 8 * half : low + 8 * half + 8, :]
             for j in range(STEP):
                 column = jnp.broadcast_to(left[:, low + j : low + j + 1], (8, BASE))
@@ -146,7 +146,7 @@
             a.append(jnp.where(inside, jnp.where(lane == sub + (low + 8 * half), 1.0, 0.0), left))
             lines[8 * half : 8 * half + 8, :] = a[half]
         d = []
-        for half in range(2):
+        for half in range(HALVES):
             diagonal = c[half][8 * half]
             for j in range(8 * half + 1, 8 * half + 8):
                 diagonal = jnp.where(sub == j % 8, c[half][j], diagonal)
@@ -157,7 +157,7 @@
             scale = lax.rsqrt(pivot)
             first = j // 8
             line = repeat(lines, j) * scale
-            for half in range(first, 2):
+            for half in range(first, HALVES):
                 c[half][j] = c[half][j] * scale
                 solved[j, 8 * half : 8 * half + 8, :] = c[half][j]
                 if j + 2 < STEP:
@@ -167,15 +167,15 @@
                 factor = repeat(solved.at[j], k)
                 if k == j + 1:
                     pivot = repeat(spread.at[j], k) - factor * factor
-                for half in range(k // 8, 2):
+                for half in range(k // 8, HALVES):
                     c[half][k] = c[half][k] - c[half][j] * factor
-            for half in range(first, 2):
+            for half in range(first, HALVES):
                 update = a[half] - c[half][j] * line
                 if half == first:
                     update = jnp.where(sub > j % 8, update, jnp.where(sub == j % 8, line, a[half]))
                 a[half] = update
                 lines[8 * half : 8 * half + 8, :] = update
-        for half in range(2):
+        for half in range(HALVES):
             work[low + 8 * half : low + 8 * half + 8, :] = a[half]
         if high < BASE:
             w0, w1, w2 = split3(jnp.concatenate(a, 0))
@@ -255,24 +255,23 @@
         @pl.loop(0, blocks - 1 - k)
         def _(i):
             there = pl.multiple_of((i + 1) * BASE, BASE)
-            first, second, third = split3(jnp.transpose(state[rows, pl.ds(pl.multiple_of(here + there, BASE), BASE)]))
-            part = pl.ds(pl.multiple_of(i * BASE, BASE), BASE)
-            tall[part, 0:128] = first
-            tall[part, 128:256] = first
-            tall[part, 256:384] = second
-            tall[part, 384:512] = second
-            tall[part, 512:640] = first
-            tall[part, 640:768] = third
-
-        @pl.loop(0, (blocks - k) // 2)
-        def _(pair):
-            part = pl.ds(pl.multiple_of(pair * 256, 256), 256)
-            below = pl.ds(pl.multiple_of(here + BASE + pair * 256, BASE), 256)
-            update = dot(tall[part, 0:256], stack[0:256, :])
-            update += dot(tall[part, 256:512], stack[0:256, :])
-            update += dot(tall[part, 512:768], stack[256:512, :])
-            state[below, window] = state[below, window] - update[:, :WINDOW]
-            side[below, :] = side[below, :] - update[:, WINDOW:]
+            parts = split3(jnp.transpose(state[rows, pl.ds(pl.multiple_of(here + there, BASE), BASE)]))
+            for n, part in enumerate(parts):
+                tall[pl.ds(pl.multiple_of(i * BASE, BASE), BASE), n * 128 : n * 128 + 128] = part
+
+        for pair in range(blocks // 2):
+            @pl.when(pair < (blocks - k) // 2)
+            def _():
+                skip = pair * 256
+                below = pl.ds(pl.multiple_of(here + BASE + skip, BASE), 256)
+                t0, t1, t2 = [tall[skip : skip + 256, n * 128 : n * 128 + 128] for n in range(3)]
+                update = dot(both([t0, t0], 1), stack[0:256, skip:])
+                update += dot(both([t1, t1], 1), stack[0:256, skip:])
+                update += dot(both([t0, t2], 1), stack[256:512, skip:])
+                width = WINDOW - skip
+                into = pl.ds(pl.multiple_of(here + skip, BASE), width)
+                state[below, into] = state[below, into] - update[:, :width]
+                side[below, :] = side[below, :] - update[:, width:]
 
     which = info[11]
 
@@ -375,8 +374,7 @@
     rows, cols = lax.axis_size("row"), lax.axis_size("col")
     row, col = lax.axis_index("row"), lax.axis_index("col")
     width = shift.shape[0]
-    fill = jnp.zeros((7, width), F32)
-    shard = jnp.concatenate([points.reshape(12, width), weights, shift[None], fill], 0)
+    shard = jnp.concatenate([points.reshape(12, width), weights, shift[None]], 0)[:, None]
     gathered = gather_shards(shard)
 
     slots = jnp.arange(4, dtype=jnp.int32)
@@ -392,13 +390,12 @@
     dz = (col % 4 - slots) % 4
     where = ((((dc * 4 + dy) * 4 + dx) * 4)[:, None] + dz[None, :]).reshape(-1).astype(jnp.int32)
 
-    part = lambda z: pl.BlockSpec((None, 24, width), lambda t, at: (at[4 * t + z], 0, 0))
     u, v, wr, wc = pl.pallas_call(
         prep_kernel,
         grid_spec=pltpu.PrefetchScalarGridSpec(
             num_scalar_prefetch=1,
             grid=(8,),
-            in_specs=[part(z) for z in range(4)],
+            in_specs=whole(1),
             out_specs=[
                 pl.BlockSpec((None, QUAD, TILE, FEAT), lambda t, at: (t, 0, 0, 0)),
                 pl.BlockSpec((None, QUAD, FEAT, TILE), lambda t, at: (t, 0, 0, 0)),
@@ -414,7 +411,8 @@
             jax.ShapeDtypeStruct((8, 8, TILE), F32),
         ],
         name="prep",
-    )(where, *[gathered] * 4)
+        compiler_params=pltpu.CompilerParams(vmem_limit_bytes=16 << 20),
+    )(where, gathered)
 
     block_rows, block_cols = tile_rows[:, None], tile_cols[None, :]
     kinds = jnp.where(
@@ -462,11 +460,12 @@
                 pltpu.VMEM((STEP, STEP, BASE), F32),
                 pltpu.VMEM((STEP, BASE), F32),
                 pltpu.VMEM((4 * BASE, WINDOW + BASE), BF16),
-                pltpu.VMEM((LEAD, 6 * BASE), BF16),
+                pltpu.VMEM((LEAD, 3 * BASE), BF16),
             ],
         ),
         out_shape=[jax.ShapeDtypeStruct((TILE, TILE), F32), jax.ShapeDtypeStruct((LEAD, BASE), F32)],
         name="chain",
+        compiler_params=pltpu.CompilerParams(vmem_limit_bytes=36 << 20),
     )(info, u, v, wr, wc, v, wc)
 
     tall = jax.ShapeDtypeStruct((4 * TILE, LEAD), BF16)
@@ -489,6 +488,7 @@
                 flops=count * 15_000_000_000, bytes_accessed=count * 4_000_000, transcendentals=count * 8_000_000
             ),
             name=f"panel{base}",
+            compiler_params=pltpu.CompilerParams(vmem_limit_bytes=20 << 20),
         )(info, u, v, wr, wc, *held)
 
     near = [send(weights_part, lambda y, c, x, z, k=k: (y + k, c, x, z), rows, cols) for k in range(1, 4)]
@@ -511,6 +511,7 @@
         ),
         out_shape=jax.ShapeDtypeStruct((4 * TILE * 8, 128), F32),
         name="final",
+        compiler_params=pltpu.CompilerParams(vmem_limit_bytes=24 << 20),
     )(info, u, v, wr, wc, factor, *parts, ah, al)
     return out.reshape(4, 1, TILE, 2, 1, TILE)
 

time: 173 us -> 152 us (0.88)
  Pallas kernels: 129 us -> 111 us
  local copies, waits for them, and re-layouts: 4.56 us -> 1.84 us
    pallas_call x1, Pallas kernels: 60.7 us -> 50.8 us  [shards(): pl.pallas_call(chain_kernel, grid_spec=pltpu.PrefetchScalarGridSpec(num_s...]
    pallas_call x1, Pallas kernels: 7.4 us -> 3.88 us  [shards(): pl.pallas_call(prep_kernel, grid_spec=pltpu.PrefetchScalarGridSpec(num_sc...]
    pallas_call x2, Pallas kernels: 28.3 us -> 25.8 us  [panel(): pl.pallas_call(functools.partial(panel_kernel, base), grid_spec=pltpu.Pre...]
    pallas_call x1, Pallas kernels: 32.9 us -> 30.8 us  [shards(): pl.pallas_call(final_kernel, grid_spec=pltpu.PrefetchScalarGridSpec(num_s...]
  transfers between devices with their start and end apart: 17 -> 17, of which waited for: 9 -> 7; matrix products, arithmetic and copies ran while one was open for 2% -> 1% of each run, Pallas kernels for 16% -> 17%
where the time goes in v5:
time: 152 us; the launch traced here: 151 us
  Pallas kernels  111 us (73%)
  starting transfers between devices  23.7 us (16%)
  waiting for transfers between devices  12.8 us (8%)
  local copies, waits for them, and re-layouts  1.84 us (1%)
  other arithmetic  1.83 us (1%)
    pallas_call x1, Pallas kernels, shards(): pl.pallas_call(chain_kernel, grid_spec=pltpu.PrefetchScalarGridSpec(num_s...  50.8 us
    pallas_call x1, Pallas kernels, shards(): pl.pallas_call(final_kernel, grid_spec=pltpu.PrefetchScalarGridSpec(num_s...  30.8 us
    pallas_call x2, Pallas kernels, panel(): pl.pallas_call(functools.partial(panel_kernel, base), grid_spec=pltpu.Pre...  25.8 us
    ppermute x17, starting transfers between devices, send(): return lax.ppermute(value, ('row', 'col'), pairs)  23.7 us
    ppermute x17, waiting for transfers between devices, send(): return lax.ppermute(value, ('row', 'col'), pairs)  12.8 us
    pallas_call x1, Pallas kernels, shards(): pl.pallas_call(prep_kernel, grid_spec=pltpu.PrefetchScalarGridSpec(num_sc...  3.88 us
  transfers between devices with their start and end apart: 17, of which 7 were waited for; matrix products, arithmetic and copies ran while one was open for 1% of the time, Pallas kernels for 17%

profile of v5, /device:TPU:73, one launch (start us, length us, event | category | flops | bytes accessed | tf_op | source)
XLA Modules:
  0.0 151.4 jit_solution(4420437271611690999)
XLA Ops:
  0.0 0.7 reshape.151
  0.7 0.7 pad_maximum_fusion
  1.4 0.1 collective-permute-start.2
  1.5 3.1 %collective-permute-start.1 = (f32[1,17,1,128]{3,2,1,0:T(1,128)S(1)}, f32[1,17,1,128]{3,2,1,0:T(1,128)S(1)}, u32[]{:S(2)}, u32[]{:S(2)}) collective-permute-start(f32[1,17,1,128]{3,2,1,0:T(1,128)S(1)} %broadcast_in_dim_broadcast_in_dim.3), channel_id=1, source_target_pairs={{0,2},{1,3},{2,0},{3,1},{4,6},{5,7},{6,4},{7,5},{8,10},{9,11},{10,... | collective-permute-start | bytes 26120 | tf_op jit(solution)/shard_map/ppermute | solution.py:42
  4.6 0.0 collective-permute-start
  4.6 0.1 select_select_fusion
  4.7 2.4 %collective-permute-done = f32[1,17,1,128]{3,2,1,0:T(1,128)S(1)} collective-permute-done((f32[1,17,1,128]{3,2,1,0:T(1,128)S(1)}, f32[1,17,1,128]{3,2,1,0:T(1,128)S(1)}, u32[]{:S(2)}, u32[]{:S(2)}) %collective-permute-start) | collective-permute-done | bytes 8736 | tf_op jit(solution)/shard_map/ppermute | solution.py:42
  7.2 0.0 collective-permute-done.1
  7.2 0.0 collective-permute-done.2
  7.2 1.3 collective-permute-start.3
  8.5 0.1 pad_add_fusion
  8.6 1.5 collective-permute-start.5
  10.1 1.5 %collective-permute-start.4 = (f32[4,17,1,128]{3,2,1,0:T(1,128)S(1)}, f32[4,17,1,128]{3,2,1,0:T(1,128)S(1)}, u32[]{:S(2)}, u32[]{:S(2)}) collective-permute-start(f32[4,17,1,128]{3,2,1,0:T(1,128)S(1)} %get-tuple-element.75), channel_id=1, source_target_pairs={{0,8},{1,9},{2,10},{3,11},{4,12},{5,13},{6,14},{7,15},{8,0},{9,1},... | collective-permute-start | bytes 104456 | tf_op jit(solution)/shard_map/ppermute | solution.py:42
  11.6 0.0 collective-permute-done.3
  11.6 0.1 constant_dynamic-update-slice_fusion.16
  11.7 2.8 %collective-permute-done.4 = f32[4,17,1,128]{3,2,1,0:T(1,128)S(1)} collective-permute-done((f32[4,17,1,128]{3,2,1,0:T(1,128)S(1)}, f32[4,17,1,128]{3,2,1,0:T(1,128)S(1)}, u32[]{:S(2)}, u32[]{:S(2)}) %collective-permute-start.4) | collective-permute-done | bytes 34848 | tf_op jit(solution)/shard_map/ppermute | solution.py:42
  14.5 0.1 constant_dynamic-update-slice_fusion.15
  14.5 0.0 collective-permute-done.5
  14.5 0.1 constant_dynamic-update-slice_fusion.14
  14.6 1.4 collective-permute-start.6
  16.0 0.8 select_reduce_fusion
  16.8 0.8 collective-permute-start.7
  17.6 0.1 select_n.154
  17.7 2.1 %collective-permute-start.8 = (f32[16,17,1,128]{3,2,1,0:T(1,128)S(1)}, f32[16,17,1,128]{3,2,1,0:T(1,128)S(1)}, u32[]{:S(2)}, u32[]{:S(2)}) collective-permute-start(f32[16,17,1,128]{3,2,1,0:T(1,128)S(1)} %get-tuple-element.65), channel_id=1, source_target_pairs={{0,96},{1,97},{2,98},{3,99},{4,100},{5,101},{6,102},{7,103},{8,104... | collective-permute-start | bytes 417800 | tf_op jit(solution)/shard_map/ppermute | solution.py:42
  19.8 0.0 collective-permute-done.6
  19.8 0.2 constant_dynamic-update-slice_fusion.13
  20.0 2.4 %collective-permute-done.7 = f32[16,17,1,128]{3,2,1,0:T(1,128)S(1)} collective-permute-done((f32[16,17,1,128]{3,2,1,0:T(1,128)S(1)}, f32[16,17,1,128]{3,2,1,0:T(1,128)S(1)}, u32[]{:S(2)}, u32[]{:S(2)}) %collective-permute-start.7) | collective-permute-done | bytes 139296 | tf_op jit(solution)/shard_map/ppermute | solution.py:42
  22.4 0.2 constant_dynamic-update-slice_fusion.12
  22.6 0.9 collective-permute-done.8
  23.4 0.2 constant_dynamic-update-slice_fusion.11
  23.6 5.6 %collective-permute-start.9 = (f32[64,17,1,128]{3,2,1,0:T(1,128)S(1)}, f32[64,17,1,128]{3,2,1,0:T(1,128)S(1)}, u32[]{:S(2)}, u32[]{:S(2)}) collective-permute-start(f32[64,17,1,128]{3,2,1,0:T(1,128)S(1)} %get-tuple-element.57), channel_id=1, source_target_pairs={{0,16},{1,17},{2,18},{3,19},{4,20},{5,21},{6,22},{7,23},{8,24},{9,... | collective-permute-start | bytes 1671176 | tf_op jit(solution)/shard_map/ppermute | solution.py:42
  29.2 0.1 broadcast_add_fusion
  29.3 0.1 add.172.where_ref
  29.4 0.1 concatenate.24.info
  29.5 1.3 collective-permute-done.9
  30.8 0.1 constant_dynamic-update-slice_fusion.21.g_ref
  30.9 3.9 %prep.1 = (bf16[8,4,512,48]{3,2,1,0:T(8,128)(2,1)S(1)}, bf16[8,4,48,512]{3,2,1,0:T(8,128)(2,1)S(1)}, f32[8,512,128]{2,1,0:T(8,128)S(1)}, f32[8,8,512]{2,1,0:T(8,128)S(1)}) custom-call(s32[32]{0:T(128)S(1)} %add.172.where_ref, f32[128,17,1,128]{3,2,1,0:T(1,128)S(1)} %constant_dynamic-update-slice_fusion.21.g_ref), custom_call_target="tpu_custom_call" | custom-call | tf_op jit(solution)/shard_map/prep/pallas_call | solution.py:393
  34.8 50.8 %chain.1 = (f32[512,512]{1,0:T(8,128)S(1)}, f32[1024,128]{1,0:T(8,128)S(1)}) custom-call(s32[20]{0:T(128)S(1)} %concatenate.24.info, bf16[8,4,512,48]{3,2,1,0:T(8,128)(2,1)S(1)} %get-tuple-element.30.u_ref, bf16[8,4,48,512]{3,2,1,0:T(8,128)(2,1)S(1)} %get-tuple-element.31.v_ref.vj_ref, f32[8,512,128]{2,1,0:T(8,128)S(1)} %get-tuple-element.32.wr_ref, ...), custom_call_target="tpu_custom_call" | custom-call | tf_op jit(solution)/shard_map/chain/pallas_call | solution.py:441
  85.5 0.5 collective-permute-start.13
  86.0 0.6 collective-permute-start.12
  86.6 1.4 collective-permute-start.11
  88.0 2.1 %collective-permute-start.10 = (f32[1024,128]{1,0:T(8,128)S(1)}, f32[1024,128]{1,0:T(8,128)S(1)}, u32[]{:S(2)}, u32[]{:S(2)}) collective-permute-start(f32[1024,128]{1,0:T(8,128)S(1)} %get-tuple-element.45.rest_0_), channel_id=1, source_target_pairs={{0,32},{1,33},{2,34},{3,35},{4,36},{5,37},{6,38},{7,39},{8,40},{9,... | collective-permute-start | bytes 1572872 | tf_op jit(solution)/shard_map/ppermute | solution.py:42
  90.1 19.1 %panel0.1 = (bf16[2048,1024]{1,0:T(8,128)(2,1)S(1)}, bf16[2048,1024]{1,0:T(8,128)(2,1)S(1)}) custom-call(s32[20]{0:T(128)S(1)} %concatenate.24.info, bf16[8,4,512,48]{3,2,1,0:T(8,128)(2,1)S(1)} %get-tuple-element.30.u_ref, bf16[8,4,48,512]{3,2,1,0:T(8,128)(2,1)S(1)} %get-tuple-element.31.v_ref.vj_ref, f32[8,512,128]{2,1,0:T(8,128)S(1)} %get-tuple-element.32.wr_ref, ...), custom_call_target="tpu_custom_call" | custom-call | flops 44999999488 | bytes 12000000 | tf_op jit(solution)/shard_map/panel0/pallas_call | solution.py:476
  109.2 0.0 collective-permute-done.12.rest_3_
  109.2 2.0 %collective-permute-done.11.rest_2_ = f32[1024,128]{1,0:T(8,128)S(1)} collective-permute-done((f32[1024,128]{1,0:T(8,128)S(1)}, f32[1024,128]{1,0:T(8,128)S(1)}, u32[]{:S(2)}, u32[]{:S(2)}) %collective-permute-start.11) | collective-permute-done | bytes 524320 | tf_op jit(solution)/shard_map/ppermute | solution.py:42
  111.2 0.9 collective-permute-done.10.rest_1_
  112.1 1.3 collective-permute-start.14
  113.4 0.0 collective-permute-start.15
  113.4 0.5 collective-permute-start.16
  113.9 6.7 %panel3.1 = (bf16[2048,1024]{1,0:T(8,128)(2,1)S(1)}, bf16[2048,1024]{1,0:T(8,128)(2,1)S(1)}) custom-call(s32[20]{0:T(128)S(1)} %concatenate.24.info, bf16[8,4,512,48]{3,2,1,0:T(8,128)(2,1)S(1)} %get-tuple-element.30.u_ref, bf16[8,4,48,512]{3,2,1,0:T(8,128)(2,1)S(1)} %get-tuple-element.31.v_ref.vj_ref, ...), custom_call_target="tpu_custom_call", output_to_operand_aliasing={{0}: (5, {}), {1}: (6, {})} | custom-call | flops 15000000512 | bytes 4000000 | tf_op jit(solution)/shard_map/panel3/pallas_call | solution.py:476
  120.6 0.0 collective-permute-done.13.rest_4_
  120.6 0.0 collective-permute-done.14.rest_5_
  120.6 0.0 collective-permute-done.15.rest_6_
  120.7 0.0 collective-permute-done.16.rest_7_
  120.7 30.8 %final.1 = f32[16384,128]{1,0:T(8,128)} custom-call(s32[20]{0:T(128)S(1)} %concatenate.24.info, bf16[8,4,512,48]{3,2,1,0:T(8,128)(2,1)S(1)} %get-tuple-element.30.u_ref, bf16[8,4,48,512]{3,2,1,0:T(8,128)(2,1)S(1)} %get-tuple-element.31.v_ref.vj_ref, f32[8,512,128]{2,1,0:T(8,128)S(1)} %get-tuple-element.32.wr_ref, ...), custom_call_target="tpu_custom_call" | custom-call | tf_op jit(solution)/shard_map/final/pallas_call | solution.py:501
  (11 shorter events, 0.2 us)
Async XLA Ops:
  1.4 5.8 %collective-permute-start.2 = (f32[1,17,1,128]{3,2,1,0:T(1,128)S(1)}, f32[1,17,1,128]{3,2,1,0:T(1,128)S(1)}, u32[]{:S(2)}, u32[]{:S(2)}) collective-permute-start(f32[1,17,1,128]{3,2,1,0:T(1,128)S(1)} %broadcast_in_dim_broadcast_in_dim.3), channel_id=1, source_target_pairs={{0,3},{1,0},{2,1},{3,2},{4,7},{5,4},{6,5},{7,6},{8,11},{9,8},{10,9... | collective-permute-start | bytes 26120 | tf_op jit(solution)/shard_map/ppermute | solution.py:42
  1.5 5.7 %collective-permute-start.1 = (f32[1,17,1,128]{3,2,1,0:T(1,128)S(1)}, f32[1,17,1,128]{3,2,1,0:T(1,128)S(1)}, u32[]{:S(2)}, u32[]{:S(2)}) collective-permute-start(f32[1,17,1,128]{3,2,1,0:T(1,128)S(1)} %broadcast_in_dim_broadcast_in_dim.3), channel_id=1, source_target_pairs={{0,2},{1,3},{2,0},{3,1},{4,6},{5,7},{6,4},{7,5},{8,10},{9,11},{10,... | collective-permute-start | bytes 26120 | tf_op jit(solution)/shard_map/ppermute | solution.py:42
  4.6 2.5 %collective-permute-start = (f32[1,17,1,128]{3,2,1,0:T(1,128)S(1)}, f32[1,17,1,128]{3,2,1,0:T(1,128)S(1)}, u32[]{:S(2)}, u32[]{:S(2)}) collective-permute-start(f32[1,17,1,128]{3,2,1,0:T(1,128)S(1)} %broadcast_in_dim_broadcast_in_dim.3), channel_id=1, source_target_pairs={{0,1},{1,2},{2,3},{3,0},{4,5},{5,6},{6,7},{7,4},{8,9},{9,10},{10,1... | collective-permute-start | bytes 26120 | tf_op jit(solution)/shard_map/ppermute | solution.py:42
  7.2 4.4 %collective-permute-start.3 = (f32[4,17,1,128]{3,2,1,0:T(1,128)S(1)}, f32[4,17,1,128]{3,2,1,0:T(1,128)S(1)}, u32[]{:S(2)}, u32[]{:S(2)}) collective-permute-start(f32[4,17,1,128]{3,2,1,0:T(1,128)S(1)} %get-tuple-element.75), channel_id=1, source_target_pairs={{0,4},{1,5},{2,6},{3,7},{4,8},{5,9},{6,10},{7,11},{8,12},{9,13},{1... | collective-permute-start | bytes 104456 | tf_op jit(solution)/shard_map/ppermute | solution.py:42
  8.6 5.9 %collective-permute-start.5 = (f32[4,17,1,128]{3,2,1,0:T(1,128)S(1)}, f32[4,17,1,128]{3,2,1,0:T(1,128)S(1)}, u32[]{:S(2)}, u32[]{:S(2)}) collective-permute-start(f32[4,17,1,128]{3,2,1,0:T(1,128)S(1)} %get-tuple-element.75), channel_id=1, source_target_pairs={{0,12},{1,13},{2,14},{3,15},{4,0},{5,1},{6,2},{7,3},{8,4},{9,5},{1... | collective-permute-start | bytes 104456 | tf_op jit(solution)/shard_map/ppermute | solution.py:42
  10.1 4.4 %collective-permute-start.4 = (f32[4,17,1,128]{3,2,1,0:T(1,128)S(1)}, f32[4,17,1,128]{3,2,1,0:T(1,128)S(1)}, u32[]{:S(2)}, u32[]{:S(2)}) collective-permute-start(f32[4,17,1,128]{3,2,1,0:T(1,128)S(1)} %get-tuple-element.75), channel_id=1, source_target_pairs={{0,8},{1,9},{2,10},{3,11},{4,12},{5,13},{6,14},{7,15},{8,0},{9,1},... | collective-permute-start | bytes 104456 | tf_op jit(solution)/shard_map/ppermute | solution.py:42
  14.6 5.2 %collective-permute-start.6 = (f32[16,17,1,128]{3,2,1,0:T(1,128)S(1)}, f32[16,17,1,128]{3,2,1,0:T(1,128)S(1)}, u32[]{:S(2)}, u32[]{:S(2)}) collective-permute-start(f32[16,17,1,128]{3,2,1,0:T(1,128)S(1)} %get-tuple-element.65), channel_id=1, source_target_pairs={{0,32},{1,33},{2,34},{3,35},{4,36},{5,37},{6,38},{7,39},{8,40},{9,... | collective-permute-start | bytes 417800 | tf_op jit(solution)/shard_map/ppermute | solution.py:42
  16.8 5.6 %collective-permute-start.7 = (f32[16,17,1,128]{3,2,1,0:T(1,128)S(1)}, f32[16,17,1,128]{3,2,1,0:T(1,128)S(1)}, u32[]{:S(2)}, u32[]{:S(2)}) collective-permute-start(f32[16,17,1,128]{3,2,1,0:T(1,128)S(1)} %get-tuple-element.65), channel_id=1, source_target_pairs={{0,64},{1,65},{2,66},{3,67},{4,68},{5,69},{6,70},{7,71},{8,72},{9,... | collective-permute-start | bytes 417800 | tf_op jit(solution)/shard_map/ppermute | solution.py:42
  17.7 5.7 %collective-permute-start.8 = (f32[16,17,1,128]{3,2,1,0:T(1,128)S(1)}, f32[16,17,1,128]{3,2,1,0:T(1,128)S(1)}, u32[]{:S(2)}, u32[]{:S(2)}) collective-permute-start(f32[16,17,1,128]{3,2,1,0:T(1,128)S(1)} %get-tuple-element.65), channel_id=1, source_target_pairs={{0,96},{1,97},{2,98},{3,99},{4,100},{5,101},{6,102},{7,103},{8,104... | collective-permute-start | bytes 417800 | tf_op jit(solution)/shard_map/ppermute | solution.py:42
  23.6 7.2 %collective-permute-start.9 = (f32[64,17,1,128]{3,2,1,0:T(1,128)S(1)}, f32[64,17,1,128]{3,2,1,0:T(1,128)S(1)}, u32[]{:S(2)}, u32[]{:S(2)}) collective-permute-start(f32[64,17,1,128]{3,2,1,0:T(1,128)S(1)} %get-tuple-element.57), channel_id=1, source_target_pairs={{0,16},{1,17},{2,18},{3,19},{4,20},{5,21},{6,22},{7,23},{8,24},{9,... | collective-permute-start | bytes 1671176 | tf_op jit(solution)/shard_map/ppermute | solution.py:42
  85.5 35.1 %collective-permute-start.13 = (f32[1024,128]{1,0:T(8,128)S(1)}, f32[1024,128]{1,0:T(8,128)S(1)}, u32[]{:S(2)}, u32[]{:S(2)}) collective-permute-start(f32[1024,128]{1,0:T(8,128)S(1)} %get-tuple-element.45.rest_0_), channel_id=1, source_target_pairs={{0,16},{1,17},{2,18},{3,19},{4,20},{5,21},{6,22},{7,23},{8,24},{9,... | collective-permute-start | bytes 1572872 | tf_op jit(solution)/shard_map/ppermute | solution.py:42
  86.0 23.2 %collective-permute-start.12 = (f32[1024,128]{1,0:T(8,128)S(1)}, f32[1024,128]{1,0:T(8,128)S(1)}, u32[]{:S(2)}, u32[]{:S(2)}) collective-permute-start(f32[1024,128]{1,0:T(8,128)S(1)} %get-tuple-element.45.rest_0_), channel_id=1, source_target_pairs={{0,96},{1,97},{2,98},{3,99},{4,100},{5,101},{6,102},{7,103},{8,104... | collective-permute-start | bytes 1572872 | tf_op jit(solution)/shard_map/ppermute | solution.py:42
  86.6 24.6 %collective-permute-start.11 = (f32[1024,128]{1,0:T(8,128)S(1)}, f32[1024,128]{1,0:T(8,128)S(1)}, u32[]{:S(2)}, u32[]{:S(2)}) collective-permute-start(f32[1024,128]{1,0:T(8,128)S(1)} %get-tuple-element.45.rest_0_), channel_id=1, source_target_pairs={{0,64},{1,65},{2,66},{3,67},{4,68},{5,69},{6,70},{7,71},{8,72},{9,... | collective-permute-start | bytes 1572872 | tf_op jit(solution)/shard_map/ppermute | solution.py:42
  88.0 24.1 %collective-permute-start.10 = (f32[1024,128]{1,0:T(8,128)S(1)}, f32[1024,128]{1,0:T(8,128)S(1)}, u32[]{:S(2)}, u32[]{:S(2)}) collective-permute-start(f32[1024,128]{1,0:T(8,128)S(1)} %get-tuple-element.45.rest_0_), channel_id=1, source_target_pairs={{0,32},{1,33},{2,34},{3,35},{4,36},{5,37},{6,38},{7,39},{8,40},{9,... | collective-permute-start | bytes 1572872 | tf_op jit(solution)/shard_map/ppermute | solution.py:42
  112.1 8.5 %collective-permute-start.14 = (f32[1024,128]{1,0:T(8,128)S(1)}, f32[1024,128]{1,0:T(8,128)S(1)}, u32[]{:S(2)}, u32[]{:S(2)}) collective-permute-start(f32[1024,128]{1,0:T(8,128)S(1)} %collective-permute-done.10.rest_1_), channel_id=1, source_target_pairs={{0,16},{1,17},{2,18},{3,19},{4,20},{5,21},{6,22},{7,23},{8,24},{9,... | collective-permute-start | bytes 1572872 | tf_op jit(solution)/shard_map/ppermute | solution.py:42
  113.4 7.2 %collective-permute-start.15 = (f32[1024,128]{1,0:T(8,128)S(1)}, f32[1024,128]{1,0:T(8,128)S(1)}, u32[]{:S(2)}, u32[]{:S(2)}) collective-permute-start(f32[1024,128]{1,0:T(8,128)S(1)} %collective-permute-done.11.rest_2_), channel_id=1, source_target_pairs={{0,16},{1,17},{2,18},{3,19},{4,20},{5,21},{6,22},{7,23},{8,24},{9,... | collective-permute-start | bytes 1572872 | tf_op jit(solution)/shard_map/ppermute | solution.py:42
  113.4 7.3 %collective-permute-start.16 = (f32[1024,128]{1,0:T(8,128)S(1)}, f32[1024,128]{1,0:T(8,128)S(1)}, u32[]{:S(2)}, u32[]{:S(2)}) collective-permute-start(f32[1024,128]{1,0:T(8,128)S(1)} %collective-permute-done.12.rest_3_), channel_id=1, source_target_pairs={{0,16},{1,17},{2,18},{3,19},{4,20},{5,21},{6,22},{7,23},{8,24},{9,... | collective-permute-start | bytes 1572872 | tf_op jit(solution)/shard_map/ppermute | solution.py:42

commit v6 on v5

--- a/solution.py
+++ b/solution.py
@@ -45,12 +45,12 @@
 def gather_shards(shard):
     rows, cols = lax.axis_size("row"), lax.axis_size("col")
     held = shard[None]
-    for axis in (3, 2, 0):
-        moved = [held]
-        for k in range(1, 4):
-            move = lambda *at, k=k: [part + k * (i == axis) for i, part in enumerate(at)]
-            moved.append(send(held, move, rows, cols))
-        held = jnp.concatenate(moved, 0)
+    for axis in (3, 0):
+        for bit in (1, 2):
+            move = lambda *at: [part ^ (bit * (i == axis)) for i, part in enumerate(at)]
+            held = jnp.concatenate([held, send(held, move, rows, cols)], 0)
+    moved = [held] + [send(held, lambda y, c, x, z, k=k: (y, c, x + k, z), rows, cols) for k in range(1, 4)]
+    held = jnp.concatenate(moved, 0)
     return jnp.concatenate([held, send(held, lambda y, c, x, z: (y, c + 1, x, z), rows, cols)], 0)
 
 
@@ -235,19 +235,16 @@
         state[rows, pl.ds(pl.multiple_of(LEAD + here, BASE), BASE)] = eye
         work[...] = state[rows, pl.ds(here, BASE)]
         eliminate_base(work, spread, solved, lines)
-        l0, l1, l2 = split3(jnp.where(row >= lane, work[...], 0.0))
+        l0, l1 = split(jnp.where(row >= lane, work[...], 0.0))
         window = pl.ds(here, WINDOW)
 
         def load(values):
-            first, second, third = split3(values)
+            first, second = split(values)
             stack[0:128, :] = first
             stack[128:256, :] = second
-            stack[256:384, :] = third
-            stack[384:512, :] = first
 
         load(both([state[rows, window], side[rows, :]], 1))
-        two = dot(both([both([l0, l0], 1), both([l1, l1], 1)], 0), stack[0:256, :])
-        done = two[:BASE] + (two[BASE:] + dot(both([l0, l2], 1), stack[256:512, :]))
+        done = dot(both([l0, l0], 1), stack[...]) + dot(l1, stack[0:128, :])
         state[rows, window] = done[:, :WINDOW]
         side[rows, :] = done[:, WINDOW:]
         load(done)
@@ -255,7 +252,7 @@
         @pl.loop(0, blocks - 1 - k)
         def _(i):
             there = pl.multiple_of((i + 1) * BASE, BASE)
-            parts = split3(jnp.transpose(state[rows, pl.ds(pl.multiple_of(here + there, BASE), BASE)]))
+            parts = split(jnp.transpose(state[rows, pl.ds(pl.multiple_of(here + there, BASE), BASE)]))
             for n, part in enumerate(parts):
                 tall[pl.ds(pl.multiple_of(i * BASE, BASE), BASE), n * 128 : n * 128 + 128] = part
 
@@ -264,10 +261,8 @@
             def _():
                 skip = pair * 256
                 below = pl.ds(pl.multiple_of(here + BASE + skip, BASE), 256)
-                t0, t1, t2 = [tall[skip : skip + 256, n * 128 : n * 128 + 128] for n in range(3)]
-                update = dot(both([t0, t0], 1), stack[0:256, skip:])
-                update += dot(both([t1, t1], 1), stack[0:256, skip:])
-                update += dot(both([t0, t2], 1), stack[256:512, skip:])
+                t0, t1 = [tall[skip : skip + 256, n * 128 : n * 128 + 128] for n in range(2)]
+                update = dot(both([t0, t0], 1), stack[:, skip:]) + dot(t1, stack[0:128, skip:])
                 width = WINDOW - skip
                 into = pl.ds(pl.multiple_of(here + skip, BASE), width)
                 state[below, into] = state[below, into] - update[:, :width]
@@ -304,9 +299,8 @@
         y_ref[out * 256 : out * 256 + 256, :] = total
 
 
-def panel_kernel(base, info, u_ref, v_ref, wr_ref, wc_ref, *refs):
-    ah_ref, al_ref = refs[-2:]
-    slot, chunk = base + pl.program_id(0), pl.program_id(1)
+def panel_kernel(info, u_ref, v_ref, wr_ref, wc_ref, ah_ref, al_ref):
+    slot, chunk = pl.program_id(0), pl.program_id(1)
     start = pl.multiple_of(chunk * CHUNK, CHUNK)
     kinds = [info[3 + slot * 2], info[4 + slot * 2]]
     needed = lambda kind: (kind != ZERO) & (kind != FACTOR)
@@ -319,37 +313,11 @@
             ah_ref[:, cols], al_ref[:, cols] = split(values)
 
 
-CHUNK = 256
-ZERO, UPDATE, DIAGONAL, PANEL, FACTOR = range(5)
-
-
-def final_kernel(info, u_ref, v_ref, wr_ref, wc_ref, f_ref, *rest):
-    parts, (ah, al, out_ref, yh, yl) = rest[:8], rest[8:]
+def own_kernel(info, u_ref, v_ref, wr_ref, wc_ref, own_ref):
     slot, chunk = pl.program_id(0), pl.program_id(1)
     start = pl.multiple_of(chunk * CHUNK, CHUNK)
-    kinds = [info[3 + slot * 2], info[4 + slot * 2]]
-
-    @pl.when((slot == 0) & (chunk == 0))
-    def _():
-        for p, part in enumerate(parts):
-            source = info[12 + p]
-            lanes = pl.ds(pl.multiple_of(source % 4 * 128, 128), 128)
-            yh[source // 4, :, lanes], yl[source // 4, :, lanes] = split(part[...])
-
-    def store(j, values):
-        for q in range(TILE // 128):
-            out_ref[pl.ds(j * 4 + q, CHUNK, stride=8), :] = values[:, q * 128 : (q + 1) * 128]
-
     for j in range(2):
-        kind = kinds[j]
-
-        @pl.when(kind == ZERO)
-        def _():
-            store(j, jnp.zeros((CHUNK, TILE), F32))
-
-        @pl.when(kind == PANEL)
-        def _():
-            store(j, -dot3(ah[...], al[...], yh[j], yl[j]))
+        kind = info[3 + slot * 2 + j]
 
         @pl.when((kind == UPDATE) | (kind == DIAGONAL))
         def _():
@@ -358,6 +326,44 @@
             col = lax.broadcasted_iota(jnp.int32, (CHUNK, TILE), 1)
             shift = wr_ref[0, pl.ds(start, CHUNK), 4:5]
             values = values + jnp.where((row == col) & (kind == DIAGONAL), shift, 0.0)
+            own_ref[:, j * TILE : j * TILE + TILE] = values
+
+
+CHUNK = 256
+ZERO, UPDATE, DIAGONAL, PANEL, FACTOR = range(5)
+
+
+def final_kernel(info, f_ref, *rest):
+    parts, (ah, al, own, out_ref, yh, yl) = rest[:8], rest[8:]
+    slot, chunk = pl.program_id(0), pl.program_id(1)
+    start = pl.multiple_of(chunk * CHUNK, CHUNK)
+    kinds = [info[3 + slot * 2], info[4 + slot * 2]]
+
+    @pl.when((slot == 0) & (chunk == 0))
+    def _():
+        for p, part in enumerate(parts):
+            source = info[12 + p]
+            lanes = pl.ds(pl.multiple_of(source % 4 * 128, 128), 128)
+            yh[source // 4, :, lanes], yl[source // 4, :, lanes] = split(part[...])
+
+    def store(j, values):
+        for q in range(TILE // 128):
+            out_ref[pl.ds(j * 4 + q, CHUNK, stride=8), :] = values[:, q * 128 : (q + 1) * 128]
+
+    for j in range(2):
+        kind = kinds[j]
+
+        @pl.when(kind == ZERO)
+        def _():
+            store(j, jnp.zeros((CHUNK, TILE), F32))
+
+        @pl.when(kind == PANEL)
+        def _():
+            store(j, -dot3(ah[...], al[...], yh[j], yl[j]))
+
+        @pl.when((kind == UPDATE) | (kind == DIAGONAL))
+        def _():
+            values = own[:, j * TILE : j * TILE + TILE]
             store(j, values - dot3(ah[...], al[...], yh[j], yl[j]))
 
         if j == 0:
@@ -384,11 +390,11 @@
     clusters = jnp.arange(cluster_rank.shape[0], dtype=jnp.int32)
     found = jnp.sum(jnp.where(cluster_rank[None, :] == wanted[:, None], clusters[None, :], 0), axis=1)
     from_row, from_x = found // 4, found % 4
-    dy = (row // 2 - from_row // 2) % 4
+    dy = (row // 2) ^ (from_row // 2)
     dc = (row % 2 - from_row % 2) % 2
     dx = (col // 4 - from_x) % 4
-    dz = (col % 4 - slots) % 4
-    where = ((((dc * 4 + dy) * 4 + dx) * 4)[:, None] + dz[None, :]).reshape(-1).astype(jnp.int32)
+    dz = (col % 4) ^ slots
+    where = ((((dc * 4 + dx) * 4 + dy) * 4)[:, None] + dz[None, :]).reshape(-1).astype(jnp.int32)
 
     u, v, wr, wc = pl.pallas_call(
         prep_kernel,
@@ -459,8 +465,8 @@
                 pltpu.VMEM((STEP, STEP, BASE), F32),
                 pltpu.VMEM((STEP, STEP, BASE), F32),
                 pltpu.VMEM((STEP, BASE), F32),
-                pltpu.VMEM((4 * BASE, WINDOW + BASE), BF16),
-                pltpu.VMEM((LEAD, 3 * BASE), BF16),
+                pltpu.VMEM((2 * BASE, WINDOW + BASE), BF16),
+                pltpu.VMEM((LEAD, 2 * BASE), BF16),
             ],
         ),
         out_shape=[jax.ShapeDtypeStruct((TILE, TILE), F32), jax.ShapeDtypeStruct((LEAD, BASE), F32)],
@@ -471,31 +477,32 @@
     tall = jax.ShapeDtypeStruct((4 * TILE, LEAD), BF16)
     chunks = TILE // CHUNK
 
-    def panel(base, count, held):
-        blocked = pl.BlockSpec((CHUNK, LEAD), lambda i, h, info: ((base + i) * chunks + h, 0))
+    blocked = pl.BlockSpec((CHUNK, LEAD), lambda i, h, info: (i * chunks + h, 0))
+
+    def assembled(kernel, right, shapes, tiles, name):
         return pl.pallas_call(
-            functools.partial(panel_kernel, base),
+            kernel,
             grid_spec=pltpu.PrefetchScalarGridSpec(
                 num_scalar_prefetch=1,
-                grid=(count, chunks),
-                in_specs=geometry(lambda i, h, info: 2 + base + i, 0, 1)
-                + [pl.BlockSpec(memory_space=pl.ANY)] * len(held),
-                out_specs=[blocked] * 2,
+                grid=(4, chunks),
+                in_specs=geometry(lambda i, h, info: 2 + i, right, 1),
+                out_specs=[blocked] * len(shapes),
             ),
-            out_shape=[tall] * 2,
-            input_output_aliases={5 + i: i for i in range(len(held))},
+            out_shape=shapes,
             cost_estimate=pl.CostEstimate(
-                flops=count * 15_000_000_000, bytes_accessed=count * 4_000_000, transcendentals=count * 8_000_000
+                flops=tiles * 7_500_000_000, bytes_accessed=tiles * 2_000_000, transcendentals=tiles * 4_000_000
             ),
-            name=f"panel{base}",
+            name=name,
             compiler_params=pltpu.CompilerParams(vmem_limit_bytes=20 << 20),
-        )(info, u, v, wr, wc, *held)
+        )(info, u, v, wr, wc)
 
     near = [send(weights_part, lambda y, c, x, z, k=k: (y + k, c, x, z), rows, cols) for k in range(1, 4)]
-    *near, ah, al = lax.optimization_barrier((*near, *panel(0, 3, [])))
+    panels = assembled(panel_kernel, 0, [tall] * 2, 8, "panel")
+    *near, ah, al = lax.optimization_barrier((*near, *panels))
     parts = [weights_part] + near
     parts = parts + [send(part, lambda y, c, x, z: (y, c + 1, x, z), rows, cols) for part in parts]
-    *parts, ah, al = lax.optimization_barrier((*parts, *panel(3, 1, [ah, al])))
+    own = assembled(own_kernel, 3, [jax.ShapeDtypeStruct((4 * TILE, LEAD), F32)], 6, "own")
+    *parts, own = lax.optimization_barrier((*parts, *own))
 
     lines = CHUNK * 8
     out = pl.pallas_call(
@@ -503,16 +510,14 @@
         grid_spec=pltpu.PrefetchScalarGridSpec(
             num_scalar_prefetch=1,
             grid=(4, chunks),
-            in_specs=geometry(lambda i, h, info: 2 + i, 3, 1)
-            + whole(9)
-            + [pl.BlockSpec((CHUNK, LEAD), lambda i, h, info: (i * chunks + h, 0))] * 2,
+            in_specs=whole(9) + [blocked] * 3,
             out_specs=pl.BlockSpec((lines, 128), lambda i, h, info: (i * chunks + h, 0)),
             scratch_shapes=[pltpu.VMEM((2, LEAD, TILE), BF16)] * 2,
         ),
         out_shape=jax.ShapeDtypeStruct((4 * TILE * 8, 128), F32),
         name="final",
         compiler_params=pltpu.CompilerParams(vmem_limit_bytes=24 << 20),
-    )(info, u, v, wr, wc, factor, *parts, ah, al)
+    )(info, factor, *parts, ah, al, own)
     return out.reshape(4, 1, TILE, 2, 1, TILE)
 
 

time: 152 us -> 151 us (level)
  starting transfers between devices: 23.7 us -> 21.8 us
    pallas_call x2, Pallas kernels: 25.8 us -> 43.8 us  [assembled(): pl.pallas_call(kernel, grid_spec=pltpu.PrefetchScalarGridSpec(num_scalar_...]
    pallas_call x1, Pallas kernels: 30.8 us -> 15.7 us  [shards(): pl.pallas_call(final_kernel, grid_spec=pltpu.PrefetchScalarGridSpec(num_s...]
    pallas_call x1, Pallas kernels: 50.8 us -> 47.4 us  [shards(): pl.pallas_call(chain_kernel, grid_spec=pltpu.PrefetchScalarGridSpec(num_s...]
    ppermute x17 -> x15, starting transfers between devices: 23.7 us -> 21.8 us  [send(): return lax.ppermute(value, ('row', 'col'), pairs)]
    ppermute x17 -> x15, waiting for transfers between devices: 12.8 us -> 14.3 us  [send(): return lax.ppermute(value, ('row', 'col'), pairs)]
  transfers between devices with their start and end apart: 17 -> 15, of which waited for: 7 -> 7; matrix products, arithmetic and copies ran while one was open for 1% -> 1% of each run, Pallas kernels for 17% -> 29%
where the time goes in v6:
time: 151 us
  Pallas kernels  111 us (74%)
  starting transfers between devices  21.8 us (14%)
  waiting for transfers between devices  14.3 us (9%)
  other arithmetic  1.94 us (1%)
  local copies, waits for them, and re-layouts  1.81 us (1%)
    pallas_call x1, Pallas kernels, shards(): pl.pallas_call(chain_kernel, grid_spec=pltpu.PrefetchScalarGridSpec(num_s...  47.4 us
    pallas_call x2, Pallas kernels, assembled(): pl.pallas_call(kernel, grid_spec=pltpu.PrefetchScalarGridSpec(num_scalar_...  43.8 us
    ppermute x15, starting transfers between devices, send(): return lax.ppermute(value, ('row', 'col'), pairs)  21.8 us
    pallas_call x1, Pallas kernels, shards(): pl.pallas_call(final_kernel, grid_spec=pltpu.PrefetchScalarGridSpec(num_s...  15.7 us
    ppermute x15, waiting for transfers between devices, send(): return lax.ppermute(value, ('row', 'col'), pairs)  14.3 us
    pallas_call x1, Pallas kernels, shards(): pl.pallas_call(prep_kernel, grid_spec=pltpu.PrefetchScalarGridSpec(num_sc...  3.88 us
  transfers between devices with their start and end apart: 15, of which 7 were waited for; matrix products, arithmetic and copies ran while one was open for 1% of the time, Pallas kernels for 29%

profile of v6, /device:TPU:73, one launch (start us, length us, event | category | flops | bytes accessed | tf_op | source)
XLA Modules:
  0.0 150.8 jit_solution(2207879873870205973)
XLA Ops:
  0.0 0.7 reshape.129
  0.7 0.7 pad_maximum_fusion.3
  1.4 1.4 collective-permute-start
  2.9 0.1 select_select_fusion
  3.0 0.1 pad_add_fusion
  3.0 1.0 collective-permute-done
  4.0 0.1 collective-permute-start.1
  4.1 4.1 %collective-permute-done.1 = f32[2,17,1,128]{3,2,1,0:T(1,128)S(1)} collective-permute-done((f32[2,17,1,128]{3,2,1,0:T(1,128)S(1)}, f32[2,17,1,128]{3,2,1,0:T(1,128)S(1)}, u32[]{:S(2)}, u32[]{:S(2)}) %collective-permute-start.1) | collective-permute-done | bytes 17440 | tf_op jit(solution)/shard_map/ppermute | solution.py:42
  8.2 0.2 collective-permute-start.2
  8.5 2.6 %collective-permute-done.2 = f32[4,17,1,128]{3,2,1,0:T(1,128)S(1)} collective-permute-done((f32[4,17,1,128]{3,2,1,0:T(1,128)S(1)}, f32[4,17,1,128]{3,2,1,0:T(1,128)S(1)}, u32[]{:S(2)}, u32[]{:S(2)}) %collective-permute-start.2) | collective-permute-done | bytes 34848 | tf_op jit(solution)/shard_map/ppermute | solution.py:42
  11.1 0.1 pad_maximum_fusion
  11.2 2.1 %collective-permute-start.3 = (f32[8,17,1,128]{3,2,1,0:T(1,128)S(1)}, f32[8,17,1,128]{3,2,1,0:T(1,128)S(1)}, u32[]{:S(2)}, u32[]{:S(2)}) collective-permute-start(f32[8,17,1,128]{3,2,1,0:T(1,128)S(1)} %pad_maximum_fusion), channel_id=1, source_target_pairs={{0,64},{1,65},{2,66},{3,67},{4,68},{5,69},{6,70},{7,71},{8,72},{9,... | collective-permute-start | bytes 208904 | tf_op jit(solution)/shard_map/ppermute | solution.py:42
  13.3 0.1 constant_dynamic-update-slice_fusion.9
  13.3 3.0 %collective-permute-done.3 = f32[8,17,1,128]{3,2,1,0:T(1,128)S(1)} collective-permute-done((f32[8,17,1,128]{3,2,1,0:T(1,128)S(1)}, f32[8,17,1,128]{3,2,1,0:T(1,128)S(1)}, u32[]{:S(2)}, u32[]{:S(2)}) %collective-permute-start.3) | collective-permute-done | bytes 69664 | tf_op jit(solution)/shard_map/ppermute | solution.py:42
  16.3 0.1 constant_dynamic-update-slice_fusion.8
  16.4 1.3 collective-permute-start.4
  17.7 0.8 select_reduce_fusion
  18.6 2.5 %collective-permute-start.5 = (f32[16,17,1,128]{3,2,1,0:T(1,128)S(1)}, f32[16,17,1,128]{3,2,1,0:T(1,128)S(1)}, u32[]{:S(2)}, u32[]{:S(2)}) collective-permute-start(f32[16,17,1,128]{3,2,1,0:T(1,128)S(1)} %get-tuple-element.59), channel_id=1, source_target_pairs={{0,8},{1,9},{2,10},{3,11},{4,12},{5,13},{6,14},{7,15},{8,0},{9,1},... | collective-permute-start | bytes 417800 | tf_op jit(solution)/shard_map/ppermute | solution.py:42
  21.1 0.1 select_n.136
  21.2 1.2 collective-permute-start.6
  22.3 0.0 collective-permute-done.4
  22.3 0.2 constant_dynamic-update-slice_fusion.7
  22.5 1.6 %collective-permute-done.5 = f32[16,17,1,128]{3,2,1,0:T(1,128)S(1)} collective-permute-done((f32[16,17,1,128]{3,2,1,0:T(1,128)S(1)}, f32[16,17,1,128]{3,2,1,0:T(1,128)S(1)}, u32[]{:S(2)}, u32[]{:S(2)}) %collective-permute-start.5) | collective-permute-done | bytes 139296 | tf_op jit(solution)/shard_map/ppermute | solution.py:42
  24.1 0.2 constant_dynamic-update-slice_fusion.6
  24.3 0.8 collective-permute-done.6
  25.1 0.2 constant_dynamic-update-slice_fusion.5
  25.3 6.9 %collective-permute-start.7 = (f32[64,17,1,128]{3,2,1,0:T(1,128)S(1)}, f32[64,17,1,128]{3,2,1,0:T(1,128)S(1)}, u32[]{:S(2)}, u32[]{:S(2)}) collective-permute-start(f32[64,17,1,128]{3,2,1,0:T(1,128)S(1)} %get-tuple-element.51), channel_id=1, source_target_pairs={{0,16},{1,17},{2,18},{3,19},{4,20},{5,21},{6,22},{7,23},{8,24},{9,... | collective-permute-start | bytes 1671176 | tf_op jit(solution)/shard_map/ppermute | solution.py:42
  32.2 0.1 broadcast_add_fusion
  32.2 0.1 add.152.where_ref
  32.3 0.1 concatenate.32.info
  32.4 1.3 collective-permute-done.7
  33.7 0.1 constant_dynamic-update-slice_fusion.13.g_ref
  33.8 3.9 %prep.1 = (bf16[8,4,512,48]{3,2,1,0:T(8,128)(2,1)S(1)}, bf16[8,4,48,512]{3,2,1,0:T(8,128)(2,1)S(1)}, f32[8,512,128]{2,1,0:T(8,128)S(1)}, f32[8,8,512]{2,1,0:T(8,128)S(1)}) custom-call(s32[32]{0:T(128)S(1)} %add.152.where_ref, f32[128,17,1,128]{3,2,1,0:T(1,128)S(1)} %constant_dynamic-update-slice_fusion.13.g_ref), custom_call_target="tpu_custom_call" | custom-call | tf_op jit(solution)/shard_map/prep/pallas_call | solution.py:399
  37.7 47.4 %chain.1 = (f32[512,512]{1,0:T(8,128)S(1)}, f32[1024,128]{1,0:T(8,128)S(1)}) custom-call(s32[20]{0:T(128)S(1)} %concatenate.32.info, bf16[8,4,512,48]{3,2,1,0:T(8,128)(2,1)S(1)} %get-tuple-element.27.u_ref, bf16[8,4,48,512]{3,2,1,0:T(8,128)(2,1)S(1)} %get-tuple-element.28.v_ref.vj_ref, f32[8,512,128]{2,1,0:T(8,128)S(1)} %get-tuple-element.29.wr_ref, ...), custom_call_target="tpu_custom_call" | custom-call | tf_op jit(solution)/shard_map/chain/pallas_call | solution.py:447
  85.1 0.5 collective-permute-start.11
  85.5 0.2 collective-permute-start.10
  85.7 2.6 %collective-permute-start.9 = (f32[1024,128]{1,0:T(8,128)S(1)}, f32[1024,128]{1,0:T(8,128)S(1)}, u32[]{:S(2)}, u32[]{:S(2)}) collective-permute-start(f32[1024,128]{1,0:T(8,128)S(1)} %get-tuple-element.38.rest_0_), channel_id=1, source_target_pairs={{0,64},{1,65},{2,66},{3,67},{4,68},{5,69},{6,70},{7,71},{8,72},{9,... | collective-permute-start | bytes 1572872 | tf_op jit(solution)/shard_map/ppermute | solution.py:42
  88.4 1.2 collective-permute-start.8
  89.6 25.2 %panel.1 = (bf16[2048,1024]{1,0:T(8,128)(2,1)S(1)}, bf16[2048,1024]{1,0:T(8,128)(2,1)S(1)}) custom-call(s32[20]{0:T(128)S(1)} %concatenate.32.info, bf16[8,4,512,48]{3,2,1,0:T(8,128)(2,1)S(1)} %get-tuple-element.27.u_ref, bf16[8,4,48,512]{3,2,1,0:T(8,128)(2,1)S(1)} %get-tuple-element.28.v_ref.vj_ref, f32[8,512,128]{2,1,0:T(8,128)S(1)} %get-tuple-element.29.wr_ref, ...), custom_call_target="tpu_custom_call" | custom-call | flops 60000002048 | bytes 16000000 | tf_op jit(solution)/shard_map/panel/pallas_call | solution.py:483
  114.9 0.0 collective-permute-done.10.rest_3_
  114.9 0.0 collective-permute-done.9.rest_2_
  114.9 0.0 collective-permute-done.8.rest_1_
  114.9 1.0 collective-permute-start.12
  115.9 0.1 collective-permute-start.13
  116.0 0.4 collective-permute-start.14
  116.4 18.6 %own.1.rest_10_ = f32[2048,1024]{1,0:T(8,128)S(1)} custom-call(s32[20]{0:T(128)S(1)} %concatenate.32.info, bf16[8,4,512,48]{3,2,1,0:T(8,128)(2,1)S(1)} %get-tuple-element.27.u_ref, bf16[8,4,48,512]{3,2,1,0:T(8,128)(2,1)S(1)} %get-tuple-element.28.v_ref.vj_ref, f32[8,512,128]{2,1,0:T(8,128)S(1)} %get-tuple-element.29.wr_ref, ...), custom_call_target="tpu_custom_call" | custom-call | flops 44999999488 | bytes 12000000 | tf_op jit(solution)/shard_map/own/pallas_call | solution.py:483
  135.0 0.0 collective-permute-done.11.rest_4_
  135.1 0.0 collective-permute-done.12.rest_5_
  135.1 0.0 collective-permute-done.13.rest_6_
  135.1 0.0 collective-permute-done.14.rest_7_
  135.1 15.7 %final.1 = f32[16384,128]{1,0:T(8,128)} custom-call(s32[20]{0:T(128)S(1)} %concatenate.32.info, f32[512,512]{1,0:T(8,128)S(1)} %get-tuple-element.31.f_ref, f32[1024,128]{1,0:T(8,128)S(1)} %get-tuple-element.38.rest_0_, f32[1024,128]{1,0:T(8,128)S(1)} %collective-permute-done.8.rest_1_, f32[1024,128]{1,0:T(8,128)S(1)} %collective-permute-done.9.rest_2_, ...), custom_call_target="tpu_custom_call" | custom-call | tf_op jit(solution)/shard_map/final/pallas_call | solution.py:508
  (12 shorter events, 0.2 us)
Async XLA Ops:
  1.4 2.6 %collective-permute-start = (f32[1,17,1,128]{3,2,1,0:T(1,128)S(1)}, f32[1,17,1,128]{3,2,1,0:T(1,128)S(1)}, u32[]{:S(2)}, u32[]{:S(2)}) collective-permute-start(f32[1,17,1,128]{3,2,1,0:T(1,128)S(1)} %broadcast_in_dim_broadcast_in_dim.3), channel_id=1, source_target_pairs={{0,1},{1,0},{2,3},{3,2},{4,5},{5,4},{6,7},{7,6},{8,9},{9,8},{10,11... | collective-permute-start | bytes 26120 | tf_op jit(solution)/shard_map/ppermute | solution.py:42
  4.0 4.2 %collective-permute-start.1 = (f32[2,17,1,128]{3,2,1,0:T(1,128)S(1)}, f32[2,17,1,128]{3,2,1,0:T(1,128)S(1)}, u32[]{:S(2)}, u32[]{:S(2)}) collective-permute-start(f32[2,17,1,128]{3,2,1,0:T(1,128)S(1)} %pad_maximum_fusion.2), channel_id=1, source_target_pairs={{0,2},{1,3},{2,0},{3,1},{4,6},{5,7},{6,4},{7,5},{8,10},{9,11},{10,... | collective-permute-start | bytes 52232 | tf_op jit(solution)/shard_map/ppermute | solution.py:42
  8.2 2.9 %collective-permute-start.2 = (f32[4,17,1,128]{3,2,1,0:T(1,128)S(1)}, f32[4,17,1,128]{3,2,1,0:T(1,128)S(1)}, u32[]{:S(2)}, u32[]{:S(2)}) collective-permute-start(f32[4,17,1,128]{3,2,1,0:T(1,128)S(1)} %pad_maximum_fusion.1), channel_id=1, source_target_pairs={{0,32},{1,33},{2,34},{3,35},{4,36},{5,37},{6,38},{7,39},{8,40},{9,... | collective-permute-start | bytes 104456 | tf_op jit(solution)/shard_map/ppermute | solution.py:42
  11.2 5.1 %collective-permute-start.3 = (f32[8,17,1,128]{3,2,1,0:T(1,128)S(1)}, f32[8,17,1,128]{3,2,1,0:T(1,128)S(1)}, u32[]{:S(2)}, u32[]{:S(2)}) collective-permute-start(f32[8,17,1,128]{3,2,1,0:T(1,128)S(1)} %pad_maximum_fusion), channel_id=1, source_target_pairs={{0,64},{1,65},{2,66},{3,67},{4,68},{5,69},{6,70},{7,71},{8,72},{9,... | collective-permute-start | bytes 208904 | tf_op jit(solution)/shard_map/ppermute | solution.py:42
  16.4 5.9 %collective-permute-start.4 = (f32[16,17,1,128]{3,2,1,0:T(1,128)S(1)}, f32[16,17,1,128]{3,2,1,0:T(1,128)S(1)}, u32[]{:S(2)}, u32[]{:S(2)}) collective-permute-start(f32[16,17,1,128]{3,2,1,0:T(1,128)S(1)} %get-tuple-element.59), channel_id=1, source_target_pairs={{0,4},{1,5},{2,6},{3,7},{4,8},{5,9},{6,10},{7,11},{8,12},{9,13},{1... | collective-permute-start | bytes 417800 | tf_op jit(solution)/shard_map/ppermute | solution.py:42
  18.6 5.5 %collective-permute-start.5 = (f32[16,17,1,128]{3,2,1,0:T(1,128)S(1)}, f32[16,17,1,128]{3,2,1,0:T(1,128)S(1)}, u32[]{:S(2)}, u32[]{:S(2)}) collective-permute-start(f32[16,17,1,128]{3,2,1,0:T(1,128)S(1)} %get-tuple-element.59), channel_id=1, source_target_pairs={{0,8},{1,9},{2,10},{3,11},{4,12},{5,13},{6,14},{7,15},{8,0},{9,1},... | collective-permute-start | bytes 417800 | tf_op jit(solution)/shard_map/ppermute | solution.py:42
  21.2 3.9 %collective-permute-start.6 = (f32[16,17,1,128]{3,2,1,0:T(1,128)S(1)}, f32[16,17,1,128]{3,2,1,0:T(1,128)S(1)}, u32[]{:S(2)}, u32[]{:S(2)}) collective-permute-start(f32[16,17,1,128]{3,2,1,0:T(1,128)S(1)} %get-tuple-element.59), channel_id=1, source_target_pairs={{0,12},{1,13},{2,14},{3,15},{4,0},{5,1},{6,2},{7,3},{8,4},{9,5},{1... | collective-permute-start | bytes 417800 | tf_op jit(solution)/shard_map/ppermute | solution.py:42
  25.3 8.5 %collective-permute-start.7 = (f32[64,17,1,128]{3,2,1,0:T(1,128)S(1)}, f32[64,17,1,128]{3,2,1,0:T(1,128)S(1)}, u32[]{:S(2)}, u32[]{:S(2)}) collective-permute-start(f32[64,17,1,128]{3,2,1,0:T(1,128)S(1)} %get-tuple-element.51), channel_id=1, source_target_pairs={{0,16},{1,17},{2,18},{3,19},{4,20},{5,21},{6,22},{7,23},{8,24},{9,... | collective-permute-start | bytes 1671176 | tf_op jit(solution)/shard_map/ppermute | solution.py:42
  85.1 50.0 %collective-permute-start.11 = (f32[1024,128]{1,0:T(8,128)S(1)}, f32[1024,128]{1,0:T(8,128)S(1)}, u32[]{:S(2)}, u32[]{:S(2)}) collective-permute-start(f32[1024,128]{1,0:T(8,128)S(1)} %get-tuple-element.38.rest_0_), channel_id=1, source_target_pairs={{0,16},{1,17},{2,18},{3,19},{4,20},{5,21},{6,22},{7,23},{8,24},{9,... | collective-permute-start | bytes 1572872 | tf_op jit(solution)/shard_map/ppermute | solution.py:42
  85.5 29.3 %collective-permute-start.10 = (f32[1024,128]{1,0:T(8,128)S(1)}, f32[1024,128]{1,0:T(8,128)S(1)}, u32[]{:S(2)}, u32[]{:S(2)}) collective-permute-start(f32[1024,128]{1,0:T(8,128)S(1)} %get-tuple-element.38.rest_0_), channel_id=1, source_target_pairs={{0,96},{1,97},{2,98},{3,99},{4,100},{5,101},{6,102},{7,103},{8,104... | collective-permute-start | bytes 1572872 | tf_op jit(solution)/shard_map/ppermute | solution.py:42
  85.7 29.1 %collective-permute-start.9 = (f32[1024,128]{1,0:T(8,128)S(1)}, f32[1024,128]{1,0:T(8,128)S(1)}, u32[]{:S(2)}, u32[]{:S(2)}) collective-permute-start(f32[1024,128]{1,0:T(8,128)S(1)} %get-tuple-element.38.rest_0_), channel_id=1, source_target_pairs={{0,64},{1,65},{2,66},{3,67},{4,68},{5,69},{6,70},{7,71},{8,72},{9,... | collective-permute-start | bytes 1572872 | tf_op jit(solution)/shard_map/ppermute | solution.py:42
  88.4 26.5 %collective-permute-start.8 = (f32[1024,128]{1,0:T(8,128)S(1)}, f32[1024,128]{1,0:T(8,128)S(1)}, u32[]{:S(2)}, u32[]{:S(2)}) collective-permute-start(f32[1024,128]{1,0:T(8,128)S(1)} %get-tuple-element.38.rest_0_), channel_id=1, source_target_pairs={{0,32},{1,33},{2,34},{3,35},{4,36},{5,37},{6,38},{7,39},{8,40},{9,... | collective-permute-start | bytes 1572872 | tf_op jit(solution)/shard_map/ppermute | solution.py:42
  114.9 20.2 %collective-permute-start.12 = (f32[1024,128]{1,0:T(8,128)S(1)}, f32[1024,128]{1,0:T(8,128)S(1)}, u32[]{:S(2)}, u32[]{:S(2)}) collective-permute-start(f32[1024,128]{1,0:T(8,128)S(1)} %collective-permute-done.8.rest_1_), channel_id=1, source_target_pairs={{0,16},{1,17},{2,18},{3,19},{4,20},{5,21},{6,22},{7,23},{8,24},{9,... | collective-permute-start | bytes 1572872 | tf_op jit(solution)/shard_map/ppermute | solution.py:42
  115.9 19.1 %collective-permute-start.13 = (f32[1024,128]{1,0:T(8,128)S(1)}, f32[1024,128]{1,0:T(8,128)S(1)}, u32[]{:S(2)}, u32[]{:S(2)}) collective-permute-start(f32[1024,128]{1,0:T(8,128)S(1)} %collective-permute-done.9.rest_2_), channel_id=1, source_target_pairs={{0,16},{1,17},{2,18},{3,19},{4,20},{5,21},{6,22},{7,23},{8,24},{9,... | collective-permute-start | bytes 1572872 | tf_op jit(solution)/shard_map/ppermute | solution.py:42
  116.0 19.1 %collective-permute-start.14 = (f32[1024,128]{1,0:T(8,128)S(1)}, f32[1024,128]{1,0:T(8,128)S(1)}, u32[]{:S(2)}, u32[]{:S(2)}) collective-permute-start(f32[1024,128]{1,0:T(8,128)S(1)} %collective-permute-done.10.rest_3_), channel_id=1, source_target_pairs={{0,16},{1,17},{2,18},{3,19},{4,20},{5,21},{6,22},{7,23},{8,24},{9,... | collective-permute-start | bytes 1572872 | tf_op jit(solution)/shard_map/ppermute | solution.py:42

commit v7 on v6

--- a/solution.py
+++ b/solution.py
@@ -45,12 +45,12 @@
 def gather_shards(shard):
     rows, cols = lax.axis_size("row"), lax.axis_size("col")
     held = shard[None]
-    for axis in (3, 0):
-        for bit in (1, 2):
-            move = lambda *at: [part ^ (bit * (i == axis)) for i, part in enumerate(at)]
-            held = jnp.concatenate([held, send(held, move, rows, cols)], 0)
-    moved = [held] + [send(held, lambda y, c, x, z, k=k: (y, c, x + k, z), rows, cols) for k in range(1, 4)]
-    held = jnp.concatenate(moved, 0)
+    for axis in (3, 2, 0):
+        moved = [held]
+        for k in range(1, 4):
+            move = lambda *at, k=k: [part + k * (i == axis) for i, part in enumerate(at)]
+            moved.append(send(held, move, rows, cols))
+        held = jnp.concatenate(moved, 0)
     return jnp.concatenate([held, send(held, lambda y, c, x, z: (y, c + 1, x, z), rows, cols)], 0)
 
 
@@ -129,7 +129,7 @@
     return lax.dot_general(left, right, (((0,), (0,)), ((), ())), preferred_element_type=F32)
 
 
-def eliminate_base(work, spread, solved, lines):
+def eliminate_base(work, spread, solved, lines, raw):
     lane = lax.broadcasted_iota(jnp.int32, (8, BASE), 1)
     sub = lax.broadcasted_iota(jnp.int32, (8, BASE), 0)
     repeat = lambda ref, i: ref[pl.ds(i, 8, stride=0), :]
@@ -153,8 +153,12 @@
             d.append(diagonal)
             spread[0, 8 * half : 8 * half + 8, :] = diagonal
         pivot = repeat(spread.at[0], 0)
+        raw[0] = c[0][0]
         for j in range(STEP):
             scale = lax.rsqrt(pivot)
+            if j + 1 < STEP:
+                below = repeat(raw.at[j], (j + 1) % 8)
+                pivot = repeat(spread.at[j], j + 1) - (below * below) * (scale * scale)
             first = j // 8
             line = repeat(lines, j) * scale
             for half in range(first, HALVES):
@@ -165,10 +169,10 @@
                     spread[j + 1, 8 * half : 8 * half + 8, :] = d[half]
             for k in range(j + 1, STEP):
                 factor = repeat(solved.at[j], k)
-                if k == j + 1:
-                    pivot = repeat(spread.at[j], k) - factor * factor
                 for half in range(k // 8, HALVES):
                     c[half][k] = c[half][k] - c[half][j] * factor
+                if k == j + 1 and k + 1 < STEP:
+                    raw[k] = c[(k + 1) // 8][k]
             for half in range(first, HALVES):
                 update = a[half] - c[half][j] * line
                 if half == first:
@@ -190,7 +194,7 @@
 def chain_kernel(
     info, u_ref, v_ref, wr_ref, wc_ref, vj_ref, wj_ref,
     f_ref, y_ref,
-    state, side, work, spread, solved, lines, stack, tall,
+    state, side, work, spread, solved, lines, raw, stack, tall,
 ):
     state[:, LEAD:] = jnp.zeros((LEAD + BASE, LEAD), F32)
     state[LEAD:, :LEAD] = jnp.zeros((BASE, LEAD), F32)
@@ -234,7 +238,7 @@
         rows = pl.ds(here, BASE)
         state[rows, pl.ds(pl.multiple_of(LEAD + here, BASE), BASE)] = eye
         work[...] = state[rows, pl.ds(here, BASE)]
-        eliminate_base(work, spread, solved, lines)
+        eliminate_base(work, spread, solved, lines, raw)
         l0, l1 = split(jnp.where(row >= lane, work[...], 0.0))
         window = pl.ds(here, WINDOW)
 
@@ -390,11 +394,11 @@
     clusters = jnp.arange(cluster_rank.shape[0], dtype=jnp.int32)
     found = jnp.sum(jnp.where(cluster_rank[None, :] == wanted[:, None], clusters[None, :], 0), axis=1)
     from_row, from_x = found // 4, found % 4
-    dy = (row // 2) ^ (from_row // 2)
+    dy = (row // 2 - from_row // 2) % 4
     dc = (row % 2 - from_row % 2) % 2
     dx = (col // 4 - from_x) % 4
-    dz = (col % 4) ^ slots
-    where = ((((dc * 4 + dx) * 4 + dy) * 4)[:, None] + dz[None, :]).reshape(-1).astype(jnp.int32)
+    dz = (col % 4 - slots) % 4
+    where = ((((dc * 4 + dy) * 4 + dx) * 4)[:, None] + dz[None, :]).reshape(-1).astype(jnp.int32)
 
     u, v, wr, wc = pl.pallas_call(
         prep_kernel,
@@ -465,6 +469,7 @@
                 pltpu.VMEM((STEP, STEP, BASE), F32),
                 pltpu.VMEM((STEP, STEP, BASE), F32),
                 pltpu.VMEM((STEP, BASE), F32),
+                pltpu.VMEM((STEP, 8, BASE), F32),
                 pltpu.VMEM((2 * BASE, WINDOW + BASE), BF16),
                 pltpu.VMEM((LEAD, 2 * BASE), BF16),
             ],

time: 151 us -> 147 us (0.974)
  waiting for transfers between devices: 14.3 us -> 9.8 us
  starting transfers between devices: 21.8 us -> 23.5 us
    ppermute x15 -> x17, waiting for transfers between devices: 14.3 us -> 9.8 us  [send(): return lax.ppermute(value, ('row', 'col'), pairs)]
    ppermute x15 -> x17, starting transfers between devices: 21.8 us -> 23.5 us  [send(): return lax.ppermute(value, ('row', 'col'), pairs)]
  transfers between devices with their start and end apart: 15 -> 17, of which waited for: 7 -> 5; matrix products, arithmetic and copies ran while one was open for 1% -> 1% of each run, Pallas kernels for 29% -> 30%
where the time goes in v7:
time: 147 us
  Pallas kernels  110 us (75%)
  starting transfers between devices  23.5 us (16%)
  waiting for transfers between devices  9.8 us (7%)
  local copies, waits for them, and re-layouts  1.84 us (1%)
  other arithmetic  1.83 us (1%)
    pallas_call x1, Pallas kernels, shards(): pl.pallas_call(chain_kernel, grid_spec=pltpu.PrefetchScalarGridSpec(num_s...  46.5 us
    pallas_call x2, Pallas kernels, assembled(): pl.pallas_call(kernel, grid_spec=pltpu.PrefetchScalarGridSpec(num_scalar_...  43.8 us
    ppermute x17, starting transfers between devices, send(): return lax.ppermute(value, ('row', 'col'), pairs)  23.5 us
    pallas_call x1, Pallas kernels, shards(): pl.pallas_call(final_kernel, grid_spec=pltpu.PrefetchScalarGridSpec(num_s...  15.7 us
    ppermute x17, waiting for transfers between devices, send(): return lax.ppermute(value, ('row', 'col'), pairs)  9.8 us
    pallas_call x1, Pallas kernels, shards(): pl.pallas_call(prep_kernel, grid_spec=pltpu.PrefetchScalarGridSpec(num_sc...  3.88 us
  transfers between devices with their start and end apart: 17, of which 5 were waited for; matrix products, arithmetic and copies ran while one was open for 1% of the time, Pallas kernels for 30%

profile of v7, /device:TPU:73, one launch (start us, length us, event | category | flops | bytes accessed | tf_op | source)
XLA Modules:
  0.0 146.9 jit_solution(7344267256283210137)
XLA Ops:
  0.0 0.7 reshape.151
  0.7 0.7 pad_maximum_fusion
  1.4 0.1 collective-permute-start.2
  1.5 3.1 %collective-permute-start.1 = (f32[1,17,1,128]{3,2,1,0:T(1,128)S(1)}, f32[1,17,1,128]{3,2,1,0:T(1,128)S(1)}, u32[]{:S(2)}, u32[]{:S(2)}) collective-permute-start(f32[1,17,1,128]{3,2,1,0:T(1,128)S(1)} %broadcast_in_dim_broadcast_in_dim.3), channel_id=1, source_target_pairs={{0,2},{1,3},{2,0},{3,1},{4,6},{5,7},{6,4},{7,5},{8,10},{9,11},{10,... | collective-permute-start | bytes 26120 | tf_op jit(solution)/shard_map/ppermute | solution.py:42
  4.6 0.0 collective-permute-start
  4.6 0.1 select_select_fusion
  4.7 2.4 %collective-permute-done = f32[1,17,1,128]{3,2,1,0:T(1,128)S(1)} collective-permute-done((f32[1,17,1,128]{3,2,1,0:T(1,128)S(1)}, f32[1,17,1,128]{3,2,1,0:T(1,128)S(1)}, u32[]{:S(2)}, u32[]{:S(2)}) %collective-permute-start) | collective-permute-done | bytes 8736 | tf_op jit(solution)/shard_map/ppermute | solution.py:42
  7.2 0.0 collective-permute-done.1
  7.2 0.0 collective-permute-done.2
  7.2 1.3 collective-permute-start.3
  8.5 0.1 pad_add_fusion
  8.6 1.5 %collective-permute-start.5 = (f32[4,17,1,128]{3,2,1,0:T(1,128)S(1)}, f32[4,17,1,128]{3,2,1,0:T(1,128)S(1)}, u32[]{:S(2)}, u32[]{:S(2)}) collective-permute-start(f32[4,17,1,128]{3,2,1,0:T(1,128)S(1)} %get-tuple-element.69), channel_id=1, source_target_pairs={{0,12},{1,13},{2,14},{3,15},{4,0},{5,1},{6,2},{7,3},{8,4},{9,5},{1... | collective-permute-start | bytes 104456 | tf_op jit(solution)/shard_map/ppermute | solution.py:42
  10.1 1.5 %collective-permute-start.4 = (f32[4,17,1,128]{3,2,1,0:T(1,128)S(1)}, f32[4,17,1,128]{3,2,1,0:T(1,128)S(1)}, u32[]{:S(2)}, u32[]{:S(2)}) collective-permute-start(f32[4,17,1,128]{3,2,1,0:T(1,128)S(1)} %get-tuple-element.69), channel_id=1, source_target_pairs={{0,8},{1,9},{2,10},{3,11},{4,12},{5,13},{6,14},{7,15},{8,0},{9,1},... | collective-permute-start | bytes 104456 | tf_op jit(solution)/shard_map/ppermute | solution.py:42
  11.6 0.0 collective-permute-done.3
  11.6 0.1 constant_dynamic-update-slice_fusion.16
  11.7 2.8 %collective-permute-done.4 = f32[4,17,1,128]{3,2,1,0:T(1,128)S(1)} collective-permute-done((f32[4,17,1,128]{3,2,1,0:T(1,128)S(1)}, f32[4,17,1,128]{3,2,1,0:T(1,128)S(1)}, u32[]{:S(2)}, u32[]{:S(2)}) %collective-permute-start.4) | collective-permute-done | bytes 34848 | tf_op jit(solution)/shard_map/ppermute | solution.py:42
  14.5 0.1 constant_dynamic-update-slice_fusion.15
  14.5 0.0 collective-permute-done.5
  14.5 0.1 constant_dynamic-update-slice_fusion.14
  14.6 1.4 collective-permute-start.6
  16.0 0.8 select_reduce_fusion
  16.8 0.8 collective-permute-start.7
  17.6 0.1 select_n.154
  17.7 2.1 %collective-permute-start.8 = (f32[16,17,1,128]{3,2,1,0:T(1,128)S(1)}, f32[16,17,1,128]{3,2,1,0:T(1,128)S(1)}, u32[]{:S(2)}, u32[]{:S(2)}) collective-permute-start(f32[16,17,1,128]{3,2,1,0:T(1,128)S(1)} %get-tuple-element.59), channel_id=1, source_target_pairs={{0,96},{1,97},{2,98},{3,99},{4,100},{5,101},{6,102},{7,103},{8,104... | collective-permute-start | bytes 417800 | tf_op jit(solution)/shard_map/ppermute | solution.py:42
  19.8 0.0 collective-permute-done.6
  19.8 0.2 constant_dynamic-update-slice_fusion.13
  20.0 2.4 %collective-permute-done.7 = f32[16,17,1,128]{3,2,1,0:T(1,128)S(1)} collective-permute-done((f32[16,17,1,128]{3,2,1,0:T(1,128)S(1)}, f32[16,17,1,128]{3,2,1,0:T(1,128)S(1)}, u32[]{:S(2)}, u32[]{:S(2)}) %collective-permute-start.7) | collective-permute-done | bytes 139296 | tf_op jit(solution)/shard_map/ppermute | solution.py:42
  22.4 0.2 constant_dynamic-update-slice_fusion.12
  22.6 0.9 collective-permute-done.8
  23.4 0.2 constant_dynamic-update-slice_fusion.11
  23.6 5.6 %collective-permute-start.9 = (f32[64,17,1,128]{3,2,1,0:T(1,128)S(1)}, f32[64,17,1,128]{3,2,1,0:T(1,128)S(1)}, u32[]{:S(2)}, u32[]{:S(2)}) collective-permute-start(f32[64,17,1,128]{3,2,1,0:T(1,128)S(1)} %get-tuple-element.51), channel_id=1, source_target_pairs={{0,16},{1,17},{2,18},{3,19},{4,20},{5,21},{6,22},{7,23},{8,24},{9,... | collective-permute-start | bytes 1671176 | tf_op jit(solution)/shard_map/ppermute | solution.py:42
  29.2 0.1 broadcast_add_fusion
  29.3 0.1 add.172.where_ref
  29.4 0.1 concatenate.24.info
  29.5 1.3 collective-permute-done.9
  30.8 0.1 constant_dynamic-update-slice_fusion.21.g_ref
  30.9 3.9 %prep.1 = (bf16[8,4,512,48]{3,2,1,0:T(8,128)(2,1)S(1)}, bf16[8,4,48,512]{3,2,1,0:T(8,128)(2,1)S(1)}, f32[8,512,128]{2,1,0:T(8,128)S(1)}, f32[8,8,512]{2,1,0:T(8,128)S(1)}) custom-call(s32[32]{0:T(128)S(1)} %add.172.where_ref, f32[128,17,1,128]{3,2,1,0:T(1,128)S(1)} %constant_dynamic-update-slice_fusion.21.g_ref), custom_call_target="tpu_custom_call" | custom-call | tf_op jit(solution)/shard_map/prep/pallas_call | solution.py:403
  34.8 46.5 %chain.1 = (f32[512,512]{1,0:T(8,128)S(1)}, f32[1024,128]{1,0:T(8,128)S(1)}) custom-call(s32[20]{0:T(128)S(1)} %concatenate.24.info, bf16[8,4,512,48]{3,2,1,0:T(8,128)(2,1)S(1)} %get-tuple-element.27.u_ref, bf16[8,4,48,512]{3,2,1,0:T(8,128)(2,1)S(1)} %get-tuple-element.28.v_ref.vj_ref, f32[8,512,128]{2,1,0:T(8,128)S(1)} %get-tuple-element.29.wr_ref, ...), custom_call_target="tpu_custom_call" | custom-call | tf_op jit(solution)/shard_map/chain/pallas_call | solution.py:451
  81.2 0.5 collective-permute-start.13
  81.7 0.6 collective-permute-start.12
  82.3 1.4 collective-permute-start.11
  83.7 2.1 %collective-permute-start.10 = (f32[1024,128]{1,0:T(8,128)S(1)}, f32[1024,128]{1,0:T(8,128)S(1)}, u32[]{:S(2)}, u32[]{:S(2)}) collective-permute-start(f32[1024,128]{1,0:T(8,128)S(1)} %get-tuple-element.38.rest_0_), channel_id=1, source_target_pairs={{0,32},{1,33},{2,34},{3,35},{4,36},{5,37},{6,38},{7,39},{8,40},{9,... | collective-permute-start | bytes 1572872 | tf_op jit(solution)/shard_map/ppermute | solution.py:42
  85.8 25.2 %panel.1 = (bf16[2048,1024]{1,0:T(8,128)(2,1)S(1)}, bf16[2048,1024]{1,0:T(8,128)(2,1)S(1)}) custom-call(s32[20]{0:T(128)S(1)} %concatenate.24.info, bf16[8,4,512,48]{3,2,1,0:T(8,128)(2,1)S(1)} %get-tuple-element.27.u_ref, bf16[8,4,48,512]{3,2,1,0:T(8,128)(2,1)S(1)} %get-tuple-element.28.v_ref.vj_ref, f32[8,512,128]{2,1,0:T(8,128)S(1)} %get-tuple-element.29.wr_ref, ...), custom_call_target="tpu_custom_call" | custom-call | flops 60000002048 | bytes 16000000 | tf_op jit(solution)/shard_map/panel/pallas_call | solution.py:488
  111.0 0.0 collective-permute-done.12.rest_3_
  111.0 0.0 collective-permute-done.11.rest_2_
  111.0 0.0 collective-permute-done.10.rest_1_
  111.0 1.1 collective-permute-start.14
  112.1 0.1 collective-permute-start.15
  112.2 0.4 collective-permute-start.16
  112.6 18.6 %own.1.rest_10_ = f32[2048,1024]{1,0:T(8,128)S(1)} custom-call(s32[20]{0:T(128)S(1)} %concatenate.24.info, bf16[8,4,512,48]{3,2,1,0:T(8,128)(2,1)S(1)} %get-tuple-element.27.u_ref, bf16[8,4,48,512]{3,2,1,0:T(8,128)(2,1)S(1)} %get-tuple-element.28.v_ref.vj_ref, f32[8,512,128]{2,1,0:T(8,128)S(1)} %get-tuple-element.29.wr_ref, ...), custom_call_target="tpu_custom_call" | custom-call | flops 44999999488 | bytes 12000000 | tf_op jit(solution)/shard_map/own/pallas_call | solution.py:488
  131.2 0.0 collective-permute-done.13.rest_4_
  131.2 0.0 collective-permute-done.14.rest_5_
  131.2 0.0 collective-permute-done.15.rest_6_
  131.3 0.0 collective-permute-done.16.rest_7_
  131.3 15.7 %final.1 = f32[16384,128]{1,0:T(8,128)} custom-call(s32[20]{0:T(128)S(1)} %concatenate.24.info, f32[512,512]{1,0:T(8,128)S(1)} %get-tuple-element.31.f_ref, f32[1024,128]{1,0:T(8,128)S(1)} %get-tuple-element.38.rest_0_, f32[1024,128]{1,0:T(8,128)S(1)} %collective-permute-done.10.rest_1_, f32[1024,128]{1,0:T(8,128)S(1)} %collective-permute-done.11.rest_2_, ...), custom_call_target="tpu_custom_call" | custom-call | tf_op jit(solution)/shard_map/final/pallas_call | solution.py:513
  (11 shorter events, 0.2 us)
Async XLA Ops:
  1.4 5.8 %collective-permute-start.2 = (f32[1,17,1,128]{3,2,1,0:T(1,128)S(1)}, f32[1,17,1,128]{3,2,1,0:T(1,128)S(1)}, u32[]{:S(2)}, u32[]{:S(2)}) collective-permute-start(f32[1,17,1,128]{3,2,1,0:T(1,128)S(1)} %broadcast_in_dim_broadcast_in_dim.3), channel_id=1, source_target_pairs={{0,3},{1,0},{2,1},{3,2},{4,7},{5,4},{6,5},{7,6},{8,11},{9,8},{10,9... | collective-permute-start | bytes 26120 | tf_op jit(solution)/shard_map/ppermute | solution.py:42
  1.5 5.7 %collective-permute-start.1 = (f32[1,17,1,128]{3,2,1,0:T(1,128)S(1)}, f32[1,17,1,128]{3,2,1,0:T(1,128)S(1)}, u32[]{:S(2)}, u32[]{:S(2)}) collective-permute-start(f32[1,17,1,128]{3,2,1,0:T(1,128)S(1)} %broadcast_in_dim_broadcast_in_dim.3), channel_id=1, source_target_pairs={{0,2},{1,3},{2,0},{3,1},{4,6},{5,7},{6,4},{7,5},{8,10},{9,11},{10,... | collective-permute-start | bytes 26120 | tf_op jit(solution)/shard_map/ppermute | solution.py:42
  4.6 2.5 %collective-permute-start = (f32[1,17,1,128]{3,2,1,0:T(1,128)S(1)}, f32[1,17,1,128]{3,2,1,0:T(1,128)S(1)}, u32[]{:S(2)}, u32[]{:S(2)}) collective-permute-start(f32[1,17,1,128]{3,2,1,0:T(1,128)S(1)} %broadcast_in_dim_broadcast_in_dim.3), channel_id=1, source_target_pairs={{0,1},{1,2},{2,3},{3,0},{4,5},{5,6},{6,7},{7,4},{8,9},{9,10},{10,1... | collective-permute-start | bytes 26120 | tf_op jit(solution)/shard_map/ppermute | solution.py:42
  7.2 4.4 %collective-permute-start.3 = (f32[4,17,1,128]{3,2,1,0:T(1,128)S(1)}, f32[4,17,1,128]{3,2,1,0:T(1,128)S(1)}, u32[]{:S(2)}, u32[]{:S(2)}) collective-permute-start(f32[4,17,1,128]{3,2,1,0:T(1,128)S(1)} %get-tuple-element.69), channel_id=1, source_target_pairs={{0,4},{1,5},{2,6},{3,7},{4,8},{5,9},{6,10},{7,11},{8,12},{9,13},{1... | collective-permute-start | bytes 104456 | tf_op jit(solution)/shard_map/ppermute | solution.py:42
  8.6 5.9 %collective-permute-start.5 = (f32[4,17,1,128]{3,2,1,0:T(1,128)S(1)}, f32[4,17,1,128]{3,2,1,0:T(1,128)S(1)}, u32[]{:S(2)}, u32[]{:S(2)}) collective-permute-start(f32[4,17,1,128]{3,2,1,0:T(1,128)S(1)} %get-tuple-element.69), channel_id=1, source_target_pairs={{0,12},{1,13},{2,14},{3,15},{4,0},{5,1},{6,2},{7,3},{8,4},{9,5},{1... | collective-permute-start | bytes 104456 | tf_op jit(solution)/shard_map/ppermute | solution.py:42
  10.1 4.4 %collective-permute-start.4 = (f32[4,17,1,128]{3,2,1,0:T(1,128)S(1)}, f32[4,17,1,128]{3,2,1,0:T(1,128)S(1)}, u32[]{:S(2)}, u32[]{:S(2)}) collective-permute-start(f32[4,17,1,128]{3,2,1,0:T(1,128)S(1)} %get-tuple-element.69), channel_id=1, source_target_pairs={{0,8},{1,9},{2,10},{3,11},{4,12},{5,13},{6,14},{7,15},{8,0},{9,1},... | collective-permute-start | bytes 104456 | tf_op jit(solution)/shard_map/ppermute | solution.py:42
  14.6 5.2 %collective-permute-start.6 = (f32[16,17,1,128]{3,2,1,0:T(1,128)S(1)}, f32[16,17,1,128]{3,2,1,0:T(1,128)S(1)}, u32[]{:S(2)}, u32[]{:S(2)}) collective-permute-start(f32[16,17,1,128]{3,2,1,0:T(1,128)S(1)} %get-tuple-element.59), channel_id=1, source_target_pairs={{0,32},{1,33},{2,34},{3,35},{4,36},{5,37},{6,38},{7,39},{8,40},{9,... | collective-permute-start | bytes 417800 | tf_op jit(solution)/shard_map/ppermute | solution.py:42
  16.8 5.6 %collective-permute-start.7 = (f32[16,17,1,128]{3,2,1,0:T(1,128)S(1)}, f32[16,17,1,128]{3,2,1,0:T(1,128)S(1)}, u32[]{:S(2)}, u32[]{:S(2)}) collective-permute-start(f32[16,17,1,128]{3,2,1,0:T(1,128)S(1)} %get-tuple-element.59), channel_id=1, source_target_pairs={{0,64},{1,65},{2,66},{3,67},{4,68},{5,69},{6,70},{7,71},{8,72},{9,... | collective-permute-start | bytes 417800 | tf_op jit(solution)/shard_map/ppermute | solution.py:42
  17.7 5.7 %collective-permute-start.8 = (f32[16,17,1,128]{3,2,1,0:T(1,128)S(1)}, f32[16,17,1,128]{3,2,1,0:T(1,128)S(1)}, u32[]{:S(2)}, u32[]{:S(2)}) collective-permute-start(f32[16,17,1,128]{3,2,1,0:T(1,128)S(1)} %get-tuple-element.59), channel_id=1, source_target_pairs={{0,96},{1,97},{2,98},{3,99},{4,100},{5,101},{6,102},{7,103},{8,104... | collective-permute-start | bytes 417800 | tf_op jit(solution)/shard_map/ppermute | solution.py:42
  23.6 7.2 %collective-permute-start.9 = (f32[64,17,1,128]{3,2,1,0:T(1,128)S(1)}, f32[64,17,1,128]{3,2,1,0:T(1,128)S(1)}, u32[]{:S(2)}, u32[]{:S(2)}) collective-permute-start(f32[64,17,1,128]{3,2,1,0:T(1,128)S(1)} %get-tuple-element.51), channel_id=1, source_target_pairs={{0,16},{1,17},{2,18},{3,19},{4,20},{5,21},{6,22},{7,23},{8,24},{9,... | collective-permute-start | bytes 1671176 | tf_op jit(solution)/shard_map/ppermute | solution.py:42
  81.2 50.0 %collective-permute-start.13 = (f32[1024,128]{1,0:T(8,128)S(1)}, f32[1024,128]{1,0:T(8,128)S(1)}, u32[]{:S(2)}, u32[]{:S(2)}) collective-permute-start(f32[1024,128]{1,0:T(8,128)S(1)} %get-tuple-element.38.rest_0_), channel_id=1, source_target_pairs={{0,16},{1,17},{2,18},{3,19},{4,20},{5,21},{6,22},{7,23},{8,24},{9,... | collective-permute-start | bytes 1572872 | tf_op jit(solution)/shard_map/ppermute | solution.py:42
  81.7 29.3 %collective-permute-start.12 = (f32[1024,128]{1,0:T(8,128)S(1)}, f32[1024,128]{1,0:T(8,128)S(1)}, u32[]{:S(2)}, u32[]{:S(2)}) collective-permute-start(f32[1024,128]{1,0:T(8,128)S(1)} %get-tuple-element.38.rest_0_), channel_id=1, source_target_pairs={{0,96},{1,97},{2,98},{3,99},{4,100},{5,101},{6,102},{7,103},{8,104... | collective-permute-start | bytes 1572872 | tf_op jit(solution)/shard_map/ppermute | solution.py:42
  82.3 28.7 %collective-permute-start.11 = (f32[1024,128]{1,0:T(8,128)S(1)}, f32[1024,128]{1,0:T(8,128)S(1)}, u32[]{:S(2)}, u32[]{:S(2)}) collective-permute-start(f32[1024,128]{1,0:T(8,128)S(1)} %get-tuple-element.38.rest_0_), channel_id=1, source_target_pairs={{0,64},{1,65},{2,66},{3,67},{4,68},{5,69},{6,70},{7,71},{8,72},{9,... | collective-permute-start | bytes 1572872 | tf_op jit(solution)/shard_map/ppermute | solution.py:42
  83.7 27.3 %collective-permute-start.10 = (f32[1024,128]{1,0:T(8,128)S(1)}, f32[1024,128]{1,0:T(8,128)S(1)}, u32[]{:S(2)}, u32[]{:S(2)}) collective-permute-start(f32[1024,128]{1,0:T(8,128)S(1)} %get-tuple-element.38.rest_0_), channel_id=1, source_target_pairs={{0,32},{1,33},{2,34},{3,35},{4,36},{5,37},{6,38},{7,39},{8,40},{9,... | collective-permute-start | bytes 1572872 | tf_op jit(solution)/shard_map/ppermute | solution.py:42
  111.0 20.2 %collective-permute-start.14 = (f32[1024,128]{1,0:T(8,128)S(1)}, f32[1024,128]{1,0:T(8,128)S(1)}, u32[]{:S(2)}, u32[]{:S(2)}) collective-permute-start(f32[1024,128]{1,0:T(8,128)S(1)} %collective-permute-done.10.rest_1_), channel_id=1, source_target_pairs={{0,16},{1,17},{2,18},{3,19},{4,20},{5,21},{6,22},{7,23},{8,24},{9,... | collective-permute-start | bytes 1572872 | tf_op jit(solution)/shard_map/ppermute | solution.py:42
  112.1 19.1 %collective-permute-start.15 = (f32[1024,128]{1,0:T(8,128)S(1)}, f32[1024,128]{1,0:T(8,128)S(1)}, u32[]{:S(2)}, u32[]{:S(2)}) collective-permute-start(f32[1024,128]{1,0:T(8,128)S(1)} %collective-permute-done.11.rest_2_), channel_id=1, source_target_pairs={{0,16},{1,17},{2,18},{3,19},{4,20},{5,21},{6,22},{7,23},{8,24},{9,... | collective-permute-start | bytes 1572872 | tf_op jit(solution)/shard_map/ppermute | solution.py:42
  112.2 19.1 %collective-permute-start.16 = (f32[1024,128]{1,0:T(8,128)S(1)}, f32[1024,128]{1,0:T(8,128)S(1)}, u32[]{:S(2)}, u32[]{:S(2)}) collective-permute-start(f32[1024,128]{1,0:T(8,128)S(1)} %collective-permute-done.12.rest_3_), channel_id=1, source_target_pairs={{0,16},{1,17},{2,18},{3,19},{4,20},{5,21},{6,22},{7,23},{8,24},{9,... | collective-permute-start | bytes 1572872 | tf_op jit(solution)/shard_map/ppermute | solution.py:42

commit v8 on v7

--- a/solution.py
+++ b/solution.py
@@ -44,13 +44,10 @@
 
 def gather_shards(shard):
     rows, cols = lax.axis_size("row"), lax.axis_size("col")
-    held = shard[None]
-    for axis in (3, 2, 0):
-        moved = [held]
-        for k in range(1, 4):
-            move = lambda *at, k=k: [part + k * (i == axis) for i, part in enumerate(at)]
-            moved.append(send(held, move, rows, cols))
-        held = jnp.concatenate(moved, 0)
+    copies = jnp.broadcast_to(shard[None], (cols, *shard.shape))
+    held = lax.all_to_all(copies, "col", 0, 0, tiled=True)
+    moved = [held] + [send(held, lambda y, c, x, z, k=k: (y + k, c, x, z), rows, cols) for k in range(1, 4)]
+    held = jnp.concatenate(moved, 0)
     return jnp.concatenate([held, send(held, lambda y, c, x, z: (y, c + 1, x, z), rows, cols)], 0)
 
 
@@ -396,9 +393,8 @@
     from_row, from_x = found // 4, found % 4
     dy = (row // 2 - from_row // 2) % 4
     dc = (row % 2 - from_row % 2) % 2
-    dx = (col // 4 - from_x) % 4
-    dz = (col % 4 - slots) % 4
-    where = ((((dc * 4 + dy) * 4 + dx) * 4)[:, None] + dz[None, :]).reshape(-1).astype(jnp.int32)
+    first = (dc * 4 + dy) * cols + from_x * 4
+    where = (first[:, None] + slots[None, :]).reshape(-1).astype(jnp.int32)
 
     u, v, wr, wc = pl.pallas_call(
         prep_kernel,

time: 147 us -> 146 us (level); the launches traced: 147 us -> 144 us
  starting transfers between devices: 23.5 us -> 20.1 us
    ppermute x17 -> x11, starting transfers between devices: 23.5 us -> 13.2 us  [send(): return lax.ppermute(value, ('row', 'col'), pairs)]
    all_to_all x0 -> x1, starting transfers between devices: none -> 6.88 us  [gather_shards(): held = lax.all_to_all(copies, 'col', 0, 0, tiled=True)]
    ppermute x17 -> x11, waiting for transfers between devices: 9.8 us -> 5.05 us  [send(): return lax.ppermute(value, ('row', 'col'), pairs)]
    all_to_all x0 -> x1, waiting for transfers between devices: none -> 4.21 us  [gather_shards(): held = lax.all_to_all(copies, 'col', 0, 0, tiled=True)]
  transfers between devices with their start and end apart: 17 -> 12, of which waited for: 5 -> 4; matrix products, arithmetic and copies ran while one was open for 1% -> 1% of each run, Pallas kernels for 30% -> 30%
where the time goes in v8:
time: 146 us; the launch traced here: 144 us
  Pallas kernels  110 us (75%)
  starting transfers between devices  20.1 us (14%)
  waiting for transfers between devices  9.26 us (6%)
  other arithmetic  2.3 us (2%)
  local copies, waits for them, and re-layouts  1.87 us (1%)
    pallas_call x1, Pallas kernels, shards(): pl.pallas_call(chain_kernel, grid_spec=pltpu.PrefetchScalarGridSpec(num_s...  46.7 us
    pallas_call x2, Pallas kernels, assembled(): pl.pallas_call(kernel, grid_spec=pltpu.PrefetchScalarGridSpec(num_scalar_...  43.8 us
    pallas_call x1, Pallas kernels, shards(): pl.pallas_call(final_kernel, grid_spec=pltpu.PrefetchScalarGridSpec(num_s...  15.7 us
    ppermute x11, starting transfers between devices, send(): return lax.ppermute(value, ('row', 'col'), pairs)  13.2 us
    all_to_all x1, starting transfers between devices, gather_shards(): held = lax.all_to_all(copies, 'col', 0, 0, tiled=True)  6.88 us
    ppermute x11, waiting for transfers between devices, send(): return lax.ppermute(value, ('row', 'col'), pairs)  5.05 us
    all_to_all x1, waiting for transfers between devices, gather_shards(): held = lax.all_to_all(copies, 'col', 0, 0, tiled=True)  4.21 us
    pallas_call x1, Pallas kernels, shards(): pl.pallas_call(prep_kernel, grid_spec=pltpu.PrefetchScalarGridSpec(num_sc...  3.88 us
  transfers between devices with their start and end apart: 12, of which 4 were waited for; matrix products, arithmetic and copies ran while one was open for 1% of the time, Pallas kernels for 30%

profile of v8, /device:TPU:73, one launch (start us, length us, event | category | flops | bytes accessed | tf_op | source)
XLA Modules:
  0.0 143.7 jit_solution(2786429445041360082)
XLA Ops:
  0.0 0.7 reshape.127
  0.7 0.7 pad_maximum_fusion.1
  1.4 0.7 broadcast_in_dim.86
  2.1 6.9 %all-to-all-start = ((f32[16,17,1,128]{3,2,1,0:T(1,128)}), f32[16,17,1,128]{3,2,1,0:T(1,128)S(1)}, u32[]{:S(2)}, u32[]{:S(2)}) async-start(f32[16,17,1,128]{3,2,1,0:T(1,128)} %broadcast_in_dim.86), calls=%async_computation | async-start | bytes 278528 | tf_op jit(solution)/shard_map/all_to_all | solution.py:48
  9.1 0.1 pad_add_fusion
  9.2 0.1 select_select_fusion
  9.2 0.1 select_n.129
  9.3 0.8 select_reduce_fusion
  10.2 4.2 %all-to-all-done = f32[16,17,1,128]{3,2,1,0:T(1,128)S(1)} async-done(((f32[16,17,1,128]{3,2,1,0:T(1,128)}), f32[16,17,1,128]{3,2,1,0:T(1,128)S(1)}, u32[]{:S(2)}, u32[]{:S(2)}) %all-to-all-start) | async-done | bytes 139296 | tf_op jit(solution)/shard_map/all_to_all | solution.py:48
  14.4 0.2 collective-permute-start.2
  14.6 2.3 %collective-permute-start.1 = (f32[16,17,1,128]{3,2,1,0:T(1,128)S(1)}, f32[16,17,1,128]{3,2,1,0:T(1,128)S(1)}, u32[]{:S(2)}, u32[]{:S(2)}) collective-permute-start(f32[16,17,1,128]{3,2,1,0:T(1,128)S(1)} %all-to-all-done), channel_id=1, source_target_pairs={{0,64},{1,65},{2,66},{3,67},{4,68},{5,69},{6,70},{7,71},{8,72},{9,... | collective-permute-start | bytes 417800 | tf_op jit(solution)/shard_map/ppermute | solution.py:42
  16.9 1.6 %collective-permute-start = (f32[16,17,1,128]{3,2,1,0:T(1,128)S(1)}, f32[16,17,1,128]{3,2,1,0:T(1,128)S(1)}, u32[]{:S(2)}, u32[]{:S(2)}) collective-permute-start(f32[16,17,1,128]{3,2,1,0:T(1,128)S(1)} %all-to-all-done), channel_id=1, source_target_pairs={{0,32},{1,33},{2,34},{3,35},{4,36},{5,37},{6,38},{7,39},{8,40},{9,... | collective-permute-start | bytes 417800 | tf_op jit(solution)/shard_map/ppermute | solution.py:42
  18.5 0.1 iota_add_fusion
  18.6 0.1 add.147.where_ref
  18.7 0.0 collective-permute-done.2
  18.7 2.9 %collective-permute-done.1 = f32[16,17,1,128]{3,2,1,0:T(1,128)S(1)} collective-permute-done((f32[16,17,1,128]{3,2,1,0:T(1,128)S(1)}, f32[16,17,1,128]{3,2,1,0:T(1,128)S(1)}, u32[]{:S(2)}, u32[]{:S(2)}) %collective-permute-start.1) | collective-permute-done | bytes 139296 | tf_op jit(solution)/shard_map/ppermute | solution.py:42
  21.5 0.8 collective-permute-done
  22.3 0.5 pad_maximum_fusion
  22.8 3.0 %collective-permute-start.3 = (f32[64,17,1,128]{3,2,1,0:T(1,128)S(1)}, f32[64,17,1,128]{3,2,1,0:T(1,128)S(1)}, u32[]{:S(2)}, u32[]{:S(2)}) collective-permute-start(f32[64,17,1,128]{3,2,1,0:T(1,128)S(1)} %pad_maximum_fusion), channel_id=1, source_target_pairs={{0,16},{1,17},{2,18},{3,19},{4,20},{5,21},{6,22},{7,23},{8,24},{9,... | collective-permute-start | bytes 1671176 | tf_op jit(solution)/shard_map/ppermute | solution.py:42
  25.8 0.1 concatenate.16.info
  26.1 1.4 collective-permute-done.3
  27.4 0.1 constant_dynamic-update-slice_fusion.g_ref
  27.5 3.9 %prep.1 = (bf16[8,4,512,48]{3,2,1,0:T(8,128)(2,1)S(1)}, bf16[8,4,48,512]{3,2,1,0:T(8,128)(2,1)S(1)}, f32[8,512,128]{2,1,0:T(8,128)S(1)}, f32[8,8,512]{2,1,0:T(8,128)S(1)}) custom-call(s32[32]{0:T(128)S(1)} %add.147.where_ref, f32[128,17,1,128]{3,2,1,0:T(1,128)S(1)} %constant_dynamic-update-slice_fusion.g_ref), custom_call_target="tpu_custom_call" | custom-call | tf_op jit(solution)/shard_map/prep/pallas_call | solution.py:399
  31.4 46.7 %chain.1 = (f32[512,512]{1,0:T(8,128)S(1)}, f32[1024,128]{1,0:T(8,128)S(1)}) custom-call(s32[20]{0:T(128)S(1)} %concatenate.16.info, bf16[8,4,512,48]{3,2,1,0:T(8,128)(2,1)S(1)} %get-tuple-element.27.u_ref, bf16[8,4,48,512]{3,2,1,0:T(8,128)(2,1)S(1)} %get-tuple-element.28.v_ref.vj_ref, f32[8,512,128]{2,1,0:T(8,128)S(1)} %get-tuple-element.29.wr_ref, ...), custom_call_target="tpu_custom_call" | custom-call | tf_op jit(solution)/shard_map/chain/pallas_call | solution.py:447
  78.1 0.5 collective-permute-start.7
  78.5 2.6 %collective-permute-start.6 = (f32[1024,128]{1,0:T(8,128)S(1)}, f32[1024,128]{1,0:T(8,128)S(1)}, u32[]{:S(2)}, u32[]{:S(2)}) collective-permute-start(f32[1024,128]{1,0:T(8,128)S(1)} %get-tuple-element.38.rest_0_), channel_id=1, source_target_pairs={{0,96},{1,97},{2,98},{3,99},{4,100},{5,101},{6,102},{7,103},{8,104... | collective-permute-start | bytes 1572872 | tf_op jit(solution)/shard_map/ppermute | solution.py:42
  81.1 0.0 collective-permute-start.5
  81.1 1.5 %collective-permute-start.4 = (f32[1024,128]{1,0:T(8,128)S(1)}, f32[1024,128]{1,0:T(8,128)S(1)}, u32[]{:S(2)}, u32[]{:S(2)}) collective-permute-start(f32[1024,128]{1,0:T(8,128)S(1)} %get-tuple-element.38.rest_0_), channel_id=1, source_target_pairs={{0,32},{1,33},{2,34},{3,35},{4,36},{5,37},{6,38},{7,39},{8,40},{9,... | collective-permute-start | bytes 1572872 | tf_op jit(solution)/shard_map/ppermute | solution.py:42
  82.6 25.2 %panel.1 = (bf16[2048,1024]{1,0:T(8,128)(2,1)S(1)}, bf16[2048,1024]{1,0:T(8,128)(2,1)S(1)}) custom-call(s32[20]{0:T(128)S(1)} %concatenate.16.info, bf16[8,4,512,48]{3,2,1,0:T(8,128)(2,1)S(1)} %get-tuple-element.27.u_ref, bf16[8,4,48,512]{3,2,1,0:T(8,128)(2,1)S(1)} %get-tuple-element.28.v_ref.vj_ref, f32[8,512,128]{2,1,0:T(8,128)S(1)} %get-tuple-element.29.wr_ref, ...), custom_call_target="tpu_custom_call" | custom-call | flops 60000002048 | bytes 16000000 | tf_op jit(solution)/shard_map/panel/pallas_call | solution.py:484
  107.8 0.0 collective-permute-done.6.rest_3_
  107.8 0.0 collective-permute-done.5.rest_2_
  107.9 0.0 collective-permute-done.4.rest_1_
  107.9 1.0 collective-permute-start.8
  108.9 0.1 collective-permute-start.9
  109.0 0.4 collective-permute-start.10
  109.4 18.6 %own.1.rest_10_ = f32[2048,1024]{1,0:T(8,128)S(1)} custom-call(s32[20]{0:T(128)S(1)} %concatenate.16.info, bf16[8,4,512,48]{3,2,1,0:T(8,128)(2,1)S(1)} %get-tuple-element.27.u_ref, bf16[8,4,48,512]{3,2,1,0:T(8,128)(2,1)S(1)} %get-tuple-element.28.v_ref.vj_ref, f32[8,512,128]{2,1,0:T(8,128)S(1)} %get-tuple-element.29.wr_ref, ...), custom_call_target="tpu_custom_call" | custom-call | flops 44999999488 | bytes 12000000 | tf_op jit(solution)/shard_map/own/pallas_call | solution.py:484
  128.0 0.0 collective-permute-done.7.rest_4_
  128.0 0.0 collective-permute-done.8.rest_5_
  128.0 0.0 collective-permute-done.9.rest_6_
  128.1 0.0 collective-permute-done.10.rest_7_
  128.1 15.7 %final.1 = f32[16384,128]{1,0:T(8,128)} custom-call(s32[20]{0:T(128)S(1)} %concatenate.16.info, f32[512,512]{1,0:T(8,128)S(1)} %get-tuple-element.31.f_ref, f32[1024,128]{1,0:T(8,128)S(1)} %get-tuple-element.38.rest_0_, f32[1024,128]{1,0:T(8,128)S(1)} %collective-permute-done.4.rest_1_, f32[1024,128]{1,0:T(8,128)S(1)} %collective-permute-done.5.rest_2_, ...), custom_call_target="tpu_custom_call" | custom-call | tf_op jit(solution)/shard_map/final/pallas_call | solution.py:509
  (9 shorter events, 0.2 us)
Async XLA Ops:
  2.1 12.3 %all-to-all-start = ((f32[16,17,1,128]{3,2,1,0:T(1,128)}), f32[16,17,1,128]{3,2,1,0:T(1,128)S(1)}, u32[]{:S(2)}, u32[]{:S(2)}) async-start(f32[16,17,1,128]{3,2,1,0:T(1,128)} %broadcast_in_dim.86), calls=%async_computation | async-start | bytes 278528 | tf_op jit(solution)/shard_map/all_to_all | solution.py:48
  14.4 4.2 %collective-permute-start.2 = (f32[16,17,1,128]{3,2,1,0:T(1,128)S(1)}, f32[16,17,1,128]{3,2,1,0:T(1,128)S(1)}, u32[]{:S(2)}, u32[]{:S(2)}) collective-permute-start(f32[16,17,1,128]{3,2,1,0:T(1,128)S(1)} %all-to-all-done), channel_id=1, source_target_pairs={{0,96},{1,97},{2,98},{3,99},{4,100},{5,101},{6,102},{7,103},{8,104... | collective-permute-start | bytes 417800 | tf_op jit(solution)/shard_map/ppermute | solution.py:42
  14.6 7.0 %collective-permute-start.1 = (f32[16,17,1,128]{3,2,1,0:T(1,128)S(1)}, f32[16,17,1,128]{3,2,1,0:T(1,128)S(1)}, u32[]{:S(2)}, u32[]{:S(2)}) collective-permute-start(f32[16,17,1,128]{3,2,1,0:T(1,128)S(1)} %all-to-all-done), channel_id=1, source_target_pairs={{0,64},{1,65},{2,66},{3,67},{4,68},{5,69},{6,70},{7,71},{8,72},{9,... | collective-permute-start | bytes 417800 | tf_op jit(solution)/shard_map/ppermute | solution.py:42
  16.9 5.4 %collective-permute-start = (f32[16,17,1,128]{3,2,1,0:T(1,128)S(1)}, f32[16,17,1,128]{3,2,1,0:T(1,128)S(1)}, u32[]{:S(2)}, u32[]{:S(2)}) collective-permute-start(f32[16,17,1,128]{3,2,1,0:T(1,128)S(1)} %all-to-all-done), channel_id=1, source_target_pairs={{0,32},{1,33},{2,34},{3,35},{4,36},{5,37},{6,38},{7,39},{8,40},{9,... | collective-permute-start | bytes 417800 | tf_op jit(solution)/shard_map/ppermute | solution.py:42
  22.8 4.6 %collective-permute-start.3 = (f32[64,17,1,128]{3,2,1,0:T(1,128)S(1)}, f32[64,17,1,128]{3,2,1,0:T(1,128)S(1)}, u32[]{:S(2)}, u32[]{:S(2)}) collective-permute-start(f32[64,17,1,128]{3,2,1,0:T(1,128)S(1)} %pad_maximum_fusion), channel_id=1, source_target_pairs={{0,16},{1,17},{2,18},{3,19},{4,20},{5,21},{6,22},{7,23},{8,24},{9,... | collective-permute-start | bytes 1671176 | tf_op jit(solution)/shard_map/ppermute | solution.py:42
  78.1 50.0 %collective-permute-start.7 = (f32[1024,128]{1,0:T(8,128)S(1)}, f32[1024,128]{1,0:T(8,128)S(1)}, u32[]{:S(2)}, u32[]{:S(2)}) collective-permute-start(f32[1024,128]{1,0:T(8,128)S(1)} %get-tuple-element.38.rest_0_), channel_id=1, source_target_pairs={{0,16},{1,17},{2,18},{3,19},{4,20},{5,21},{6,22},{7,23},{8,24},{9,... | collective-permute-start | bytes 1572872 | tf_op jit(solution)/shard_map/ppermute | solution.py:42
  78.5 29.3 %collective-permute-start.6 = (f32[1024,128]{1,0:T(8,128)S(1)}, f32[1024,128]{1,0:T(8,128)S(1)}, u32[]{:S(2)}, u32[]{:S(2)}) collective-permute-start(f32[1024,128]{1,0:T(8,128)S(1)} %get-tuple-element.38.rest_0_), channel_id=1, source_target_pairs={{0,96},{1,97},{2,98},{3,99},{4,100},{5,101},{6,102},{7,103},{8,104... | collective-permute-start | bytes 1572872 | tf_op jit(solution)/shard_map/ppermute | solution.py:42
  81.1 26.7 %collective-permute-start.5 = (f32[1024,128]{1,0:T(8,128)S(1)}, f32[1024,128]{1,0:T(8,128)S(1)}, u32[]{:S(2)}, u32[]{:S(2)}) collective-permute-start(f32[1024,128]{1,0:T(8,128)S(1)} %get-tuple-element.38.rest_0_), channel_id=1, source_target_pairs={{0,64},{1,65},{2,66},{3,67},{4,68},{5,69},{6,70},{7,71},{8,72},{9,... | collective-permute-start | bytes 1572872 | tf_op jit(solution)/shard_map/ppermute | solution.py:42
  81.1 26.7 %collective-permute-start.4 = (f32[1024,128]{1,0:T(8,128)S(1)}, f32[1024,128]{1,0:T(8,128)S(1)}, u32[]{:S(2)}, u32[]{:S(2)}) collective-permute-start(f32[1024,128]{1,0:T(8,128)S(1)} %get-tuple-element.38.rest_0_), channel_id=1, source_target_pairs={{0,32},{1,33},{2,34},{3,35},{4,36},{5,37},{6,38},{7,39},{8,40},{9,... | collective-permute-start | bytes 1572872 | tf_op jit(solution)/shard_map/ppermute | solution.py:42
  107.9 20.2 %collective-permute-start.8 = (f32[1024,128]{1,0:T(8,128)S(1)}, f32[1024,128]{1,0:T(8,128)S(1)}, u32[]{:S(2)}, u32[]{:S(2)}) collective-permute-start(f32[1024,128]{1,0:T(8,128)S(1)} %collective-permute-done.4.rest_1_), channel_id=1, source_target_pairs={{0,16},{1,17},{2,18},{3,19},{4,20},{5,21},{6,22},{7,23},{8,24},{9,... | collective-permute-start | bytes 1572872 | tf_op jit(solution)/shard_map/ppermute | solution.py:42
  108.9 19.1 %collective-permute-start.9 = (f32[1024,128]{1,0:T(8,128)S(1)}, f32[1024,128]{1,0:T(8,128)S(1)}, u32[]{:S(2)}, u32[]{:S(2)}) collective-permute-start(f32[1024,128]{1,0:T(8,128)S(1)} %collective-permute-done.5.rest_2_), channel_id=1, source_target_pairs={{0,16},{1,17},{2,18},{3,19},{4,20},{5,21},{6,22},{7,23},{8,24},{9,... | collective-permute-start | bytes 1572872 | tf_op jit(solution)/shard_map/ppermute | solution.py:42
  109.0 19.1 %collective-permute-start.10 = (f32[1024,128]{1,0:T(8,128)S(1)}, f32[1024,128]{1,0:T(8,128)S(1)}, u32[]{:S(2)}, u32[]{:S(2)}) collective-permute-start(f32[1024,128]{1,0:T(8,128)S(1)} %collective-permute-done.6.rest_3_), channel_id=1, source_target_pairs={{0,16},{1,17},{2,18},{3,19},{4,20},{5,21},{6,22},{7,23},{8,24},{9,... | collective-permute-start | bytes 1572872 | tf_op jit(solution)/shard_map/ppermute | solution.py:42

commit v9 on v8

--- a/solution.py
+++ b/solution.py
@@ -260,9 +260,9 @@
         for pair in range(blocks // 2):
             @pl.when(pair < (blocks - k) // 2)
             def _():
-                skip = pair * 256
-                below = pl.ds(pl.multiple_of(here + BASE + skip, BASE), 256)
-                t0, t1 = [tall[skip : skip + 256, n * 128 : n * 128 + 128] for n in range(2)]
+                skip = pair * 256 + BASE
+                below = pl.ds(pl.multiple_of(here + skip, BASE), 256)
+                t0, t1 = [tall[pair * 256 : pair * 256 + 256, n * 128 : n * 128 + 128] for n in range(2)]
                 update = dot(both([t0, t0], 1), stack[:, skip:]) + dot(t1, stack[0:128, skip:])
                 width = WINDOW - skip
                 into = pl.ds(pl.multiple_of(here + skip, BASE), width)
@@ -338,6 +338,7 @@
     parts, (ah, al, own, out_ref, yh, yl) = rest[:8], rest[8:]
     slot, chunk = pl.program_id(0), pl.program_id(1)
     start = pl.multiple_of(chunk * CHUNK, CHUNK)
+    rows = pl.ds(pl.multiple_of(slot * TILE + start, CHUNK), CHUNK)
     kinds = [info[3 + slot * 2], info[4 + slot * 2]]
 
     @pl.when((slot == 0) & (chunk == 0))
@@ -360,12 +361,12 @@
 
         @pl.when(kind == PANEL)
         def _():
-            store(j, -dot3(ah[...], al[...], yh[j], yl[j]))
+            store(j, -dot3(ah[rows, :], al[rows, :], yh[j], yl[j]))
 
         @pl.when((kind == UPDATE) | (kind == DIAGONAL))
         def _():
-            values = own[:, j * TILE : j * TILE + TILE]
-            store(j, values - dot3(ah[...], al[...], yh[j], yl[j]))
+            values = own[rows, j * TILE : j * TILE + TILE]
+            store(j, values - dot3(ah[rows, :], al[rows, :], yh[j], yl[j]))
 
         if j == 0:
             @pl.when(kind == FACTOR)
@@ -511,7 +512,7 @@
         grid_spec=pltpu.PrefetchScalarGridSpec(
             num_scalar_prefetch=1,
             grid=(4, chunks),
-            in_specs=whole(9) + [blocked] * 3,
+            in_specs=whole(12),
             out_specs=pl.BlockSpec((lines, 128), lambda i, h, info: (i * chunks + h, 0)),
             scratch_shapes=[pltpu.VMEM((2, LEAD, TILE), BF16)] * 2,
         ),

time: 146 us -> 145 us (level)
  transfers between devices with their start and end apart: 12 -> 12, of which waited for: 4 -> 4; matrix products, arithmetic and copies ran while one was open for 1% -> 1% of each run, Pallas kernels for 30% -> 31%
where the time goes in v9:
time: 145 us; the launch traced here: 144 us
  Pallas kernels  110 us (76%)
  starting transfers between devices  20.1 us (14%)
  waiting for transfers between devices  9.26 us (6%)
  other arithmetic  2.3 us (2%)
  local copies, waits for them, and re-layouts  1.87 us (1%)
    pallas_call x1, Pallas kernels, shards(): pl.pallas_call(chain_kernel, grid_spec=pltpu.PrefetchScalarGridSpec(num_s...  46.5 us
    pallas_call x2, Pallas kernels, assembled(): pl.pallas_call(kernel, grid_spec=pltpu.PrefetchScalarGridSpec(num_scalar_...  43.8 us
    pallas_call x1, Pallas kernels, shards(): pl.pallas_call(final_kernel, grid_spec=pltpu.PrefetchScalarGridSpec(num_s...  15.7 us
    ppermute x11, starting transfers between devices, send(): return lax.ppermute(value, ('row', 'col'), pairs)  13.2 us
    all_to_all x1, starting transfers between devices, gather_shards(): held = lax.all_to_all(copies, 'col', 0, 0, tiled=True)  6.88 us
    ppermute x11, waiting for transfers between devices, send(): return lax.ppermute(value, ('row', 'col'), pairs)  5.05 us
    all_to_all x1, waiting for transfers between devices, gather_shards(): held = lax.all_to_all(copies, 'col', 0, 0, tiled=True)  4.21 us
    pallas_call x1, Pallas kernels, shards(): pl.pallas_call(prep_kernel, grid_spec=pltpu.PrefetchScalarGridSpec(num_sc...  3.88 us
  transfers between devices with their start and end apart: 12, of which 4 were waited for; matrix products, arithmetic and copies ran while one was open for 1% of the time, Pallas kernels for 31%

profile of v9, /device:TPU:73, one launch (start us, length us, event | category | flops | bytes accessed | tf_op | source)
XLA Modules:
  0.0 143.6 jit_solution(1131911458974806757)
XLA Ops:
  0.0 0.7 reshape.127
  0.7 0.7 pad_maximum_fusion.1
  1.4 0.7 broadcast_in_dim.86
  2.1 6.9 %all-to-all-start = ((f32[16,17,1,128]{3,2,1,0:T(1,128)}), f32[16,17,1,128]{3,2,1,0:T(1,128)S(1)}, u32[]{:S(2)}, u32[]{:S(2)}) async-start(f32[16,17,1,128]{3,2,1,0:T(1,128)} %broadcast_in_dim.86), calls=%async_computation | async-start | bytes 278528 | tf_op jit(solution)/shard_map/all_to_all | solution.py:48
  9.1 0.1 pad_add_fusion
  9.2 0.1 select_select_fusion
  9.2 0.1 select_n.129
  9.3 0.8 select_reduce_fusion
  10.2 4.2 %all-to-all-done = f32[16,17,1,128]{3,2,1,0:T(1,128)S(1)} async-done(((f32[16,17,1,128]{3,2,1,0:T(1,128)}), f32[16,17,1,128]{3,2,1,0:T(1,128)S(1)}, u32[]{:S(2)}, u32[]{:S(2)}) %all-to-all-start) | async-done | bytes 139296 | tf_op jit(solution)/shard_map/all_to_all | solution.py:48
  14.4 0.2 collective-permute-start.2
  14.6 2.3 %collective-permute-start.1 = (f32[16,17,1,128]{3,2,1,0:T(1,128)S(1)}, f32[16,17,1,128]{3,2,1,0:T(1,128)S(1)}, u32[]{:S(2)}, u32[]{:S(2)}) collective-permute-start(f32[16,17,1,128]{3,2,1,0:T(1,128)S(1)} %all-to-all-done), channel_id=1, source_target_pairs={{0,64},{1,65},{2,66},{3,67},{4,68},{5,69},{6,70},{7,71},{8,72},{9,... | collective-permute-start | bytes 417800 | tf_op jit(solution)/shard_map/ppermute | solution.py:42
  16.9 1.6 %collective-permute-start = (f32[16,17,1,128]{3,2,1,0:T(1,128)S(1)}, f32[16,17,1,128]{3,2,1,0:T(1,128)S(1)}, u32[]{:S(2)}, u32[]{:S(2)}) collective-permute-start(f32[16,17,1,128]{3,2,1,0:T(1,128)S(1)} %all-to-all-done), channel_id=1, source_target_pairs={{0,32},{1,33},{2,34},{3,35},{4,36},{5,37},{6,38},{7,39},{8,40},{9,... | collective-permute-start | bytes 417800 | tf_op jit(solution)/shard_map/ppermute | solution.py:42
  18.5 0.1 iota_add_fusion
  18.6 0.1 add.147.where_ref
  18.7 0.0 collective-permute-done.2
  18.7 2.9 %collective-permute-done.1 = f32[16,17,1,128]{3,2,1,0:T(1,128)S(1)} collective-permute-done((f32[16,17,1,128]{3,2,1,0:T(1,128)S(1)}, f32[16,17,1,128]{3,2,1,0:T(1,128)S(1)}, u32[]{:S(2)}, u32[]{:S(2)}) %collective-permute-start.1) | collective-permute-done | bytes 139296 | tf_op jit(solution)/shard_map/ppermute | solution.py:42
  21.5 0.8 collective-permute-done
  22.3 0.5 pad_maximum_fusion
  22.8 3.0 %collective-permute-start.3 = (f32[64,17,1,128]{3,2,1,0:T(1,128)S(1)}, f32[64,17,1,128]{3,2,1,0:T(1,128)S(1)}, u32[]{:S(2)}, u32[]{:S(2)}) collective-permute-start(f32[64,17,1,128]{3,2,1,0:T(1,128)S(1)} %pad_maximum_fusion), channel_id=1, source_target_pairs={{0,16},{1,17},{2,18},{3,19},{4,20},{5,21},{6,22},{7,23},{8,24},{9,... | collective-permute-start | bytes 1671176 | tf_op jit(solution)/shard_map/ppermute | solution.py:42
  25.8 0.1 concatenate.16.info
  26.1 1.4 collective-permute-done.3
  27.4 0.1 constant_dynamic-update-slice_fusion.g_ref
  27.5 3.9 %prep.1 = (bf16[8,4,512,48]{3,2,1,0:T(8,128)(2,1)S(1)}, bf16[8,4,48,512]{3,2,1,0:T(8,128)(2,1)S(1)}, f32[8,512,128]{2,1,0:T(8,128)S(1)}, f32[8,8,512]{2,1,0:T(8,128)S(1)}) custom-call(s32[32]{0:T(128)S(1)} %add.147.where_ref, f32[128,17,1,128]{3,2,1,0:T(1,128)S(1)} %constant_dynamic-update-slice_fusion.g_ref), custom_call_target="tpu_custom_call" | custom-call | tf_op jit(solution)/shard_map/prep/pallas_call | solution.py:400
  31.4 46.5 %chain.1 = (f32[512,512]{1,0:T(8,128)S(1)}, f32[1024,128]{1,0:T(8,128)S(1)}) custom-call(s32[20]{0:T(128)S(1)} %concatenate.16.info, bf16[8,4,512,48]{3,2,1,0:T(8,128)(2,1)S(1)} %get-tuple-element.27.u_ref, bf16[8,4,48,512]{3,2,1,0:T(8,128)(2,1)S(1)} %get-tuple-element.28.v_ref.vj_ref, f32[8,512,128]{2,1,0:T(8,128)S(1)} %get-tuple-element.29.wr_ref, ...), custom_call_target="tpu_custom_call" | custom-call | tf_op jit(solution)/shard_map/chain/pallas_call | solution.py:448
  77.9 0.5 collective-permute-start.7
  78.4 2.6 %collective-permute-start.6 = (f32[1024,128]{1,0:T(8,128)S(1)}, f32[1024,128]{1,0:T(8,128)S(1)}, u32[]{:S(2)}, u32[]{:S(2)}) collective-permute-start(f32[1024,128]{1,0:T(8,128)S(1)} %get-tuple-element.38.rest_0_), channel_id=1, source_target_pairs={{0,96},{1,97},{2,98},{3,99},{4,100},{5,101},{6,102},{7,103},{8,104... | collective-permute-start | bytes 1572872 | tf_op jit(solution)/shard_map/ppermute | solution.py:42
  81.0 0.0 collective-permute-start.5
  81.0 1.5 %collective-permute-start.4 = (f32[1024,128]{1,0:T(8,128)S(1)}, f32[1024,128]{1,0:T(8,128)S(1)}, u32[]{:S(2)}, u32[]{:S(2)}) collective-permute-start(f32[1024,128]{1,0:T(8,128)S(1)} %get-tuple-element.38.rest_0_), channel_id=1, source_target_pairs={{0,32},{1,33},{2,34},{3,35},{4,36},{5,37},{6,38},{7,39},{8,40},{9,... | collective-permute-start | bytes 1572872 | tf_op jit(solution)/shard_map/ppermute | solution.py:42
  82.5 25.2 %panel.1 = (bf16[2048,1024]{1,0:T(8,128)(2,1)S(1)}, bf16[2048,1024]{1,0:T(8,128)(2,1)S(1)}) custom-call(s32[20]{0:T(128)S(1)} %concatenate.16.info, bf16[8,4,512,48]{3,2,1,0:T(8,128)(2,1)S(1)} %get-tuple-element.27.u_ref, bf16[8,4,48,512]{3,2,1,0:T(8,128)(2,1)S(1)} %get-tuple-element.28.v_ref.vj_ref, f32[8,512,128]{2,1,0:T(8,128)S(1)} %get-tuple-element.29.wr_ref, ...), custom_call_target="tpu_custom_call" | custom-call | flops 60000002048 | bytes 16000000 | tf_op jit(solution)/shard_map/panel/pallas_call | solution.py:485
  107.7 0.0 collective-permute-done.6.rest_3_
  107.7 0.0 collective-permute-done.5.rest_2_
  107.7 0.0 collective-permute-done.4.rest_1_
  107.7 1.1 collective-permute-start.8
  108.8 0.1 collective-permute-start.9
  108.9 0.4 collective-permute-start.10
  109.3 18.6 %own.1.rest_10_ = f32[2048,1024]{1,0:T(8,128)S(1)} custom-call(s32[20]{0:T(128)S(1)} %concatenate.16.info, bf16[8,4,512,48]{3,2,1,0:T(8,128)(2,1)S(1)} %get-tuple-element.27.u_ref, bf16[8,4,48,512]{3,2,1,0:T(8,128)(2,1)S(1)} %get-tuple-element.28.v_ref.vj_ref, f32[8,512,128]{2,1,0:T(8,128)S(1)} %get-tuple-element.29.wr_ref, ...), custom_call_target="tpu_custom_call" | custom-call | flops 44999999488 | bytes 12000000 | tf_op jit(solution)/shard_map/own/pallas_call | solution.py:485
  127.9 0.0 collective-permute-done.7.rest_4_
  127.9 0.0 collective-permute-done.8.rest_5_
  127.9 0.0 collective-permute-done.9.rest_6_
  127.9 0.0 collective-permute-done.10.rest_7_
  127.9 15.7 %final.1 = f32[16384,128]{1,0:T(8,128)} custom-call(s32[20]{0:T(128)S(1)} %concatenate.16.info, f32[512,512]{1,0:T(8,128)S(1)} %get-tuple-element.31.f_ref, f32[1024,128]{1,0:T(8,128)S(1)} %get-tuple-element.38.rest_0_, f32[1024,128]{1,0:T(8,128)S(1)} %collective-permute-done.4.rest_1_, f32[1024,128]{1,0:T(8,128)S(1)} %collective-permute-done.5.rest_2_, ...), custom_call_target="tpu_custom_call" | custom-call | tf_op jit(solution)/shard_map/final/pallas_call | solution.py:510
  (9 shorter events, 0.2 us)
Async XLA Ops:
  2.1 12.3 %all-to-all-start = ((f32[16,17,1,128]{3,2,1,0:T(1,128)}), f32[16,17,1,128]{3,2,1,0:T(1,128)S(1)}, u32[]{:S(2)}, u32[]{:S(2)}) async-start(f32[16,17,1,128]{3,2,1,0:T(1,128)} %broadcast_in_dim.86), calls=%async_computation | async-start | bytes 278528 | tf_op jit(solution)/shard_map/all_to_all | solution.py:48
  14.4 4.2 %collective-permute-start.2 = (f32[16,17,1,128]{3,2,1,0:T(1,128)S(1)}, f32[16,17,1,128]{3,2,1,0:T(1,128)S(1)}, u32[]{:S(2)}, u32[]{:S(2)}) collective-permute-start(f32[16,17,1,128]{3,2,1,0:T(1,128)S(1)} %all-to-all-done), channel_id=1, source_target_pairs={{0,96},{1,97},{2,98},{3,99},{4,100},{5,101},{6,102},{7,103},{8,104... | collective-permute-start | bytes 417800 | tf_op jit(solution)/shard_map/ppermute | solution.py:42
  14.6 7.0 %collective-permute-start.1 = (f32[16,17,1,128]{3,2,1,0:T(1,128)S(1)}, f32[16,17,1,128]{3,2,1,0:T(1,128)S(1)}, u32[]{:S(2)}, u32[]{:S(2)}) collective-permute-start(f32[16,17,1,128]{3,2,1,0:T(1,128)S(1)} %all-to-all-done), channel_id=1, source_target_pairs={{0,64},{1,65},{2,66},{3,67},{4,68},{5,69},{6,70},{7,71},{8,72},{9,... | collective-permute-start | bytes 417800 | tf_op jit(solution)/shard_map/ppermute | solution.py:42
  16.9 5.4 %collective-permute-start = (f32[16,17,1,128]{3,2,1,0:T(1,128)S(1)}, f32[16,17,1,128]{3,2,1,0:T(1,128)S(1)}, u32[]{:S(2)}, u32[]{:S(2)}) collective-permute-start(f32[16,17,1,128]{3,2,1,0:T(1,128)S(1)} %all-to-all-done), channel_id=1, source_target_pairs={{0,32},{1,33},{2,34},{3,35},{4,36},{5,37},{6,38},{7,39},{8,40},{9,... | collective-permute-start | bytes 417800 | tf_op jit(solution)/shard_map/ppermute | solution.py:42
  22.8 4.6 %collective-permute-start.3 = (f32[64,17,1,128]{3,2,1,0:T(1,128)S(1)}, f32[64,17,1,128]{3,2,1,0:T(1,128)S(1)}, u32[]{:S(2)}, u32[]{:S(2)}) collective-permute-start(f32[64,17,1,128]{3,2,1,0:T(1,128)S(1)} %pad_maximum_fusion), channel_id=1, source_target_pairs={{0,16},{1,17},{2,18},{3,19},{4,20},{5,21},{6,22},{7,23},{8,24},{9,... | collective-permute-start | bytes 1671176 | tf_op jit(solution)/shard_map/ppermute | solution.py:42
  77.9 50.0 %collective-permute-start.7 = (f32[1024,128]{1,0:T(8,128)S(1)}, f32[1024,128]{1,0:T(8,128)S(1)}, u32[]{:S(2)}, u32[]{:S(2)}) collective-permute-start(f32[1024,128]{1,0:T(8,128)S(1)} %get-tuple-element.38.rest_0_), channel_id=1, source_target_pairs={{0,16},{1,17},{2,18},{3,19},{4,20},{5,21},{6,22},{7,23},{8,24},{9,... | collective-permute-start | bytes 1572872 | tf_op jit(solution)/shard_map/ppermute | solution.py:42
  78.4 29.3 %collective-permute-start.6 = (f32[1024,128]{1,0:T(8,128)S(1)}, f32[1024,128]{1,0:T(8,128)S(1)}, u32[]{:S(2)}, u32[]{:S(2)}) collective-permute-start(f32[1024,128]{1,0:T(8,128)S(1)} %get-tuple-element.38.rest_0_), channel_id=1, source_target_pairs={{0,96},{1,97},{2,98},{3,99},{4,100},{5,101},{6,102},{7,103},{8,104... | collective-permute-start | bytes 1572872 | tf_op jit(solution)/shard_map/ppermute | solution.py:42
  81.0 26.7 %collective-permute-start.5 = (f32[1024,128]{1,0:T(8,128)S(1)}, f32[1024,128]{1,0:T(8,128)S(1)}, u32[]{:S(2)}, u32[]{:S(2)}) collective-permute-start(f32[1024,128]{1,0:T(8,128)S(1)} %get-tuple-element.38.rest_0_), channel_id=1, source_target_pairs={{0,64},{1,65},{2,66},{3,67},{4,68},{5,69},{6,70},{7,71},{8,72},{9,... | collective-permute-start | bytes 1572872 | tf_op jit(solution)/shard_map/ppermute | solution.py:42
  81.0 26.7 %collective-permute-start.4 = (f32[1024,128]{1,0:T(8,128)S(1)}, f32[1024,128]{1,0:T(8,128)S(1)}, u32[]{:S(2)}, u32[]{:S(2)}) collective-permute-start(f32[1024,128]{1,0:T(8,128)S(1)} %get-tuple-element.38.rest_0_), channel_id=1, source_target_pairs={{0,32},{1,33},{2,34},{3,35},{4,36},{5,37},{6,38},{7,39},{8,40},{9,... | collective-permute-start | bytes 1572872 | tf_op jit(solution)/shard_map/ppermute | solution.py:42
  107.7 20.2 %collective-permute-start.8 = (f32[1024,128]{1,0:T(8,128)S(1)}, f32[1024,128]{1,0:T(8,128)S(1)}, u32[]{:S(2)}, u32[]{:S(2)}) collective-permute-start(f32[1024,128]{1,0:T(8,128)S(1)} %collective-permute-done.4.rest_1_), channel_id=1, source_target_pairs={{0,16},{1,17},{2,18},{3,19},{4,20},{5,21},{6,22},{7,23},{8,24},{9,... | collective-permute-start | bytes 1572872 | tf_op jit(solution)/shard_map/ppermute | solution.py:42
  108.8 19.1 %collective-permute-start.9 = (f32[1024,128]{1,0:T(8,128)S(1)}, f32[1024,128]{1,0:T(8,128)S(1)}, u32[]{:S(2)}, u32[]{:S(2)}) collective-permute-start(f32[1024,128]{1,0:T(8,128)S(1)} %collective-permute-done.5.rest_2_), channel_id=1, source_target_pairs={{0,16},{1,17},{2,18},{3,19},{4,20},{5,21},{6,22},{7,23},{8,24},{9,... | collective-permute-start | bytes 1572872 | tf_op jit(solution)/shard_map/ppermute | solution.py:42
  108.9 19.1 %collective-permute-start.10 = (f32[1024,128]{1,0:T(8,128)S(1)}, f32[1024,128]{1,0:T(8,128)S(1)}, u32[]{:S(2)}, u32[]{:S(2)}) collective-permute-start(f32[1024,128]{1,0:T(8,128)S(1)} %collective-permute-done.6.rest_3_), channel_id=1, source_target_pairs={{0,16},{1,17},{2,18},{3,19},{4,20},{5,21},{6,22},{7,23},{8,24},{9,... | collective-permute-start | bytes 1572872 | tf_op jit(solution)/shard_map/ppermute | solution.py:42

commit v10 on v9

--- a/solution.py
+++ b/solution.py
@@ -331,14 +331,15 @@
 
 
 CHUNK = 256
+ROWS = 512
 ZERO, UPDATE, DIAGONAL, PANEL, FACTOR = range(5)
 
 
 def final_kernel(info, f_ref, *rest):
     parts, (ah, al, own, out_ref, yh, yl) = rest[:8], rest[8:]
     slot, chunk = pl.program_id(0), pl.program_id(1)
-    start = pl.multiple_of(chunk * CHUNK, CHUNK)
-    rows = pl.ds(pl.multiple_of(slot * TILE + start, CHUNK), CHUNK)
+    start = pl.multiple_of(chunk * ROWS, ROWS)
+    rows = pl.ds(pl.multiple_of(slot * TILE + start, ROWS), ROWS)
     kinds = [info[3 + slot * 2], info[4 + slot * 2]]
 
     @pl.when((slot == 0) & (chunk == 0))
@@ -350,14 +351,14 @@
 
     def store(j, values):
         for q in range(TILE // 128):
-            out_ref[pl.ds(j * 4 + q, CHUNK, stride=8), :] = values[:, q * 128 : (q + 1) * 128]
+            out_ref[pl.ds(j * 4 + q, ROWS, stride=8), :] = values[:, q * 128 : (q + 1) * 128]
 
     for j in range(2):
         kind = kinds[j]
 
         @pl.when(kind == ZERO)
         def _():
-            store(j, jnp.zeros((CHUNK, TILE), F32))
+            store(j, jnp.zeros((ROWS, TILE), F32))
 
         @pl.when(kind == PANEL)
         def _():
@@ -371,7 +372,7 @@
         if j == 0:
             @pl.when(kind == FACTOR)
             def _():
-                store(j, f_ref[pl.ds(start, CHUNK), :])
+                store(j, f_ref[pl.ds(start, ROWS), :])
 
 
 def whole(count):
@@ -506,14 +507,14 @@
     own = assembled(own_kernel, 3, [jax.ShapeDtypeStruct((4 * TILE, LEAD), F32)], 6, "own")
     *parts, own = lax.optimization_barrier((*parts, *own))
 
-    lines = CHUNK * 8
+    lines = ROWS * 8
     out = pl.pallas_call(
         final_kernel,
         grid_spec=pltpu.PrefetchScalarGridSpec(
             num_scalar_prefetch=1,
-            grid=(4, chunks),
+            grid=(4, TILE // ROWS),
             in_specs=whole(12),
-            out_specs=pl.BlockSpec((lines, 128), lambda i, h, info: (i * chunks + h, 0)),
+            out_specs=pl.BlockSpec((lines, 128), lambda i, h, info: (i * (TILE // ROWS) + h, 0)),
             scratch_shapes=[pltpu.VMEM((2, LEAD, TILE), BF16)] * 2,
         ),
         out_shape=jax.ShapeDtypeStruct((4 * TILE * 8, 128), F32),

time: 145 us -> 144 us (level)
  no operation moved by 1% of the time
where the time goes in v10:
time: 144 us; the launch traced here: 143 us
  Pallas kernels  109 us (76%)
  starting transfers between devices  20.1 us (14%)
  waiting for transfers between devices  9.26 us (6%)
  other arithmetic  2.3 us (2%)
  local copies, waits for them, and re-layouts  1.87 us (1%)
    pallas_call x1, Pallas kernels, shards(): pl.pallas_call(chain_kernel, grid_spec=pltpu.PrefetchScalarGridSpec(num_s...  46.5 us
    pallas_call x2, Pallas kernels, assembled(): pl.pallas_call(kernel, grid_spec=pltpu.PrefetchScalarGridSpec(num_scalar_...  43.8 us
    pallas_call x1, Pallas kernels, shards(): pl.pallas_call(final_kernel, grid_spec=pltpu.PrefetchScalarGridSpec(num_s...  14.6 us
    ppermute x11, starting transfers between devices, send(): return lax.ppermute(value, ('row', 'col'), pairs)  13.2 us
    all_to_all x1, starting transfers between devices, gather_shards(): held = lax.all_to_all(copies, 'col', 0, 0, tiled=True)  6.88 us
    ppermute x11, waiting for transfers between devices, send(): return lax.ppermute(value, ('row', 'col'), pairs)  5.05 us
    all_to_all x1, waiting for transfers between devices, gather_shards(): held = lax.all_to_all(copies, 'col', 0, 0, tiled=True)  4.21 us
    pallas_call x1, Pallas kernels, shards(): pl.pallas_call(prep_kernel, grid_spec=pltpu.PrefetchScalarGridSpec(num_sc...  3.88 us
  transfers between devices with their start and end apart: 12, of which 4 were waited for; matrix products, arithmetic and copies ran while one was open for 1% of the time, Pallas kernels for 31%

profile of v10, /device:TPU:73, one launch (start us, length us, event | category | flops | bytes accessed | tf_op | source)
XLA Modules:
  0.0 142.5 jit_solution(7925463740159312899)
XLA Ops:
  0.0 0.7 reshape.127
  0.7 0.7 pad_maximum_fusion.1
  1.4 0.7 broadcast_in_dim.86
  2.1 6.9 %all-to-all-start = ((f32[16,17,1,128]{3,2,1,0:T(1,128)}), f32[16,17,1,128]{3,2,1,0:T(1,128)S(1)}, u32[]{:S(2)}, u32[]{:S(2)}) async-start(f32[16,17,1,128]{3,2,1,0:T(1,128)} %broadcast_in_dim.86), calls=%async_computation | async-start | bytes 278528 | tf_op jit(solution)/shard_map/all_to_all | solution.py:48
  9.1 0.1 pad_add_fusion
  9.2 0.1 select_select_fusion
  9.2 0.1 select_n.129
  9.3 0.8 select_reduce_fusion
  10.2 4.2 %all-to-all-done = f32[16,17,1,128]{3,2,1,0:T(1,128)S(1)} async-done(((f32[16,17,1,128]{3,2,1,0:T(1,128)}), f32[16,17,1,128]{3,2,1,0:T(1,128)S(1)}, u32[]{:S(2)}, u32[]{:S(2)}) %all-to-all-start) | async-done | bytes 139296 | tf_op jit(solution)/shard_map/all_to_all | solution.py:48
  14.4 0.2 collective-permute-start.2
  14.6 2.3 %collective-permute-start.1 = (f32[16,17,1,128]{3,2,1,0:T(1,128)S(1)}, f32[16,17,1,128]{3,2,1,0:T(1,128)S(1)}, u32[]{:S(2)}, u32[]{:S(2)}) collective-permute-start(f32[16,17,1,128]{3,2,1,0:T(1,128)S(1)} %all-to-all-done), channel_id=1, source_target_pairs={{0,64},{1,65},{2,66},{3,67},{4,68},{5,69},{6,70},{7,71},{8,72},{9,... | collective-permute-start | bytes 417800 | tf_op jit(solution)/shard_map/ppermute | solution.py:42
  16.9 1.6 %collective-permute-start = (f32[16,17,1,128]{3,2,1,0:T(1,128)S(1)}, f32[16,17,1,128]{3,2,1,0:T(1,128)S(1)}, u32[]{:S(2)}, u32[]{:S(2)}) collective-permute-start(f32[16,17,1,128]{3,2,1,0:T(1,128)S(1)} %all-to-all-done), channel_id=1, source_target_pairs={{0,32},{1,33},{2,34},{3,35},{4,36},{5,37},{6,38},{7,39},{8,40},{9,... | collective-permute-start | bytes 417800 | tf_op jit(solution)/shard_map/ppermute | solution.py:42
  18.5 0.1 iota_add_fusion
  18.6 0.1 add.147.where_ref
  18.7 0.0 collective-permute-done.2
  18.7 2.9 %collective-permute-done.1 = f32[16,17,1,128]{3,2,1,0:T(1,128)S(1)} collective-permute-done((f32[16,17,1,128]{3,2,1,0:T(1,128)S(1)}, f32[16,17,1,128]{3,2,1,0:T(1,128)S(1)}, u32[]{:S(2)}, u32[]{:S(2)}) %collective-permute-start.1) | collective-permute-done | bytes 139296 | tf_op jit(solution)/shard_map/ppermute | solution.py:42
  21.5 0.8 collective-permute-done
  22.3 0.5 pad_maximum_fusion
  22.8 3.0 %collective-permute-start.3 = (f32[64,17,1,128]{3,2,1,0:T(1,128)S(1)}, f32[64,17,1,128]{3,2,1,0:T(1,128)S(1)}, u32[]{:S(2)}, u32[]{:S(2)}) collective-permute-start(f32[64,17,1,128]{3,2,1,0:T(1,128)S(1)} %pad_maximum_fusion), channel_id=1, source_target_pairs={{0,16},{1,17},{2,18},{3,19},{4,20},{5,21},{6,22},{7,23},{8,24},{9,... | collective-permute-start | bytes 1671176 | tf_op jit(solution)/shard_map/ppermute | solution.py:42
  25.8 0.1 concatenate.16.info
  26.1 1.4 collective-permute-done.3
  27.4 0.1 constant_dynamic-update-slice_fusion.g_ref
  27.5 3.9 %prep.1 = (bf16[8,4,512,48]{3,2,1,0:T(8,128)(2,1)S(1)}, bf16[8,4,48,512]{3,2,1,0:T(8,128)(2,1)S(1)}, f32[8,512,128]{2,1,0:T(8,128)S(1)}, f32[8,8,512]{2,1,0:T(8,128)S(1)}) custom-call(s32[32]{0:T(128)S(1)} %add.147.where_ref, f32[128,17,1,128]{3,2,1,0:T(1,128)S(1)} %constant_dynamic-update-slice_fusion.g_ref), custom_call_target="tpu_custom_call" | custom-call | tf_op jit(solution)/shard_map/prep/pallas_call | solution.py:401
  31.4 46.5 %chain.1 = (f32[512,512]{1,0:T(8,128)S(1)}, f32[1024,128]{1,0:T(8,128)S(1)}) custom-call(s32[20]{0:T(128)S(1)} %concatenate.16.info, bf16[8,4,512,48]{3,2,1,0:T(8,128)(2,1)S(1)} %get-tuple-element.27.u_ref, bf16[8,4,48,512]{3,2,1,0:T(8,128)(2,1)S(1)} %get-tuple-element.28.v_ref.vj_ref, f32[8,512,128]{2,1,0:T(8,128)S(1)} %get-tuple-element.29.wr_ref, ...), custom_call_target="tpu_custom_call" | custom-call | tf_op jit(solution)/shard_map/chain/pallas_call | solution.py:449
  77.9 0.5 collective-permute-start.7
  78.4 2.6 %collective-permute-start.6 = (f32[1024,128]{1,0:T(8,128)S(1)}, f32[1024,128]{1,0:T(8,128)S(1)}, u32[]{:S(2)}, u32[]{:S(2)}) collective-permute-start(f32[1024,128]{1,0:T(8,128)S(1)} %get-tuple-element.38.rest_0_), channel_id=1, source_target_pairs={{0,96},{1,97},{2,98},{3,99},{4,100},{5,101},{6,102},{7,103},{8,104... | collective-permute-start | bytes 1572872 | tf_op jit(solution)/shard_map/ppermute | solution.py:42
  81.0 0.0 collective-permute-start.5
  81.0 1.5 %collective-permute-start.4 = (f32[1024,128]{1,0:T(8,128)S(1)}, f32[1024,128]{1,0:T(8,128)S(1)}, u32[]{:S(2)}, u32[]{:S(2)}) collective-permute-start(f32[1024,128]{1,0:T(8,128)S(1)} %get-tuple-element.38.rest_0_), channel_id=1, source_target_pairs={{0,32},{1,33},{2,34},{3,35},{4,36},{5,37},{6,38},{7,39},{8,40},{9,... | collective-permute-start | bytes 1572872 | tf_op jit(solution)/shard_map/ppermute | solution.py:42
  82.5 25.2 %panel.1 = (bf16[2048,1024]{1,0:T(8,128)(2,1)S(1)}, bf16[2048,1024]{1,0:T(8,128)(2,1)S(1)}) custom-call(s32[20]{0:T(128)S(1)} %concatenate.16.info, bf16[8,4,512,48]{3,2,1,0:T(8,128)(2,1)S(1)} %get-tuple-element.27.u_ref, bf16[8,4,48,512]{3,2,1,0:T(8,128)(2,1)S(1)} %get-tuple-element.28.v_ref.vj_ref, f32[8,512,128]{2,1,0:T(8,128)S(1)} %get-tuple-element.29.wr_ref, ...), custom_call_target="tpu_custom_call" | custom-call | flops 60000002048 | bytes 16000000 | tf_op jit(solution)/shard_map/panel/pallas_call | solution.py:486
  107.7 0.0 collective-permute-done.6.rest_3_
  107.7 0.0 collective-permute-done.5.rest_2_
  107.7 0.0 collective-permute-done.4.rest_1_
  107.7 1.1 collective-permute-start.8
  108.8 0.1 collective-permute-start.9
  108.9 0.4 collective-permute-start.10
  109.3 18.6 %own.1.rest_10_ = f32[2048,1024]{1,0:T(8,128)S(1)} custom-call(s32[20]{0:T(128)S(1)} %concatenate.16.info, bf16[8,4,512,48]{3,2,1,0:T(8,128)(2,1)S(1)} %get-tuple-element.27.u_ref, bf16[8,4,48,512]{3,2,1,0:T(8,128)(2,1)S(1)} %get-tuple-element.28.v_ref.vj_ref, f32[8,512,128]{2,1,0:T(8,128)S(1)} %get-tuple-element.29.wr_ref, ...), custom_call_target="tpu_custom_call" | custom-call | flops 44999999488 | bytes 12000000 | tf_op jit(solution)/shard_map/own/pallas_call | solution.py:486
  127.9 0.0 collective-permute-done.7.rest_4_
  127.9 0.0 collective-permute-done.8.rest_5_
  127.9 0.0 collective-permute-done.9.rest_6_
  127.9 0.0 collective-permute-done.10.rest_7_
  127.9 14.6 %final.1 = f32[16384,128]{1,0:T(8,128)} custom-call(s32[20]{0:T(128)S(1)} %concatenate.16.info, f32[512,512]{1,0:T(8,128)S(1)} %get-tuple-element.31.f_ref, f32[1024,128]{1,0:T(8,128)S(1)} %get-tuple-element.38.rest_0_, f32[1024,128]{1,0:T(8,128)S(1)} %collective-permute-done.4.rest_1_, f32[1024,128]{1,0:T(8,128)S(1)} %collective-permute-done.5.rest_2_, ...), custom_call_target="tpu_custom_call" | custom-call | tf_op jit(solution)/shard_map/final/pallas_call | solution.py:511
  (9 shorter events, 0.2 us)
Async XLA Ops:
  2.1 12.3 %all-to-all-start = ((f32[16,17,1,128]{3,2,1,0:T(1,128)}), f32[16,17,1,128]{3,2,1,0:T(1,128)S(1)}, u32[]{:S(2)}, u32[]{:S(2)}) async-start(f32[16,17,1,128]{3,2,1,0:T(1,128)} %broadcast_in_dim.86), calls=%async_computation | async-start | bytes 278528 | tf_op jit(solution)/shard_map/all_to_all | solution.py:48
  14.4 4.2 %collective-permute-start.2 = (f32[16,17,1,128]{3,2,1,0:T(1,128)S(1)}, f32[16,17,1,128]{3,2,1,0:T(1,128)S(1)}, u32[]{:S(2)}, u32[]{:S(2)}) collective-permute-start(f32[16,17,1,128]{3,2,1,0:T(1,128)S(1)} %all-to-all-done), channel_id=1, source_target_pairs={{0,96},{1,97},{2,98},{3,99},{4,100},{5,101},{6,102},{7,103},{8,104... | collective-permute-start | bytes 417800 | tf_op jit(solution)/shard_map/ppermute | solution.py:42
  14.6 7.0 %collective-permute-start.1 = (f32[16,17,1,128]{3,2,1,0:T(1,128)S(1)}, f32[16,17,1,128]{3,2,1,0:T(1,128)S(1)}, u32[]{:S(2)}, u32[]{:S(2)}) collective-permute-start(f32[16,17,1,128]{3,2,1,0:T(1,128)S(1)} %all-to-all-done), channel_id=1, source_target_pairs={{0,64},{1,65},{2,66},{3,67},{4,68},{5,69},{6,70},{7,71},{8,72},{9,... | collective-permute-start | bytes 417800 | tf_op jit(solution)/shard_map/ppermute | solution.py:42
  16.9 5.4 %collective-permute-start = (f32[16,17,1,128]{3,2,1,0:T(1,128)S(1)}, f32[16,17,1,128]{3,2,1,0:T(1,128)S(1)}, u32[]{:S(2)}, u32[]{:S(2)}) collective-permute-start(f32[16,17,1,128]{3,2,1,0:T(1,128)S(1)} %all-to-all-done), channel_id=1, source_target_pairs={{0,32},{1,33},{2,34},{3,35},{4,36},{5,37},{6,38},{7,39},{8,40},{9,... | collective-permute-start | bytes 417800 | tf_op jit(solution)/shard_map/ppermute | solution.py:42
  22.8 4.6 %collective-permute-start.3 = (f32[64,17,1,128]{3,2,1,0:T(1,128)S(1)}, f32[64,17,1,128]{3,2,1,0:T(1,128)S(1)}, u32[]{:S(2)}, u32[]{:S(2)}) collective-permute-start(f32[64,17,1,128]{3,2,1,0:T(1,128)S(1)} %pad_maximum_fusion), channel_id=1, source_target_pairs={{0,16},{1,17},{2,18},{3,19},{4,20},{5,21},{6,22},{7,23},{8,24},{9,... | collective-permute-start | bytes 1671176 | tf_op jit(solution)/shard_map/ppermute | solution.py:42
  77.9 50.0 %collective-permute-start.7 = (f32[1024,128]{1,0:T(8,128)S(1)}, f32[1024,128]{1,0:T(8,128)S(1)}, u32[]{:S(2)}, u32[]{:S(2)}) collective-permute-start(f32[1024,128]{1,0:T(8,128)S(1)} %get-tuple-element.38.rest_0_), channel_id=1, source_target_pairs={{0,16},{1,17},{2,18},{3,19},{4,20},{5,21},{6,22},{7,23},{8,24},{9,... | collective-permute-start | bytes 1572872 | tf_op jit(solution)/shard_map/ppermute | solution.py:42
  78.4 29.3 %collective-permute-start.6 = (f32[1024,128]{1,0:T(8,128)S(1)}, f32[1024,128]{1,0:T(8,128)S(1)}, u32[]{:S(2)}, u32[]{:S(2)}) collective-permute-start(f32[1024,128]{1,0:T(8,128)S(1)} %get-tuple-element.38.rest_0_), channel_id=1, source_target_pairs={{0,96},{1,97},{2,98},{3,99},{4,100},{5,101},{6,102},{7,103},{8,104... | collective-permute-start | bytes 1572872 | tf_op jit(solution)/shard_map/ppermute | solution.py:42
  81.0 26.7 %collective-permute-start.5 = (f32[1024,128]{1,0:T(8,128)S(1)}, f32[1024,128]{1,0:T(8,128)S(1)}, u32[]{:S(2)}, u32[]{:S(2)}) collective-permute-start(f32[1024,128]{1,0:T(8,128)S(1)} %get-tuple-element.38.rest_0_), channel_id=1, source_target_pairs={{0,64},{1,65},{2,66},{3,67},{4,68},{5,69},{6,70},{7,71},{8,72},{9,... | collective-permute-start | bytes 1572872 | tf_op jit(solution)/shard_map/ppermute | solution.py:42
  81.0 26.7 %collective-permute-start.4 = (f32[1024,128]{1,0:T(8,128)S(1)}, f32[1024,128]{1,0:T(8,128)S(1)}, u32[]{:S(2)}, u32[]{:S(2)}) collective-permute-start(f32[1024,128]{1,0:T(8,128)S(1)} %get-tuple-element.38.rest_0_), channel_id=1, source_target_pairs={{0,32},{1,33},{2,34},{3,35},{4,36},{5,37},{6,38},{7,39},{8,40},{9,... | collective-permute-start | bytes 1572872 | tf_op jit(solution)/shard_map/ppermute | solution.py:42
  107.7 20.2 %collective-permute-start.8 = (f32[1024,128]{1,0:T(8,128)S(1)}, f32[1024,128]{1,0:T(8,128)S(1)}, u32[]{:S(2)}, u32[]{:S(2)}) collective-permute-start(f32[1024,128]{1,0:T(8,128)S(1)} %collective-permute-done.4.rest_1_), channel_id=1, source_target_pairs={{0,16},{1,17},{2,18},{3,19},{4,20},{5,21},{6,22},{7,23},{8,24},{9,... | collective-permute-start | bytes 1572872 | tf_op jit(solution)/shard_map/ppermute | solution.py:42
  108.8 19.1 %collective-permute-start.9 = (f32[1024,128]{1,0:T(8,128)S(1)}, f32[1024,128]{1,0:T(8,128)S(1)}, u32[]{:S(2)}, u32[]{:S(2)}) collective-permute-start(f32[1024,128]{1,0:T(8,128)S(1)} %collective-permute-done.5.rest_2_), channel_id=1, source_target_pairs={{0,16},{1,17},{2,18},{3,19},{4,20},{5,21},{6,22},{7,23},{8,24},{9,... | collective-permute-start | bytes 1572872 | tf_op jit(solution)/shard_map/ppermute | solution.py:42
  108.9 19.1 %collective-permute-start.10 = (f32[1024,128]{1,0:T(8,128)S(1)}, f32[1024,128]{1,0:T(8,128)S(1)}, u32[]{:S(2)}, u32[]{:S(2)}) collective-permute-start(f32[1024,128]{1,0:T(8,128)S(1)} %collective-permute-done.6.rest_3_), channel_id=1, source_target_pairs={{0,16},{1,17},{2,18},{3,19},{4,20},{5,21},{6,22},{7,23},{8,24},{9,... | collective-permute-start | bytes 1572872 | tf_op jit(solution)/shard_map/ppermute | solution.py:42
